TPU v7x, 32 devices: a whole 2x2x4 slice. The times are simulated.
32 devices in a mesh: seq: 2 (over x), fsdp: 16 (over z, y, core).
Axes of the slice: x: 2, y: 2, z: 4, core: 2. Of those that a mesh axis runs over, the one named last changes fastest.
Arguments:
- tokens: bfloat16 [2, 16, 1024, 768], P(None, 'fsdp', 'seq'), may hold values from -6 to 6
- doc_ids: int32 [2, 16, 1024], P(None, 'fsdp', 'seq'), may hold values from 0 to 5, never falling along the last dimension, each value on 1 to 512 neighbouring positions
- cotangent: bfloat16 [2, 16, 1024, 768], P(None, 'fsdp', 'seq'), may hold values from -6 to 6
- w_query: bfloat16 [768, 768], P('fsdp'), may hold values from -0.3125 to 0.3125
- w_key: bfloat16 [768, 768], P('fsdp'), may hold values from -0.3125 to 0.3125
- w_value: bfloat16 [768, 768], P('fsdp'), may hold values from -0.21875 to 0.21875
- w_out: bfloat16 [768, 768], P('fsdp'), may hold values from -0.875 to 0.875
- w_gate: bfloat16 [768, 2048], P('fsdp'), may hold values from -0.21875 to 0.21875
- w_up: bfloat16 [768, 2048], P('fsdp'), may hold values from -0.21875 to 0.21875
- w_down: bfloat16 [2048, 768], P('fsdp'), may hold values from -0.125 to 0.125
- gain_attn: bfloat16 [768], P('fsdp'), may hold values from 0.5 to 1.5
- gain_ffn: bfloat16 [768], P('fsdp'), may hold values from 0.5 to 1.5
Outputs:
- output: bfloat16 [2, 16, 1024, 768], P(None, 'fsdp', 'seq')
- grad_tokens: float32 [2, 16, 1024, 768], P(None, 'fsdp', 'seq')
- grad_w_query: float32 [768, 768], P('fsdp')
- grad_w_key: float32 [768, 768], P('fsdp')
- grad_w_value: float32 [768, 768], P('fsdp')
- grad_w_out: float32 [768, 768], P('fsdp')
- grad_w_gate: float32 [768, 2048], P('fsdp')
- grad_w_up: float32 [768, 2048], P('fsdp')
- grad_w_down: float32 [2048, 768], P('fsdp')
- grad_gain_attn: float32 [768], P('fsdp')
- grad_gain_ffn: float32 [768], P('fsdp')
Inputs may be any that keep to these rules, and one draw needn't show every extreme that they name: Along each sequence doc_ids starts at 0 and never falls; each of the 6 documents holds 1 to 512 positions and one holds exactly 512.
All inputs are finite; a program needn't handle non-finite values.
Results may differ from a plain program's by a relative error of at most 0.017.
The roundings to bfloat16 on the way count: a program that leaves them out, or rounds other values in their place, can miss the bound.
Values may be sent and summed in bfloat16 or wider, within the bound.
No kernel may reach another device: no remote copies, remote signals or barrier semaphores. Data moves between devices by JAX's collectives and lax.ppermute only.
A program may use at most 192 MiB of HBM per device.

v0:
```python
import math

import jax
import jax.numpy as jnp
from jax import lax
from jax.sharding import PartitionSpec as P

HEAD_DIM = 64


EPSILON = 1e-05
MASK_FILL = -1e30


def rope_tables(positions, head_dim):
    half_dim = head_dim // 2
    inverse = jnp.exp(
        jnp.arange(half_dim, dtype=jnp.float32) * (-2.0 * math.log(10000.0) / head_dim)
    )
    angles = positions[:, None] * inverse[None, :]
    return (jnp.cos(angles)[:, None, :], jnp.sin(angles)[:, None, :])


def rotate(values, cosine, sine_part):
    half_dim = values.shape[-1] // 2
    first_half = values[..., :half_dim]
    second_half = values[..., half_dim:]
    return jnp.concatenate(
        [
            first_half * cosine - second_half * sine_part,
            second_half * cosine + first_half * sine_part,
        ],
        axis=-1,
    )


def unrotate(values, cosine, sine_part):
    half_dim = values.shape[-1] // 2
    first_half = values[..., :half_dim]
    second_half = values[..., half_dim:]
    return jnp.concatenate(
        [
            first_half * cosine + second_half * sine_part,
            second_half * cosine - first_half * sine_part,
        ],
        axis=-1,
    )


def outer_sum(left, right):
    return lax.dot_general(
        left, right, (((0,), (0,)), ((), ())), preferred_element_type=jnp.float32
    )


def contract(left, right):
    return lax.dot_general(
        left, right, (((1,), (1,)), ((), ())), preferred_element_type=jnp.float32
    )


def block_mask(doc_row, first_row, block_rows):
    length = doc_row.shape[0]
    query_docs = lax.dynamic_slice_in_dim(doc_row, first_row, block_rows, 0)
    query_pos = first_row + jnp.arange(block_rows, dtype=jnp.int32)
    key_pos = jnp.arange(length, dtype=jnp.int32)
    return (query_docs[:, None] == doc_row[None, :]) & (query_pos[:, None] >= key_pos[None, :])


def masked_scores(query_part, key_heads, allowed):
    scores = jnp.einsum(
        "qhd,khd->hqk", query_part, key_heads, preferred_element_type=jnp.float32
    ) * HEAD_DIM ** (-0.5)
    scores = scores.astype(jnp.bfloat16).astype(jnp.float32)
    return jnp.where(allowed[None, :, :], scores, MASK_FILL)


def attend(query_heads, key_heads, value_heads, doc_row):
    length = query_heads.shape[0]
    block_rows = min(512, length)

    def one_block(block_index):
        first_row = block_index * block_rows
        query_part = lax.dynamic_slice_in_dim(query_heads, first_row, block_rows, 0)
        scores = masked_scores(query_part, key_heads, block_mask(doc_row, first_row, block_rows))
        row_max = jnp.max(scores, axis=-1, keepdims=True)
        log_total = row_max + jnp.log(jnp.sum(jnp.exp(scores - row_max), axis=-1, keepdims=True))
        prob_soft = jnp.exp(scores - log_total).astype(jnp.bfloat16)
        result = jnp.einsum(
            "hqk,khd->qhd", prob_soft, value_heads, preferred_element_type=jnp.float32
        )
        return (result.astype(jnp.bfloat16), log_total[..., 0])

    results, log_totals = lax.map(one_block, jnp.arange(length // block_rows, dtype=jnp.int32))
    return (results.reshape(length, 1, -1), log_totals)


def attend_back(query_heads, key_heads, value_heads, grad_heads, log_totals, doc_row):
    length = query_heads.shape[0]
    block_rows = min(512, length)
    scale = HEAD_DIM ** (-0.5)

    def block_step(running, block_item):
        block_index, log_part = block_item
        first_row = block_index * block_rows
        query_part = lax.dynamic_slice_in_dim(query_heads, first_row, block_rows, 0)
        grad_part = lax.dynamic_slice_in_dim(grad_heads, first_row, block_rows, 0)
        scores = masked_scores(query_part, key_heads, block_mask(doc_row, first_row, block_rows))
        prob_soft = jnp.exp(scores - log_part[..., None])
        grad_value = running[1] + jnp.einsum(
            "hqk,qhd->khd",
            prob_soft.astype(jnp.bfloat16),
            grad_part,
            preferred_element_type=jnp.float32,
        )
        grad_prob = jnp.einsum(
            "qhd,khd->hqk", grad_part, value_heads, preferred_element_type=jnp.float32
        )
        row_delta = jnp.sum(prob_soft * grad_prob, axis=-1, keepdims=True)
        grad_score = (prob_soft * (grad_prob - row_delta)).astype(jnp.bfloat16)
        grad_query = (
            jnp.einsum("hqk,khd->qhd", grad_score, key_heads, preferred_element_type=jnp.float32)
            * scale
        )
        grad_key = (
            running[0]
            + jnp.einsum("hqk,qhd->khd", grad_score, query_part, preferred_element_type=jnp.float32)
            * scale
        )
        return ((grad_key, grad_value), grad_query)

    zeros_kv = jnp.zeros(key_heads.shape, jnp.float32)
    (grad_key, grad_value), grad_query = lax.scan(
        block_step,
        (zeros_kv, zeros_kv),
        (jnp.arange(length // block_rows, dtype=jnp.int32), log_totals),
    )
    grad_query = grad_query.reshape(length, 1, -1).astype(jnp.bfloat16)
    return (
        grad_query,
        grad_key.reshape(length, 1, -1).astype(jnp.bfloat16),
        grad_value.reshape(length, 1, -1).astype(jnp.bfloat16),
    )


def norm_back(grad_normed, values, inverse, gain):
    scaled = grad_normed * gain.astype(jnp.float32)
    grad_gain = jnp.sum(grad_normed * values * inverse, axis=0)
    grad_values = inverse * scaled - values * inverse**3 * jnp.mean(
        scaled * values, axis=-1, keepdims=True
    )
    return (grad_gain, grad_values)


def forward(gathered, inputs, doc_row, cosine, sine_part, seq_count):
    w_query, w_key, w_value, w_out, w_gate, w_up, w_down, gain_attn, gain_ffn = gathered
    tok_local = inputs.shape[0]
    feat_width = inputs.shape[1]
    length = tok_local * seq_count
    resid = inputs.astype(jnp.float32)
    inv_first = lax.rsqrt(jnp.mean(resid * resid, axis=-1, keepdims=True) + EPSILON)
    normed = (resid * inv_first * gain_attn.astype(jnp.float32)).astype(jnp.bfloat16)

    def rotated(weight):
        linear = jnp.dot(normed, weight, preferred_element_type=jnp.float32).reshape(
            tok_local, -1, HEAD_DIM
        )
        return (
            rotate(linear, cosine, sine_part).astype(jnp.bfloat16).reshape(tok_local, seq_count, -1)
        )

    queries = rotated(w_query)
    key_rot = rotated(w_key)
    values = (
        jnp.dot(normed, w_value, preferred_element_type=jnp.float32)
        .astype(jnp.bfloat16)
        .reshape(tok_local, seq_count, -1)
    )
    query_heads, key_heads, value_heads = (
        lax.all_to_all(queries, "seq", split_axis=1, concat_axis=0, tiled=True),
        lax.all_to_all(key_rot, "seq", split_axis=1, concat_axis=0, tiled=True),
        lax.all_to_all(values, "seq", split_axis=1, concat_axis=0, tiled=True),
    )
    query_heads = query_heads.reshape(length, -1, HEAD_DIM)
    key_heads = key_heads.reshape(length, -1, HEAD_DIM)
    value_heads = value_heads.reshape(length, -1, HEAD_DIM)
    attended, log_totals = attend(query_heads, key_heads, value_heads, doc_row)
    joined = lax.all_to_all(attended, "seq", split_axis=0, concat_axis=1, tiled=True).reshape(
        tok_local, feat_width
    )
    middle = resid + jnp.dot(joined, w_out, preferred_element_type=jnp.float32)
    inv_second = lax.rsqrt(jnp.mean(middle * middle, axis=-1, keepdims=True) + EPSILON)
    normed_two = (middle * inv_second * gain_ffn.astype(jnp.float32)).astype(jnp.bfloat16)
    gate_proj = jnp.dot(normed_two, w_gate, preferred_element_type=jnp.float32)
    up_proj = jnp.dot(normed_two, w_up, preferred_element_type=jnp.float32)
    hidden = (jax.nn.silu(gate_proj) * up_proj).astype(jnp.bfloat16)
    result = (middle + jnp.dot(hidden, w_down, preferred_element_type=jnp.float32)).astype(
        jnp.bfloat16
    )
    stored = (
        resid,
        inv_first,
        normed,
        query_heads,
        key_heads,
        value_heads,
        log_totals,
        joined,
        middle,
        inv_second,
        normed_two,
        gate_proj,
        up_proj,
        hidden,
    )
    return (stored, result)


def backward(gathered, stored, grad_result, doc_row, cosine, sine_part, seq_count):
    w_query, w_key, w_value, w_out, w_gate, w_up, w_down, gain_attn, gain_ffn = gathered
    (
        resid,
        inv_first,
        normed,
        query_heads,
        key_heads,
        value_heads,
        log_totals,
        joined,
        middle,
        inv_second,
        normed_two,
        gate_proj,
        up_proj,
        hidden,
    ) = stored
    tok_local = grad_result.shape[0]
    feat_width = grad_result.shape[1]
    length = tok_local * seq_count
    grad_down_w = outer_sum(hidden, grad_result)
    grad_hidden = contract(grad_result, w_down)
    sigmoid_gate = jax.nn.sigmoid(gate_proj)
    grad_gate = (
        grad_hidden * up_proj * sigmoid_gate * (1.0 + gate_proj * (1.0 - sigmoid_gate))
    ).astype(jnp.bfloat16)
    grad_upper = (grad_hidden * gate_proj * sigmoid_gate).astype(jnp.bfloat16)
    grad_gate_w = outer_sum(normed_two, grad_gate)
    grad_up_w = outer_sum(normed_two, grad_upper)
    grad_norm_two = contract(grad_gate, w_gate) + contract(grad_upper, w_up)
    grad_gain_ffn, grad_mid = norm_back(grad_norm_two, middle, inv_second, gain_ffn)
    grad_mid = grad_result.astype(jnp.float32) + grad_mid
    grad_branch = grad_mid.astype(jnp.bfloat16)
    grad_out_w = outer_sum(joined, grad_branch)
    grad_joined = (
        contract(grad_branch, w_out).astype(jnp.bfloat16).reshape(tok_local, seq_count, -1)
    )
    grad_heads = lax.all_to_all(
        grad_joined, "seq", split_axis=1, concat_axis=0, tiled=True
    ).reshape(length, -1, HEAD_DIM)
    grad_qh, grad_kh, grad_vh = attend_back(
        query_heads, key_heads, value_heads, grad_heads, log_totals, doc_row
    )
    grad_qt, grad_kt, grad_vt = (
        lax.all_to_all(grad_qh, "seq", split_axis=0, concat_axis=1, tiled=True),
        lax.all_to_all(grad_kh, "seq", split_axis=0, concat_axis=1, tiled=True),
        lax.all_to_all(grad_vh, "seq", split_axis=0, concat_axis=1, tiled=True),
    )
    grad_qt = (
        unrotate(grad_qt.reshape(tok_local, -1, HEAD_DIM).astype(jnp.float32), cosine, sine_part)
        .astype(jnp.bfloat16)
        .reshape(tok_local, feat_width)
    )
    grad_kt = (
        unrotate(grad_kt.reshape(tok_local, -1, HEAD_DIM).astype(jnp.float32), cosine, sine_part)
        .astype(jnp.bfloat16)
        .reshape(tok_local, feat_width)
    )
    grad_vt = grad_vt.reshape(tok_local, feat_width)
    grad_query_w = outer_sum(normed, grad_qt)
    grad_key_w = outer_sum(normed, grad_kt)
    grad_value_w = outer_sum(normed, grad_vt)
    grad_normed = contract(grad_qt, w_query) + contract(grad_kt, w_key) + contract(grad_vt, w_value)
    grad_gain_attn, grad_first = norm_back(grad_normed, resid, inv_first, gain_attn)
    grad_inputs = grad_mid + grad_first
    return (
        grad_inputs,
        (
            grad_query_w,
            grad_key_w,
            grad_value_w,
            grad_out_w,
            grad_gate_w,
            grad_up_w,
            grad_down_w,
            grad_gain_attn,
            grad_gain_ffn,
        ),
    )


def per_device(
    tokens,
    doc_ids,
    cotangent,
    w_query,
    w_key,
    w_value,
    w_out,
    w_gate,
    w_up,
    w_down,
    gain_attn,
    gain_ffn,
):
    seq_count = lax.axis_size("seq")
    seq_rank = lax.axis_index("seq")
    fsdp_count = lax.axis_size("fsdp")
    tok_local = tokens.shape[2]
    doc_all = lax.all_gather(doc_ids, "seq", axis=2, tiled=True)
    positions = (seq_rank * tok_local + jnp.arange(tok_local, dtype=jnp.int32)).astype(jnp.float32)
    cosine, sine_part = rope_tables(positions, HEAD_DIM)
    shards = (w_query, w_key, w_value, w_out, w_gate, w_up, w_down, gain_attn, gain_ffn)

    def micro_step(totals, item):
        tok_part, doc_part, cot_part = item
        gathered = (
            lax.all_gather(w_query, "fsdp", axis=0, tiled=True),
            lax.all_gather(w_key, "fsdp", axis=0, tiled=True),
            lax.all_gather(w_value, "fsdp", axis=0, tiled=True),
            lax.all_gather(w_out, "fsdp", axis=0, tiled=True),
            lax.all_gather(w_gate, "fsdp", axis=0, tiled=True),
            lax.all_gather(w_up, "fsdp", axis=0, tiled=True),
            lax.all_gather(w_down, "fsdp", axis=0, tiled=True),
            lax.all_gather(gain_attn, "fsdp", axis=0, tiled=True),
            lax.all_gather(gain_ffn, "fsdp", axis=0, tiled=True),
        )
        stored, result = forward(gathered, tok_part, doc_part, cosine, sine_part, seq_count)
        gathered = (
            lax.all_gather(w_query, "fsdp", axis=0, tiled=True),
            lax.all_gather(w_key, "fsdp", axis=0, tiled=True),
            lax.all_gather(w_value, "fsdp", axis=0, tiled=True),
            lax.all_gather(w_out, "fsdp", axis=0, tiled=True),
            lax.all_gather(w_gate, "fsdp", axis=0, tiled=True),
            lax.all_gather(w_up, "fsdp", axis=0, tiled=True),
            lax.all_gather(w_down, "fsdp", axis=0, tiled=True),
            lax.all_gather(gain_attn, "fsdp", axis=0, tiled=True),
            lax.all_gather(gain_ffn, "fsdp", axis=0, tiled=True),
        )
        grad_inputs, grads = backward(
            gathered, stored, cot_part, doc_part, cosine, sine_part, seq_count
        )
        totals = jax.tree.map(jnp.add, totals, grads)
        return (totals, (result, grad_inputs))

    zeros_all = tuple(
        (
            jnp.zeros((piece.shape[0] * fsdp_count,) + piece.shape[1:], jnp.float32)
            for piece in shards
        )
    )
    totals, (results, grad_inputs) = lax.scan(
        micro_step, zeros_all, (tokens[:, 0], doc_all[:, 0], cotangent[:, 0])
    )
    (
        sum_query,
        sum_key,
        sum_value,
        sum_out,
        sum_gate,
        sum_up,
        sum_down,
        sum_gain_attn,
        sum_gain_ffn,
    ) = totals
    owned = (
        lax.psum_scatter(sum_query, "fsdp", scatter_dimension=0, tiled=True),
        lax.psum_scatter(sum_key, "fsdp", scatter_dimension=0, tiled=True),
        lax.psum_scatter(sum_value, "fsdp", scatter_dimension=0, tiled=True),
        lax.psum_scatter(sum_out, "fsdp", scatter_dimension=0, tiled=True),
        lax.psum_scatter(sum_gate, "fsdp", scatter_dimension=0, tiled=True),
        lax.psum_scatter(sum_up, "fsdp", scatter_dimension=0, tiled=True),
        lax.psum_scatter(sum_down, "fsdp", scatter_dimension=0, tiled=True),
        lax.psum_scatter(sum_gain_attn, "fsdp", scatter_dimension=0, tiled=True),
        lax.psum_scatter(sum_gain_ffn, "fsdp", scatter_dimension=0, tiled=True),
    )
    owned = (
        lax.psum(owned[0].astype(jnp.bfloat16), "seq").astype(jnp.float32),
        lax.psum(owned[1].astype(jnp.bfloat16), "seq").astype(jnp.float32),
        lax.psum(owned[2].astype(jnp.bfloat16), "seq").astype(jnp.float32),
        lax.psum(owned[3].astype(jnp.bfloat16), "seq").astype(jnp.float32),
        lax.psum(owned[4].astype(jnp.bfloat16), "seq").astype(jnp.float32),
        lax.psum(owned[5].astype(jnp.bfloat16), "seq").astype(jnp.float32),
        lax.psum(owned[6].astype(jnp.bfloat16), "seq").astype(jnp.float32),
        lax.psum(owned[7].astype(jnp.bfloat16), "seq").astype(jnp.float32),
        lax.psum(owned[8].astype(jnp.bfloat16), "seq").astype(jnp.float32),
    )
    output = results[:, None]
    grad_tokens = grad_inputs[:, None]
    return (
        output,
        grad_tokens,
        owned[0],
        owned[1],
        owned[2],
        owned[3],
        owned[4],
        owned[5],
        owned[6],
        owned[7],
        owned[8],
    )


def solution(mesh):
    placed = (
        P(None, "fsdp", "seq", None),
        P(None, "fsdp", "seq"),
        P(None, "fsdp", "seq", None),
        P("fsdp", None),
        P("fsdp", None),
        P("fsdp", None),
        P("fsdp", None),
        P("fsdp", None),
        P("fsdp", None),
        P("fsdp", None),
        P("fsdp"),
        P("fsdp"),
    )
    return jax.shard_map(
        per_device,
        mesh=mesh,
        in_specs=placed,
        out_specs=(
            P(None, "fsdp", "seq", None),
            P(None, "fsdp", "seq", None),
            P("fsdp", None),
            P("fsdp", None),
            P("fsdp", None),
            P("fsdp", None),
            P("fsdp", None),
            P("fsdp", None),
            P("fsdp", None),
            P("fsdp"),
            P("fsdp"),
        ),
        check_vma=False,
    )
```

profile of v0, /device:TPU:0, one launch (start us, length us, event | category | flops | bytes accessed | tf_op | source)
XLA Modules:
  0.0 1526.7 jit_solution(355786102639467229)
XLA Ops:
  15.1 926.1 %while.68 = (s32[]{:T(128)}, f32[768,768]{1,0:T(8,128)}, f32[768,768]{1,0:T(8,128)}, f32[768,768]{1,0:T(8,128)}, f32[768,768]{1,0:T(8,128)}, /*index=5*/f32[768,...) while((s32[]{:T(128)}, f32[768,768]{1,0:T(8,128)}, ...), condition=%wide.region_14.15_spmd.clone.clone.clone, body=%wide.region_0.14_spmd.clone.clone.clone.sunk | while | flops 24734355456 | bytes 710367488 | solution.py:361
  22.9 33.6 %all-reduce.15 = (bf16[768]{0:T(1024)(128)(2,1)S(1)}, bf16[768]{0:T(1024)(128)(2,1)}) all-reduce(bf16[768]{0:T(1024)(128)(2,1)S(1)} %dynamic-update-slice.10, bf16[768]{0:T(1024)(128)(2,1)S(1)} %dynamic-update-slice.11), channel_id=1, replica_groups=mesh['seq'=2,'fsdp'=16] {'fsdp'}, use_global_device_ids=true, to_apply=%add | all-reduce | flops 1536 | bytes 6144 | tf_op jit(solution)/shard_map/while
  67.0 30.9 %all-gather.10.cloned.1.call-done = bf16[768,768]{1,0:T(8,128)(2,1)} async-done(((bf16[48,768]{1,0:T(8,128)(2,1)}), bf16[768,768]{1,0:T(8,128)(2,1)}) %all-gather.10.cloned.1.call-update) | async-done | bytes 1179664 | tf_op jit(solution)/shard_map/while/body/eval_jaxpr/all_gather | solution.py:327
  99.7 37.8 %all-gather.8.cloned.1.call-done = bf16[768,768]{1,0:T(8,128)(2,1)} async-done(((bf16[48,768]{1,0:T(8,128)(2,1)}), bf16[768,768]{1,0:T(8,128)(2,1)}) %all-gather.8.cloned.1.call-update) | async-done | bytes 1179664 | tf_op jit(solution)/shard_map/while/body/eval_jaxpr/all_gather | solution.py:328
  148.1 10.4 all-to-all-done
  174.1 25.4 %while.69 = (s32[]{:T(128)}, bf16[2,512,6,64]{1,3,2,0:T(8,128)(2,1)}, f32[2,6,512]{2,1,0:T(8,128)S(1)}, s32[2]{0:T(128)S(1)}, s32[1024]{0:T(1024)S(1)}, /*index=...) while((s32[]{:T(128)}, ...), condition=%wide.region_5.5_spmd, body=%wide.region_2.4_spmd.sunk | while | flops 847967744 | bytes 29755652 | solution.py:94
  209.7 9.9 all-to-all-done.3
  238.0 31.2 %all-gather.16.cloned.1.call-done = bf16[768,2048]{1,0:T(8,128)(2,1)} async-done(((bf16[48,2048]{1,0:T(8,128)(2,1)}), bf16[768,2048]{1,0:T(8,128)(2,1)}) %all-gather.16.cloned.1.call-update) | async-done | bytes 3145744 | tf_op jit(solution)/shard_map/while/body/eval_jaxpr/all_gather | solution.py:331
  275.1 40.2 %all-gather.20.cloned.1.call-done = bf16[768,2048]{1,0:T(8,128)(2,1)} async-done(((bf16[48,2048]{1,0:T(8,128)(2,1)}), bf16[768,2048]{1,0:T(8,128)(2,1)}) %all-gather.20.cloned.1.call-update) | async-done | bytes 3145744 | tf_op jit(solution)/shard_map/while/body/eval_jaxpr/all_gather | solution.py:332
  315.3 9.2 multiply_convert_fusion.12
  360.6 39.1 %while.70 = (s32[]{:T(128)}, f32[1024,6,64]{0,2,1:T(8,128)S(1)}, f32[1024,6,64]{0,2,1:T(8,128)}, bf16[2,512,6,64]{1,3,2,0:T(8,128)(2,1)}, s32[2]{0:T(128)S(1)}, ...) while((s32[]{:T(128)}, f32[1024,6,64]{0,2,1:T(8,128)S(1)}, ...), condition=%wide.region_10.10_spmd.clone, body=%wide.region_8.9_spmd.clone.sunk | while | flops 2070476288 | bytes 107588008 | solution.py:133
  483.6 30.2 %all-reduce.15 = (bf16[768]{0:T(1024)(128)(2,1)S(1)}, bf16[768]{0:T(1024)(128)(2,1)}) all-reduce(bf16[768]{0:T(1024)(128)(2,1)S(1)} %dynamic-update-slice.10, bf16[768]{0:T(1024)(128)(2,1)S(1)} %dynamic-update-slice.11), channel_id=1, replica_groups=mesh['seq'=2,'fsdp'=16] {'fsdp'}, use_global_device_ids=true, to_apply=%add | all-reduce | flops 1536 | bytes 6144 | tf_op jit(solution)/shard_map/while
  524.2 29.9 %all-gather.10.cloned.1.call-done = bf16[768,768]{1,0:T(8,128)(2,1)} async-done(((bf16[48,768]{1,0:T(8,128)(2,1)}), bf16[768,768]{1,0:T(8,128)(2,1)}) %all-gather.10.cloned.1.call-update) | async-done | bytes 1179664 | tf_op jit(solution)/shard_map/while/body/eval_jaxpr/all_gather | solution.py:327
  555.8 37.6 %all-gather.8.cloned.1.call-done = bf16[768,768]{1,0:T(8,128)(2,1)} async-done(((bf16[48,768]{1,0:T(8,128)(2,1)}), bf16[768,768]{1,0:T(8,128)(2,1)}) %all-gather.8.cloned.1.call-update) | async-done | bytes 1179664 | tf_op jit(solution)/shard_map/while/body/eval_jaxpr/all_gather | solution.py:328
  604.1 10.4 all-to-all-done
  630.1 25.4 %while.69 = (s32[]{:T(128)}, bf16[2,512,6,64]{1,3,2,0:T(8,128)(2,1)}, f32[2,6,512]{2,1,0:T(8,128)S(1)}, s32[2]{0:T(128)S(1)}, s32[1024]{0:T(1024)S(1)}, /*index=...) while((s32[]{:T(128)}, ...), condition=%wide.region_5.5_spmd, body=%wide.region_2.4_spmd.sunk | while | flops 847967744 | bytes 29755652 | solution.py:94
  665.7 9.9 all-to-all-done.3
  694.0 31.3 %all-gather.16.cloned.1.call-done = bf16[768,2048]{1,0:T(8,128)(2,1)} async-done(((bf16[48,2048]{1,0:T(8,128)(2,1)}), bf16[768,2048]{1,0:T(8,128)(2,1)}) %all-gather.16.cloned.1.call-update) | async-done | bytes 3145744 | tf_op jit(solution)/shard_map/while/body/eval_jaxpr/all_gather | solution.py:331
  731.3 40.0 %all-gather.20.cloned.1.call-done = bf16[768,2048]{1,0:T(8,128)(2,1)} async-done(((bf16[48,2048]{1,0:T(8,128)(2,1)}), bf16[768,2048]{1,0:T(8,128)(2,1)}) %all-gather.20.cloned.1.call-update) | async-done | bytes 3145744 | tf_op jit(solution)/shard_map/while/body/eval_jaxpr/all_gather | solution.py:332
  771.3 9.2 multiply_convert_fusion.12
  794.9 8.3 select_add_fusion.22
  803.3 7.4 select_add_fusion.21
  810.7 7.2 select_add_fusion.23
  824.2 39.1 %while.70 = (s32[]{:T(128)}, f32[1024,6,64]{0,2,1:T(8,128)S(1)}, f32[1024,6,64]{0,2,1:T(8,128)}, bf16[2,512,6,64]{1,3,2,0:T(8,128)(2,1)}, s32[2]{0:T(128)S(1)}, ...) while((s32[]{:T(128)}, f32[1024,6,64]{0,2,1:T(8,128)S(1)}, ...), condition=%wide.region_10.10_spmd.clone, body=%wide.region_8.9_spmd.clone.sunk | while | flops 2070476288 | bytes 107588008 | solution.py:133
  945.8 60.5 %reduce-scatter.8.cloned.1.call-done = f32[48,768]{1,0:T(8,128)} async-done(((f32[768,768]{1,0:T(8,128)}), f32[48,768]{1,0:T(8,128)}) %reduce-scatter.8.cloned.1.call-update) | async-done | bytes 147472 | tf_op jit(solution)/shard_map/reduce_scatter | solution.py:376
  1007.9 64.5 %reduce-scatter.10.cloned.1.call-done = f32[48,768]{1,0:T(8,128)} async-done(((f32[768,768]{1,0:T(8,128)}), f32[48,768]{1,0:T(8,128)}) %reduce-scatter.10.cloned.1.call-update) | async-done | bytes 147472 | tf_op jit(solution)/shard_map/reduce_scatter | solution.py:377
  1073.9 64.5 %reduce-scatter.12.cloned.1.call-done = f32[48,768]{1,0:T(8,128)} async-done(((f32[768,768]{1,0:T(8,128)}), f32[48,768]{1,0:T(8,128)}) %reduce-scatter.12.cloned.1.call-update) | async-done | bytes 147472 | tf_op jit(solution)/shard_map/reduce_scatter | solution.py:378
  1140.0 64.7 %reduce-scatter.14.cloned.1.call-done = f32[48,768]{1,0:T(8,128)} async-done(((f32[768,768]{1,0:T(8,128)}), f32[48,768]{1,0:T(8,128)}) %reduce-scatter.14.cloned.1.call-update) | async-done | bytes 147472 | tf_op jit(solution)/shard_map/reduce_scatter | solution.py:379
  1206.2 86.4 %reduce-scatter.16.cloned.1.call-done = f32[48,2048]{1,0:T(8,128)} async-done(((f32[768,2048]{1,0:T(8,128)}), f32[48,2048]{1,0:T(8,128)}) %reduce-scatter.16.cloned.1.call-update) | async-done | bytes 393232 | tf_op jit(solution)/shard_map/reduce_scatter | solution.py:380
  1294.3 86.3 %reduce-scatter.18.cloned.1.call-done = f32[48,2048]{1,0:T(8,128)} async-done(((f32[768,2048]{1,0:T(8,128)}), f32[48,2048]{1,0:T(8,128)}) %reduce-scatter.18.cloned.1.call-update) | async-done | bytes 393232 | tf_op jit(solution)/shard_map/reduce_scatter | solution.py:381
  1382.4 86.2 %reduce-scatter.20.cloned.1.call-done = f32[128,768]{1,0:T(8,128)} async-done(((f32[2048,768]{1,0:T(8,128)}), f32[128,768]{1,0:T(8,128)}) %reduce-scatter.20.cloned.1.call-update) | async-done | bytes 393232 | tf_op jit(solution)/shard_map/reduce_scatter | solution.py:382
  1471.5 31.2 %all-reduce.11 = (bf16[768]{0:T(1024)(128)(2,1)S(1)}, bf16[768]{0:T(1024)(128)(2,1)S(1)}) all-reduce(f32[768]{0:T(1024)S(1)} %copy-done.50, f32[768]{0:T(1024)S(1)} %copy-done.47), channel_id=9, replica_groups=mesh['seq'=2,'fsdp'=16] {'fsdp'}, use_global_device_ids=true, to_apply=%region_29.30.clone | all-reduce | flops 1536 | bytes 9216
  (653 shorter events, 528.7 us)
Async XLA Ops:
  15.4 44.8 %all-gather.12.cloned.1.call-start = ((), (), s32[]{:S(2)}) async-start(), calls=%async_computation.25 | async-start | bytes 1253376 | tf_op jit(solution)/shard_map/while/body/eval_jaxpr/all_gather | solution.py:329
  16.1 81.9 %all-gather.10.cloned.1.call-start = ((), (), s32[]{:S(2)}) async-start(), calls=%async_computation.24 | async-start | bytes 1253376 | tf_op jit(solution)/shard_map/while/body/eval_jaxpr/all_gather | solution.py:327
  16.9 120.6 %all-gather.8.cloned.1.call-start = ((), (), s32[]{:S(2)}) async-start(), calls=%async_computation.23 | async-start | bytes 1253376 | tf_op jit(solution)/shard_map/while/body/eval_jaxpr/all_gather | solution.py:328
  17.6 209.3 %all-gather.14.cloned.1.call-start = ((), (), s32[]{:S(2)}) async-start(), calls=%async_computation.26 | async-start | bytes 1253376 | tf_op jit(solution)/shard_map/while/body/eval_jaxpr/all_gather | solution.py:330
  18.2 213.7 %all-gather.18.cloned.1.call-start = ((), (), s32[]{:S(2)}) async-start(), calls=%async_computation.28 | async-start | bytes 3342336 | tf_op jit(solution)/shard_map/while/body/eval_jaxpr/all_gather | solution.py:345
  18.8 250.4 %all-gather.16.cloned.1.call-start = ((), (), s32[]{:S(2)}) async-start(), calls=%async_computation.27 | async-start | bytes 3342336 | tf_op jit(solution)/shard_map/while/body/eval_jaxpr/all_gather | solution.py:331
  63.5 80.1 %all-to-all-start.2 = ((bf16[512,2,384]{2,0,1:T(8,128)(2,1)}), bf16[512,2,384]{2,0,1:T(8,128)(2,1)S(1)}, u32[]{:S(2)}, u32[]{:S(2)}) async-start(bf16[512,2,384]{2,0,1:T(8,128)(2,1)} %bitcast.348), calls=%async_computation.2 | async-start | bytes 1572864 | tf_op jit(solution)/shard_map/while/body/eval_jaxpr/all_to_all | solution.py:182
  143.6 15.0 all-to-all-start
  162.1 153.2 %all-gather.20.cloned.1.call-start = ((), (), s32[]{:S(2)}) async-start(), calls=%async_computation.29 | async-start | bytes 3342336 | tf_op jit(solution)/shard_map/while/body/eval_jaxpr/all_gather | solution.py:332
  334.2 20.2 %all-to-all-start.4 = ((bf16[512,2,384]{2,0,1:T(8,128)(2,1)}), bf16[512,2,384]{2,0,1:T(8,128)(2,1)}, u32[]{:S(2)}, u32[]{:S(2)}) async-start(bf16[512,2,384]{2,0,1:T(8,128)(2,1)} %bitcast.390), calls=%async_computation.4 | async-start | bytes 1572864 | tf_op jit(solution)/shard_map/while/body/eval_jaxpr/all_to_all | solution.py:257
  409.1 15.9 %all-to-all-start.6 = ((bf16[2,2,98304]{2,1,0:T(2,128)(2,1)}), bf16[2,2,98304]{2,1,0:T(2,128)(2,1)}, u32[]{:S(2)}, u32[]{:S(2)}) async-start(bf16[2,2,98304]{2,1,0:T(2,128)(2,1)} %reshape.564), calls=%async_computation.6 | async-start | bytes 1572864 | tf_op jit(solution)/shard_map/while/body/eval_jaxpr/all_to_all | solution.py:264
  425.0 15.0 all-to-all-start.5
  475.8 41.5 %all-gather.12.cloned.1.call-start = ((), (), s32[]{:S(2)}) async-start(), calls=%async_computation.25 | async-start | bytes 1253376 | tf_op jit(solution)/shard_map/while/body/eval_jaxpr/all_gather | solution.py:329
  476.6 77.5 %all-gather.10.cloned.1.call-start = ((), (), s32[]{:S(2)}) async-start(), calls=%async_computation.24 | async-start | bytes 1253376 | tf_op jit(solution)/shard_map/while/body/eval_jaxpr/all_gather | solution.py:327
  477.3 116.1 %all-gather.8.cloned.1.call-start = ((), (), s32[]{:S(2)}) async-start(), calls=%async_computation.23 | async-start | bytes 1253376 | tf_op jit(solution)/shard_map/while/body/eval_jaxpr/all_gather | solution.py:328
  477.9 205.1 %all-gather.14.cloned.1.call-start = ((), (), s32[]{:S(2)}) async-start(), calls=%async_computation.26 | async-start | bytes 1253376 | tf_op jit(solution)/shard_map/while/body/eval_jaxpr/all_gather | solution.py:330
  478.7 209.3 %all-gather.18.cloned.1.call-start = ((), (), s32[]{:S(2)}) async-start(), calls=%async_computation.28 | async-start | bytes 3342336 | tf_op jit(solution)/shard_map/while/body/eval_jaxpr/all_gather | solution.py:345
  479.2 246.1 %all-gather.16.cloned.1.call-start = ((), (), s32[]{:S(2)}) async-start(), calls=%async_computation.27 | async-start | bytes 3342336 | tf_op jit(solution)/shard_map/while/body/eval_jaxpr/all_gather | solution.py:331
  520.7 78.8 %all-to-all-start.2 = ((bf16[512,2,384]{2,0,1:T(8,128)(2,1)}), bf16[512,2,384]{2,0,1:T(8,128)(2,1)S(1)}, u32[]{:S(2)}, u32[]{:S(2)}) async-start(bf16[512,2,384]{2,0,1:T(8,128)(2,1)} %bitcast.348), calls=%async_computation.2 | async-start | bytes 1572864 | tf_op jit(solution)/shard_map/while/body/eval_jaxpr/all_to_all | solution.py:182
  599.5 15.0 all-to-all-start
  618.0 153.3 %all-gather.20.cloned.1.call-start = ((), (), s32[]{:S(2)}) async-start(), calls=%async_computation.29 | async-start | bytes 3342336 | tf_op jit(solution)/shard_map/while/body/eval_jaxpr/all_gather | solution.py:332
  790.2 27.7 %all-to-all-start.4 = ((bf16[512,2,384]{2,0,1:T(8,128)(2,1)}), bf16[512,2,384]{2,0,1:T(8,128)(2,1)}, u32[]{:S(2)}, u32[]{:S(2)}) async-start(bf16[512,2,384]{2,0,1:T(8,128)(2,1)} %bitcast.390), calls=%async_computation.4 | async-start | bytes 1572864 | tf_op jit(solution)/shard_map/while/body/eval_jaxpr/all_to_all | solution.py:257
  872.7 15.8 %all-to-all-start.6 = ((bf16[2,2,98304]{2,1,0:T(2,128)(2,1)}), bf16[2,2,98304]{2,1,0:T(2,128)(2,1)}, u32[]{:S(2)}, u32[]{:S(2)}) async-start(bf16[2,2,98304]{2,1,0:T(2,128)(2,1)} %reshape.564), calls=%async_computation.6 | async-start | bytes 1572864 | tf_op jit(solution)/shard_map/while/body/eval_jaxpr/all_to_all | solution.py:264
  888.6 15.0 all-to-all-start.5
  941.2 65.1 %reduce-scatter.8.cloned.1.call-start = ((), (), s32[]{:S(2)}) async-start(), calls=%async_computation.15 | async-start | bytes 2506752 | tf_op jit(solution)/shard_map/reduce_scatter | solution.py:376
  941.8 130.6 %reduce-scatter.10.cloned.1.call-start = ((), (), s32[]{:S(2)}) async-start(), calls=%async_computation.16 | async-start | bytes 2506752 | tf_op jit(solution)/shard_map/reduce_scatter | solution.py:377
  942.4 196.1 %reduce-scatter.12.cloned.1.call-start = ((), (), s32[]{:S(2)}) async-start(), calls=%async_computation.17 | async-start | bytes 2506752 | tf_op jit(solution)/shard_map/reduce_scatter | solution.py:378
  942.9 261.7 %reduce-scatter.14.cloned.1.call-start = ((), (), s32[]{:S(2)}) async-start(), calls=%async_computation.18 | async-start | bytes 2506752 | tf_op jit(solution)/shard_map/reduce_scatter | solution.py:379
  943.7 349.0 %reduce-scatter.16.cloned.1.call-start = ((), (), s32[]{:S(2)}) async-start(), calls=%async_computation.19 | async-start | bytes 6684672 | tf_op jit(solution)/shard_map/reduce_scatter | solution.py:380
  944.4 436.2 %reduce-scatter.18.cloned.1.call-start = ((), (), s32[]{:S(2)}) async-start(), calls=%async_computation.20 | async-start | bytes 6684672 | tf_op jit(solution)/shard_map/reduce_scatter | solution.py:381
  945.2 523.4 %reduce-scatter.20.cloned.1.call-start = ((), (), s32[]{:S(2)}) async-start(), calls=%async_computation.21 | async-start | bytes 6684672 | tf_op jit(solution)/shard_map/reduce_scatter | solution.py:382
  945.8 563.0 %all-reduce.18.cloned.1.call-start = ((), (), s32[]{:S(2)}) async-start(), calls=%async_computation.22 | async-start | bytes 1769472 | tf_op jit(solution)/shard_map/psum | solution.py:387
  (140 other events, 2750.5 us)
Sparse Core Ops, SparseCore 0:
  18.5 40.1 all-gather.11
  60.9 37.0 all-gather.9
  100.3 37.1 all-gather.7
  139.6 37.0 all-gather.13
  178.9 44.3 all-gather.17
  225.4 43.7 all-gather.15
  271.5 43.7 all-gather.19
  478.9 35.8 all-gather.11
  517.1 36.9 all-gather.9
  556.2 37.1 all-gather.7
  595.7 37.0 all-gather.13
  635.0 44.2 all-gather.17
  681.5 43.7 all-gather.15
  727.5 43.7 all-gather.19
Sparse Core Ops, SparseCore 1:
  945.4 60.8 reduce-scatter.7
  1010.0 62.4 reduce-scatter.9
  1076.0 62.4 reduce-scatter.11
  1142.2 62.4 reduce-scatter.13
  1208.6 83.9 reduce-scatter.15
  1296.6 84.0 reduce-scatter.17
  1384.5 84.0 reduce-scatter.19
  1472.3 35.5 all-reduce.17
where the time goes:
time: 1530 us
  waiting for transfers between devices  870 us (57%)
  matrix products  216 us (14%)
  local copies, waits for them, and re-layouts  146 us (10%)
  blocking collectives  105 us (7%)
  other arithmetic  93.9 us (6%)
  starting transfers between devices  67.6 us (4%)
  between operations  16.3 us (1%)
    reduce_scatter x1, waiting for transfers between devices, per_device(): lax.psum_scatter(sum_gate, 'fsdp', scatter_dimension=0, tiled=True)  86.4 us
    reduce_scatter x1, waiting for transfers between devices, per_device(): lax.psum_scatter(sum_up, 'fsdp', scatter_dimension=0, tiled=True)  86.3 us
    reduce_scatter x1, waiting for transfers between devices, per_device(): lax.psum_scatter(sum_down, 'fsdp', scatter_dimension=0, tiled=True)  86.2 us
    all_gather x2, waiting for transfers between devices, micro_step(): lax.all_gather(w_up, 'fsdp', axis=0, tiled=True)  80.2 us
    all_gather x2, waiting for transfers between devices, micro_step(): lax.all_gather(w_key, 'fsdp', axis=0, tiled=True)  75.5 us
    while x298, local copies, waits for them, and re-layouts  73.3 us
    reduce_scatter x1, waiting for transfers between devices, per_device(): lax.psum_scatter(sum_out, 'fsdp', scatter_dimension=0, tiled=True)  64.7 us
    reduce_scatter x1, waiting for transfers between devices, per_device(): lax.psum_scatter(sum_value, 'fsdp', scatter_dimension=0, tiled=True)  64.5 us
  transfers between devices with their start and end apart: 38, of which 27 were waited for; matrix products, arithmetic and copies ran while one was open for 16% of the time, Pallas kernels for 0%

commit v1 on v0

v1 whole, which is shorter than its diff:
```python
import functools
import math

import jax
import jax.numpy as jnp
from jax import lax
from jax.experimental import pallas as pl
from jax.experimental.pallas import tpu as pltpu
from jax.sharding import PartitionSpec as P

HEAD_DIM = 64
EPSILON = 1e-05
MASK_FILL = -1e30
LONGEST = 512
PAIR = 2 * HEAD_DIM
QBLOCK = 128
TBLOCK = 256
BF = jnp.bfloat16
F32 = jnp.float32
ANY = pl.BlockSpec(memory_space=pl.ANY)


def cost(flops, nbytes, trans=0):
    return pl.CostEstimate(flops=int(flops), bytes_accessed=int(nbytes), transcendentals=int(trans))


def whole(shape):
    zeros = (0,) * len(shape)
    return pl.BlockSpec(shape, lambda *_: zeros)


def dot_nt(left, right):
    return lax.dot_general(left, right, (((1,), (1,)), ((), ())), preferred_element_type=F32)


def dot_nn(left, right):
    return lax.dot_general(left, right, (((1,), (0,)), ((), ())), preferred_element_type=F32)


def swap_halves(values):
    lane = lax.broadcasted_iota(jnp.int32, values.shape, 1)
    width = values.shape[1]
    half = HEAD_DIM // 2
    ahead = pltpu.roll(values, width - half, 1)
    behind = pltpu.roll(values, half, 1)
    return jnp.where((lane & (HEAD_DIM - 1)) < half, ahead, behind)


def wide(table, width):
    return jnp.concatenate([table] * (width // table.shape[1]), axis=1)


def load_copies(pieces, scratch, sems):
    rows = pieces[0].shape[0]
    me = lax.axis_index("fsdp")
    copies = []
    for place, piece in enumerate(pieces):
        if len(pieces) == 1:
            target = scratch
        else:
            owner = lax.bitwise_xor(me, place)
            target = scratch.at[pl.ds(pl.multiple_of(owner * rows, 16), rows), :]
        copies.append(pltpu.make_async_copy(piece, target, sems.at[place]))
    return copies


def rows_of(block):
    return jnp.transpose(block.astype(F32))[0:8, :]


def project_kernel(count, width, *refs):
    x_ref, cos_ref, sin_ref = refs[:3]
    pieces = refs[3 : 3 + count]
    n_ref, q_ref, k_ref, v_ref, gains_ref = refs[3 + count : 8 + count]
    weights, gain, sems = refs[8 + count :]

    @pl.when(pl.program_id(0) == 0)
    def _():
        copies = load_copies(pieces, weights, sems)
        for copy in copies:
            copy.start()
        for copy in copies:
            copy.wait()
        gain[...] = rows_of(weights[:, 3 * width : 3 * width + 128])
        gains_ref[...] = gain[...]

    x = x_ref[...].astype(F32)
    inverse = lax.rsqrt(jnp.mean(x * x, axis=1, keepdims=True) + EPSILON)
    normed = (x * inverse * gain[0:1, :]).astype(BF)
    n_ref[...] = normed
    cosine, sine = cos_ref[...], sin_ref[...]
    for part, out in enumerate((q_ref, k_ref)):
        for at in range(0, width, 256):
            linear = dot_nn(normed, weights[:, part * width + at : part * width + at + 256])
            turned = linear * wide(cosine, 256) + swap_halves(linear) * wide(sine, 256)
            turned = turned.astype(BF)
            if part == 0:
                turned = turned * jnp.asarray(HEAD_DIM**-0.5, BF)
            out[:, at : at + 256] = turned
    v_ref[...] = dot_nn(normed, weights[:, 2 * width : 3 * width]).astype(BF)


def project(x, cosine, sine, pieces):
    tokens, width = x.shape
    total = pieces[0].shape[1]
    shape = jax.ShapeDtypeStruct((tokens, width), BF)
    block = pl.BlockSpec((TBLOCK, width), lambda i: (i, 0))
    table = pl.BlockSpec((TBLOCK, PAIR), lambda i: (i, 0))
    return pl.pallas_call(
        functools.partial(project_kernel, len(pieces), width),
        name="project",
        out_shape=[shape] * 4 + [jax.ShapeDtypeStruct((8, width), F32)],
        grid=(tokens // TBLOCK,),
        in_specs=[block, table, table] + [ANY] * len(pieces),
        out_specs=[block] * 4 + [whole((8, width))],
        scratch_shapes=[
            pltpu.VMEM((width, total), BF),
            pltpu.VMEM((8, width), F32),
            pltpu.SemaphoreType.DMA((len(pieces),)),
        ],
        cost_estimate=cost(6 * tokens * width * width, 6 * width * width + 10 * tokens * width),
    )(x, cosine, sine, *pieces)


def split_heads(values):
    lane = lax.broadcasted_iota(jnp.int32, values.shape, 1)
    zero = jnp.zeros_like(values)
    return jnp.concatenate(
        [jnp.where(lane < HEAD_DIM, values, zero), jnp.where(lane < HEAD_DIM, zero, values)], axis=0
    )


def join_heads(both):
    rows = both.shape[1] // 2
    own = jnp.concatenate([both[:HEAD_DIM, :rows], both[HEAD_DIM:, rows:]], axis=0)
    return jnp.transpose(own)


def masked_bias(starts_row, first_key, span, first_row):
    key = first_key + lax.broadcasted_iota(jnp.int32, (span, QBLOCK), 0)
    query = first_row + lax.broadcasted_iota(jnp.int32, (span, QBLOCK), 1)
    allowed = (key >= starts_row) & (key <= query)
    return jnp.where(allowed, 0.0, MASK_FILL)


def per_span(first_ref, length, body):
    block = pl.program_id(0)
    seen = block - first_ref[block] + 1
    most = min(length, LONGEST + QBLOCK) // QBLOCK
    for blocks in range(1, most + 1):

        @pl.when(seen == blocks)
        def _(blocks=blocks):
            first_key = pl.multiple_of((block - blocks + 1) * QBLOCK, QBLOCK)
            body(blocks * QBLOCK, first_key, block * QBLOCK)


def attend_kernel(pairs, first_ref, q_ref, k_ref, v_ref, starts_ref, out_ref, lse_ref, v_turned, bias):
    @pl.when(pl.program_id(0) == 0)
    def _():
        v_turned[...] = jnp.transpose(v_ref[...])

    def body(span, first_key, first_row):
        bias[:span, :] = masked_bias(starts_ref[...], first_key, span, first_row)
        for pair in range(pairs):
            lanes = slice(pair * PAIR, (pair + 1) * PAIR)
            queries = split_heads(q_ref[:, lanes])
            scores = dot_nt(k_ref[pl.ds(first_key, span), lanes], queries)
            fill = bias[:span, :]
            scores = scores.astype(BF).astype(F32) + jnp.concatenate([fill, fill], axis=1)
            top = jnp.max(scores, axis=0, keepdims=True)
            weights = jnp.exp(scores - top)
            total = jnp.sum(weights, axis=0, keepdims=True)
            lse_ref[0, pair : pair + 1, :] = top + jnp.log(total)
            weights = (weights * (1.0 / total)).astype(BF)
            both = dot_nn(v_turned[lanes, pl.ds(first_key, span)], weights)
            out_ref[:, lanes] = join_heads(both).astype(BF)

    per_span(first_ref, k_ref.shape[0], body)


def attend(queries, keys, values, starts, first):
    length, width = queries.shape
    pairs = width // PAIR
    blocks = length // QBLOCK
    block = pl.BlockSpec((QBLOCK, width), lambda i, f: (i, 0))
    return pl.pallas_call(
        functools.partial(attend_kernel, pairs),
        name="attend",
        out_shape=[
            jax.ShapeDtypeStruct((length, width), BF),
            jax.ShapeDtypeStruct((blocks, pairs, 2 * QBLOCK), F32),
        ],
        grid_spec=pltpu.PrefetchScalarGridSpec(
            num_scalar_prefetch=1,
            grid=(blocks,),
            in_specs=[
                block,
                whole((length, width)),
                whole((length, width)),
                pl.BlockSpec((1, QBLOCK), lambda i, f: (0, i)),
            ],
            out_specs=[block, pl.BlockSpec((1, pairs, 2 * QBLOCK), lambda i, f: (i, 0, 0))],
            scratch_shapes=[
                pltpu.VMEM((width, length), BF),
                pltpu.VMEM((min(length, LONGEST + QBLOCK), QBLOCK), F32),
            ],
        ),
        cost_estimate=cost(4 * length * length * width, 10 * length * width),
    )(first, queries, keys, values, starts)


def attend_back_kernel(
    pairs, first_ref, q_ref, k_ref, v_ref, g_ref, lse_ref, starts_ref, cos_ref, sin_ref, out_ref, k_turned, bias, dk, dv
):
    width = pairs * PAIR
    block = pl.program_id(0)

    @pl.when(block == 0)
    def _():
        k_turned[...] = jnp.transpose(k_ref[...])
        dk[...] = jnp.zeros_like(dk)
        dv[...] = jnp.zeros_like(dv)

    rows = pl.ds(pl.multiple_of(block * QBLOCK, QBLOCK), QBLOCK)
    cosine, sine = cos_ref[rows, :], sin_ref[rows, :]

    def body(span, first_key, first_row):
        bias[:span, :] = masked_bias(starts_ref[...], first_key, span, first_row)
        keys_at = pl.ds(first_key, span)
        for pair in range(pairs):
            lanes = slice(pair * PAIR, (pair + 1) * PAIR)
            queries = split_heads(q_ref[:, lanes])
            grads = split_heads(g_ref[:, lanes])
            scores = dot_nt(k_ref[keys_at, lanes], queries)
            grad_probs = dot_nt(v_ref[keys_at, lanes], grads)
            fill = bias[:span, :]
            scores = scores.astype(BF).astype(F32) + jnp.concatenate([fill, fill], axis=1)
            probs = jnp.exp(scores - lse_ref[0, pair : pair + 1, :])
            dv[keys_at, lanes] += dot_nn(probs.astype(BF), grads)
            delta = jnp.sum(probs * grad_probs, axis=0, keepdims=True)
            grad_scores = (probs * (grad_probs - delta)).astype(BF)
            dk[keys_at, lanes] += dot_nn(grad_scores, queries)
            both = dot_nn(k_turned[lanes, keys_at], grad_scores)
            dq = (join_heads(both) * HEAD_DIM**-0.5).astype(BF).astype(F32)
            out_ref[rows, lanes] = (dq * cosine - swap_halves(dq) * sine).astype(BF)

    per_span(first_ref, k_ref.shape[0], body)

    @pl.when(block == pl.num_programs(0) - 1)
    def _():
        def finish(step, carry):
            at = pl.ds(pl.multiple_of(step * QBLOCK, QBLOCK), QBLOCK)
            turn, slant = cos_ref[at, :], sin_ref[at, :]
            for pair in range(pairs):
                lanes = slice(pair * PAIR, (pair + 1) * PAIR)
                grad = dk[at, lanes].astype(BF).astype(F32)
                out_ref[at, width + pair * PAIR : width + (pair + 1) * PAIR] = (
                    grad * turn - swap_halves(grad) * slant
                ).astype(BF)
            out_ref[at, 2 * width : 3 * width] = dv[at, :].astype(BF)
            return carry

        lax.fori_loop(0, k_ref.shape[0] // QBLOCK, finish, 0)


def attend_back(queries, keys, values, grads, lse, starts, first, cosine, sine):
    length, width = queries.shape
    pairs = width // PAIR
    blocks = length // QBLOCK
    block = pl.BlockSpec((QBLOCK, width), lambda i, f: (i, 0))
    full = whole((length, width))
    table = whole((length, PAIR))
    return pl.pallas_call(
        functools.partial(attend_back_kernel, pairs),
        name="attend_back",
        out_shape=jax.ShapeDtypeStruct((length, 3 * width), BF),
        grid_spec=pltpu.PrefetchScalarGridSpec(
            num_scalar_prefetch=1,
            grid=(blocks,),
            in_specs=[
                block,
                full,
                full,
                block,
                pl.BlockSpec((1, pairs, 2 * QBLOCK), lambda i, f: (i, 0, 0)),
                pl.BlockSpec((1, QBLOCK), lambda i, f: (0, i)),
                table,
                table,
            ],
            out_specs=whole((length, 3 * width)),
            scratch_shapes=[
                pltpu.VMEM((width, length), BF),
                pltpu.VMEM((min(length, LONGEST + QBLOCK), QBLOCK), F32),
                pltpu.VMEM((length, width), F32),
                pltpu.VMEM((length, width), F32),
            ],
        ),
        cost_estimate=cost(10 * length * length * width, 16 * length * width),
    )(first, queries, keys, values, grads, lse, starts, cosine, sine)


def feed_kernel(counts, width, hidden_width, *refs):
    x_ref, att_ref, dy_ref, gain_ref = refs[:4]
    refs = refs[4:]
    first, refs = refs[: counts[0]], refs[counts[0] :]
    second, refs = refs[: counts[1]], refs[counts[1] :]
    y_ref, n_ref, hid_ref, dgate_ref, dup_ref, dm_ref, dmr_ref, datt_ref = refs[:8]
    w_first, w_down, sems_first, sems_second = refs[8:]

    @pl.when(pl.program_id(0) == 0)
    def _():
        copies = load_copies(first, w_first, sems_first) + load_copies(second, w_down, sems_second)
        for copy in copies:
            copy.start()
        for copy in copies:
            copy.wait()

    gain = gain_ref[1:2, :]
    dy = dy_ref[...]
    middle = x_ref[...].astype(F32) + dot_nn(att_ref[...], w_first[:, :width])
    inverse = lax.rsqrt(jnp.mean(middle * middle, axis=1, keepdims=True) + EPSILON)
    normed = (middle * inverse * gain).astype(BF)
    n_ref[...] = normed
    result = middle
    back = jnp.zeros_like(middle)
    step = min(512, hidden_width)
    for at in range(0, hidden_width, step):
        part = slice(at, at + step)
        w_gate = w_first[:, width + at : width + at + step]
        w_up = w_first[:, width + hidden_width + at : width + hidden_width + at + step]
        gate = dot_nn(normed, w_gate)
        up = dot_nn(normed, w_up)
        sigma = 1.0 / (1.0 + jnp.exp(-gate))
        silu = gate * sigma
        hidden = (silu * up).astype(BF)
        hid_ref[:, part] = hidden
        result = result + dot_nn(hidden, w_down[part, :])
        dh = dot_nt(dy, w_down[part, :])
        dgate = (dh * up * sigma * (1.0 + gate * (1.0 - sigma))).astype(BF)
        dup = (dh * silu).astype(BF)
        dgate_ref[:, part] = dgate
        dup_ref[:, part] = dup
        back = back + dot_nt(dgate, w_gate) + dot_nt(dup, w_up)
    y_ref[...] = result.astype(BF)
    scaled = back * gain
    dm = dy.astype(F32) + inverse * scaled - middle * (inverse * inverse * inverse) * jnp.mean(
        scaled * middle, axis=1, keepdims=True
    )
    dm_ref[...] = dm
    dmr = dm.astype(BF)
    dmr_ref[...] = dmr
    datt_ref[...] = dot_nt(dmr, w_first[:, :width]).astype(BF)


def feed(x, attended, dy, gain, first, second, hidden_width):
    tokens, width = x.shape
    block = pl.BlockSpec((TBLOCK, width), lambda i: (i, 0))
    broad = pl.BlockSpec((TBLOCK, hidden_width), lambda i: (i, 0))
    narrow, large = jax.ShapeDtypeStruct((tokens, width), BF), jax.ShapeDtypeStruct((tokens, hidden_width), BF)
    return pl.pallas_call(
        functools.partial(feed_kernel, (len(first), len(second)), width, hidden_width),
        name="feed",
        out_shape=[narrow, narrow, large, large, large, jax.ShapeDtypeStruct((tokens, width), F32), narrow, narrow],
        grid=(tokens // TBLOCK,),
        in_specs=[block, block, block, whole((8, width))] + [ANY] * (len(first) + len(second)),
        out_specs=[block, block, broad, broad, broad, block, block, block],
        scratch_shapes=[
            pltpu.VMEM((width, width + 2 * hidden_width), BF),
            pltpu.VMEM((hidden_width, width), BF),
            pltpu.SemaphoreType.DMA((len(first),)),
            pltpu.SemaphoreType.DMA((len(second),)),
        ],
        cost_estimate=cost(4 * tokens * width * (width + 3 * hidden_width), 20 * tokens * width + 6 * tokens * hidden_width),
    )(x, attended, dy, gain, *first, *second)


def write_pieces(parts, total, keep, send):
    if parts == 1:
        keep[...] = total[...].astype(BF)
        return
    rows = total.shape[0] // parts
    me = lax.axis_index("fsdp")
    for place in range(parts // 2):
        upper, y_bit = place % (parts // 4), place // (parts // 4)
        for core, out in enumerate((keep, send)):
            owner = lax.bitwise_xor(me, upper * 4 + y_bit * 2 + core)
            out[place] = total[pl.ds(pl.multiple_of(owner * rows, 16), rows), :].astype(BF)


def outer_kernel(parts, edges, *refs):
    count = len(edges)
    lefts, rights = refs[:count], refs[count : 2 * count]
    outs = refs[2 * count : -1 - count]
    turned, total = refs[-1 - count : -1], refs[-1]
    step = pl.program_id(0)
    low = 0
    for left, right, turn, high in zip(lefts, rights, turned, edges):

        @pl.when(step == low)
        def _(left=left, turn=turn):
            turn[...] = jnp.transpose(left[...])

        @pl.when((step >= low) & (step < high))
        def _(right=right, turn=turn):
            total[...] = dot_nn(turn[...], right[...])

        low = high
    write_pieces(parts, total, *((outs + (None,))[:2]))


def outer_sums(parts, lefts, rights, name):
    tile = 256
    tokens, rows = lefts[0].shape
    edges, specs, low = [], [], 0
    for right in rights:
        steps = right.shape[1] // tile
        specs.append(
            pl.BlockSpec((tokens, tile), lambda j, low=low, steps=steps: (0, jnp.clip(j - low, 0, steps - 1)))
        )
        low += steps
        edges.append(low)
    width = low * tile
    kept_lefts, kept_edges = [], []
    shape = (rows, width) if parts == 1 else (parts // 2, rows // parts, width)
    out_block = (rows, tile) if parts == 1 else (parts // 2, rows // parts, tile)
    index = (lambda j: (0, j)) if parts == 1 else (lambda j: (0, 0, j))
    n_out = 1 if parts == 1 else 2
    outs = pl.pallas_call(
        functools.partial(outer_kernel, parts, tuple(edges)),
        name=name,
        out_shape=[jax.ShapeDtypeStruct(shape, BF)] * n_out,
        grid=(low,),
        in_specs=[whole((tokens, rows)) for _ in lefts] + specs,
        out_specs=[pl.BlockSpec(out_block, index)] * n_out,
        scratch_shapes=[pltpu.VMEM((rows, tokens), BF) for _ in lefts] + [pltpu.VMEM((rows, tile), F32)],
        cost_estimate=cost(2 * tokens * rows * width, 2 * tokens * (rows + width) + 2 * rows * width),
    )(*lefts, *rights)
    return outs


def input_grad_kernel(count, width, *refs):
    x_ref, dm_ref, grads_ref, gains_ref = refs[:4]
    pieces = refs[4 : 4 + count]
    out_ref = refs[4 + count]
    weights, sems = refs[5 + count :]

    @pl.when(pl.program_id(0) == 0)
    def _():
        copies = load_copies(pieces, weights, sems)
        for copy in copies:
            copy.start()
        for copy in copies:
            copy.wait()

    x = x_ref[...].astype(F32)
    inverse = lax.rsqrt(jnp.mean(x * x, axis=1, keepdims=True) + EPSILON)
    scaled = dot_nt(grads_ref[...], weights[:, : 3 * width]) * gains_ref[0:1, :]
    out_ref[...] = (
        dm_ref[...]
        + inverse * scaled
        - x * (inverse * inverse * inverse) * jnp.mean(scaled * x, axis=1, keepdims=True)
    )


def input_grad(x, dm, grads, gains, pieces):
    tokens, width = x.shape
    block = pl.BlockSpec((TBLOCK, width), lambda i: (i, 0))
    return pl.pallas_call(
        functools.partial(input_grad_kernel, len(pieces), width),
        name="input_grad",
        out_shape=jax.ShapeDtypeStruct((tokens, width), F32),
        grid=(tokens // TBLOCK,),
        in_specs=[block, block, pl.BlockSpec((TBLOCK, 3 * width), lambda i: (i, 0)), whole((8, width))]
        + [ANY] * len(pieces),
        out_specs=block,
        scratch_shapes=[
            pltpu.VMEM((width, pieces[0].shape[1]), BF),
            pltpu.SemaphoreType.DMA((len(pieces),)),
        ],
        cost_estimate=cost(6 * tokens * width * width, 6 * width * width + 16 * tokens * width),
    )(x, dm, grads, gains, *pieces)


def flip(values, bits):
    count = lax.axis_size("fsdp")
    return lax.ppermute(values, "fsdp", [(i, i ^ bits) for i in range(count)])


def across(values):
    return lax.ppermute(values, "seq", [(0, 1), (1, 0)])


def aligned(rows, count):
    return rows % 16 == 0 and count >= 4 and count & (count - 1) == 0


def gather_rows(shard, parts):
    if parts == 1:
        return [lax.all_gather(shard, "fsdp", axis=0, tiled=True)]
    pieces = [None] * parts
    pieces[0] = shard
    for upper in range(4, parts, 4):
        pieces[upper] = flip(shard, upper)
    for upper in range(0, parts, 4):
        pieces[upper + 2] = flip(pieces[upper], 2)
    for even in range(0, parts, 2):
        pieces[even + 1] = flip(pieces[even], 1)
    return pieces


def scatter_rows(outs, parts):
    if parts == 1:
        total = lax.psum_scatter(outs[0], "fsdp", scatter_dimension=0, tiled=True)
    else:
        keep, send = outs
        upper = parts // 4
        got = flip(send, 1)
        ahead = (keep[upper:].astype(F32) + got[upper:].astype(F32)).astype(BF)
        ahead = flip(ahead, 2)
        parts_sum = [
            keep[j].astype(F32) + got[j].astype(F32) + ahead[j].astype(F32) for j in range(upper)
        ]
        arrived = [flip(parts_sum[j].astype(BF), 4 * j) for j in range(1, upper)]
        total = parts_sum[0]
        for piece in arrived:
            total = total + piece.astype(F32)
        total = total.astype(BF)
    return total.astype(F32) + across(total).astype(F32)


def rope_tables(length):
    half = HEAD_DIM // 2
    inverse = jnp.exp(jnp.arange(half, dtype=F32) * (-2.0 * math.log(10000.0) / HEAD_DIM))
    angles = jnp.arange(length, dtype=jnp.int32).astype(F32)[:, None] * inverse[None, :]
    cosine, sine = jnp.cos(angles), jnp.sin(angles)
    return (
        jnp.concatenate([cosine] * 4, axis=1),
        jnp.concatenate([-sine, sine, -sine, sine], axis=1),
    )


def per_device(
    tokens, doc_ids, cotangent, w_query, w_key, w_value, w_out, w_gate, w_up, w_down, gain_attn, gain_ffn
):
    seq_rank = lax.axis_index("seq")
    count = lax.axis_size("fsdp")
    micro, _, span, width = tokens.shape
    hidden_width = w_gate.shape[1]
    rows = w_query.shape[0]
    parts = count if aligned(rows, count) and aligned(w_down.shape[0], count) else 1

    def mine(array):
        own = lax.dynamic_index_in_dim(array, seq_rank, 0, keepdims=False)[0]
        other = across(lax.dynamic_index_in_dim(array, 1 - seq_rank, 0, keepdims=False)[0])
        return jnp.where(seq_rank == 0, jnp.concatenate([own, other]), jnp.concatenate([other, own]))

    def halves(array):
        own = lax.dynamic_slice_in_dim(array, seq_rank * span, span, 0)
        other = lax.dynamic_slice_in_dim(array, (1 - seq_rank) * span, span, 0)
        return own, other

    def give_back(own, other):
        first, second = jnp.where(seq_rank == 0, own, other), jnp.where(seq_rank == 0, other, own)
        return jnp.stack([first, second])[:, None]

    column = jnp.pad(jnp.stack([gain_attn, gain_ffn], axis=1), ((0, 0), (0, 126)))
    group_in = jnp.concatenate([w_query, w_key, w_value, column], axis=1)
    group_mid = jnp.concatenate([w_out, w_gate, w_up], axis=1)

    x = mine(tokens)
    docs = mine(doc_ids)
    pieces_in = gather_rows(group_in, parts)
    pieces_mid = gather_rows(group_mid, parts)
    pieces_down = gather_rows(w_down, parts)
    dy = mine(cotangent)

    length = x.shape[0]
    cosine, sine = rope_tables(length)
    starts = jnp.sum((docs[None, :] < docs[:, None]).astype(jnp.int32), axis=1)
    first = starts[::QBLOCK] // QBLOCK
    starts = starts[None, :]

    normed, queries, keys, values, gains = project(x, cosine, sine, pieces_in)
    attended, lse = attend(queries, keys, values, starts, first)
    y, normed_two, hidden, dgate, dup, dm, dmr, datt = feed(
        x, attended, dy, gains, pieces_mid, pieces_down, hidden_width
    )
    own_y, other_y = halves(y)
    output = give_back(own_y, across(other_y))
    sum_down = scatter_rows(outer_sums(parts, [hidden], [dy], "grad_down"), parts)
    sum_mid = scatter_rows(
        outer_sums(parts, [attended, normed_two, normed_two], [dmr, dgate, dup], "grad_mid"), parts
    )
    grads = attend_back(queries, keys, values, datt, lse, starts, first, cosine, sine)
    sum_in = scatter_rows(outer_sums(parts, [normed], [grads], "grad_in"), parts)
    grad_x = input_grad(x, dm, grads, gains, pieces_in)
    own_g, other_g = halves(grad_x)
    grad_tokens = give_back(own_g, across(other_g.astype(BF)).astype(F32))

    sum_out, sum_gate, sum_up = (
        sum_mid[:, :width],
        sum_mid[:, width : width + hidden_width],
        sum_mid[:, width + hidden_width :],
    )
    w_in = group_in[:, : 3 * width].astype(F32)
    grad_gain_attn = jnp.sum(w_in * sum_in, axis=1) / gain_attn.astype(F32)
    grad_gain_ffn = jnp.sum(
        group_mid[:, width:].astype(F32) * sum_mid[:, width:], axis=1
    ) / gain_ffn.astype(F32)
    return (
        output,
        grad_tokens,
        sum_in[:, :width],
        sum_in[:, width : 2 * width],
        sum_in[:, 2 * width :],
        sum_out,
        sum_gate,
        sum_up,
        sum_down,
        grad_gain_attn,
        grad_gain_ffn,
    )


def solution(mesh):
    rows = P("fsdp", None)
    acts = P(None, "fsdp", "seq", None)
    return jax.shard_map(
        per_device,
        mesh=mesh,
        in_specs=(acts, P(None, "fsdp", "seq"), acts) + (rows,) * 7 + (P("fsdp"),) * 2,
        out_specs=(acts, acts) + (rows,) * 7 + (P("fsdp"),) * 2,
        check_vma=False,
    )
```

time: 1530 us -> 473 us (0.31)
  waiting for transfers between devices: 870 us -> 209 us
  matrix products: 216 us -> 0 us
  Pallas kernels: 0 us -> 150 us
  local copies, waits for them, and re-layouts: 146 us -> 16.5 us
  blocking collectives: 105 us -> 0 us
  other arithmetic: 93.9 us -> 33.3 us
    reduce_scatter x7 -> x0, waiting for transfers between devices: 513 us -> none  [the longest x1 86.4 us: per_device(): lax.psum_scatter(sum_gate, 'fsdp', scatter_dimension=0, tiled=True)]
    all_gather x14 -> x0, waiting for transfers between devices: 279 us -> none  [the longest x2 80.2 us: micro_step(): lax.all_gather(w_up, 'fsdp', axis=0, tiled=True)]
    dot_general x70 -> x0, matrix products: 216 us -> none  [the longest x14 55.6 us: outer_sum(): lax.dot_general(left, right, (((0,), (0,)), ((), ())), preferred_element_...]
    ppermute x0 -> x68, waiting for transfers between devices: none -> 209 us  [the longest x60 169 us: flip(): return lax.ppermute(values, 'fsdp', [(i, i ^ bits) for i in range(count)])]
    pallas_call x0 -> x8, Pallas kernels: none -> 150 us  [the longest x3 41.3 us: outer_sums(): pl.pallas_call(functools.partial(outer_kernel, parts, tuple(edges)), name...]
    while x300 -> x0, local copies, waits for them, and re-layouts: 77.1 us -> none
    all_to_all x16 -> x0, waiting for transfers between devices: 65.8 us -> none  [the longest x2 20.9 us: forward(): lax.all_to_all(queries, 'seq', split_axis=1, concat_axis=0, tiled=True)]
    all_to_all x16 -> x0, starting transfers between devices: 65.6 us -> none  [the longest x2 9.41 us: backward(): lax.all_to_all(grad_joined, 'seq', split_axis=1, concat_axis=0, tiled=True)]
  transfers between devices with their start and end apart: 38 -> 68, of which waited for: 27 -> 27; matrix products, arithmetic and copies ran while one was open for 16% -> 10% of each run, Pallas kernels for 0% -> 20%
where the time goes in v1:
time: 473 us; the launch traced here: 465 us
  waiting for transfers between devices  209 us (44%)
  Pallas kernels  150 us (32%)
  starting transfers between devices  54.3 us (11%)
  other arithmetic  33.3 us (7%)
  local copies, waits for them, and re-layouts  16.5 us (3%)
    ppermute x60, waiting for transfers between devices, flip(): return lax.ppermute(values, 'fsdp', [(i, i ^ bits) for i in range(count)])  169 us
    ppermute x60, starting transfers between devices, flip(): return lax.ppermute(values, 'fsdp', [(i, i ^ bits) for i in range(count)])  46.6 us
    pallas_call x3, Pallas kernels, outer_sums(): pl.pallas_call(functools.partial(outer_kernel, parts, tuple(edges)), name...  41.3 us
    ppermute x8, waiting for transfers between devices, across(): return lax.ppermute(values, 'seq', [(0, 1), (1, 0)])  40 us
    pallas_call x1, Pallas kernels, feed(): pl.pallas_call(functools.partial(feed_kernel, (len(first), len(second)),...  36.4 us
    pallas_call x1, Pallas kernels, attend_back(): pl.pallas_call(functools.partial(attend_back_kernel, pairs), name='attend...  28 us
    pallas_call x1, Pallas kernels, attend(): pl.pallas_call(functools.partial(attend_kernel, pairs), name='attend', ou...  23.8 us
    pallas_call x1, Pallas kernels, input_grad(): pl.pallas_call(functools.partial(input_grad_kernel, len(pieces), width),...  11 us
  transfers between devices with their start and end apart: 68, of which 27 were waited for; matrix products, arithmetic and copies ran while one was open for 10% of the time, Pallas kernels for 20%

profile of v1, /device:TPU:0, one launch (start us, length us, event | category | flops | bytes accessed | tf_op | source)
XLA Modules:
  0.0 465.4 jit_solution(7133924489369529146)
XLA Ops:
  0.6 4.1 collective-permute-start.40
  14.2 4.2 collective-permute-start.13
  22.1 4.9 %collective-permute-done.13.refs_15_.refs_16_ = bf16[48,2432]{1,0:T(8,128)(2,1)S(1)} collective-permute-done((bf16[48,2432]{1,0:T(8,128)(2,1)S(1)}, bf16[48,2432]{1,0:T(8,128)(2,1)S(1)}, u32[]{:S(2)}, u32[]{:S(2)}) %collective-permute-start.13) | collective-permute-done | bytes 233504 | tf_op jit(solution)/shard_map/ppermute | solution.py:487
  27.1 16.2 %collective-permute-done.9.refs_11_.refs_12_ = bf16[48,2432]{1,0:T(8,128)(2,1)S(1)} collective-permute-done((bf16[48,2432]{1,0:T(8,128)(2,1)S(1)}, bf16[48,2432]{1,0:T(8,128)(2,1)S(1)}, u32[]{:S(2)}, u32[]{:S(2)}) %collective-permute-start.9) | collective-permute-done | bytes 233504 | tf_op jit(solution)/shard_map/ppermute | solution.py:487
  46.9 4.3 collective-permute-done.38.refs_26_
  62.5 2.9 collective-permute-done.11.refs_13_.refs_14_
  73.8 7.3 %collective-permute-done.29.refs_16_ = bf16[48,4864]{1,0:T(8,128)(2,1)} collective-permute-done((bf16[48,4864]{1,0:T(8,128)(2,1)}, bf16[48,4864]{1,0:T(8,128)(2,1)}, u32[]{:S(2)}, u32[]{:S(2)}) %collective-permute-start.29) | collective-permute-done | bytes 466976 | tf_op jit(solution)/shard_map/ppermute | solution.py:487
  82.3 24.5 %collective-permute-done.25.refs_12_ = bf16[48,4864]{1,0:T(8,128)(2,1)} collective-permute-done((bf16[48,4864]{1,0:T(8,128)(2,1)}, bf16[48,4864]{1,0:T(8,128)(2,1)}, u32[]{:S(2)}, u32[]{:S(2)}) %collective-permute-start.25) | collective-permute-done | bytes 466976 | tf_op jit(solution)/shard_map/ppermute | solution.py:487
  117.0 7.5 %collective-permute-done.17 = bf16[512,768]{1,0:T(8,128)(2,1)} collective-permute-done((bf16[512,768]{1,0:T(8,128)(2,1)S(1)}, bf16[512,768]{1,0:T(8,128)(2,1)}, u32[]{:S(2)}, u32[]{:S(2)}) %collective-permute-start.17) | collective-permute-done | bytes 786464 | tf_op jit(solution)/shard_map/ppermute | solution.py:491
  127.3 3.2 maximum_select_fusion.refs_0_
  131.0 7.6 %collective-permute-done.27.refs_14_ = bf16[48,4864]{1,0:T(8,128)(2,1)} collective-permute-done((bf16[48,4864]{1,0:T(8,128)(2,1)}, bf16[48,4864]{1,0:T(8,128)(2,1)}, u32[]{:S(2)}, u32[]{:S(2)}) %collective-permute-start.27) | collective-permute-done | bytes 466976 | tf_op jit(solution)/shard_map/ppermute | solution.py:487
  139.1 8.5 %collective-permute-done.23.refs_10_ = bf16[48,4864]{1,0:T(8,128)(2,1)S(1)} collective-permute-done((bf16[48,4864]{1,0:T(8,128)(2,1)}, bf16[48,4864]{1,0:T(8,128)(2,1)S(1)}, u32[]{:S(2)}, u32[]{:S(2)}) %collective-permute-start.23) | collective-permute-done | bytes 466976 | tf_op jit(solution)/shard_map/ppermute | solution.py:487
  147.6 9.9 %project.1 = (bf16[1024,768]{1,0:T(8,128)(2,1)}, bf16[1024,768]{1,0:T(8,128)(2,1)}, bf16[1024,768]{1,0:T(8,128)(2,1)}, bf16[1024,768]{1,0:T(8,128)(2,1)}, f32[8,768]{1,0:T(8,128)}) custom-call(bf16[1024,768]{1,0:T(8,128)(2,1)} %maximum_select_fusion.refs_0_, f32[1024,128]{1,0:T(8,128)} %get-tuple-element.126.refs_1_.cos_ref, ...), custom_call_target="tpu_custom_call" | custom-call | flops 3623878656 | bytes 11403264 | tf_op jit(solution)/shard_map/project/pallas_call | solution.py:109
  157.6 3.1 maximum_select_fusion.1.refs_2_.refs_1_
  160.7 23.8 %attend.1 = (bf16[1024,768]{1,0:T(8,128)(2,1)}, f32[8,6,256]{2,1,0:T(8,128)}) custom-call(s32[8]{0:T(128)} %and_select_fusion.first_ref, bf16[1024,768]{1,0:T(8,128)(2,1)} %get-tuple-element.32.q_ref, bf16[1024,768]{1,0:T(8,128)(2,1)} %get-tuple-element.33.k_ref, bf16[1024,768]{1,0:T(8,128)(2,1)} %get-tuple-element.34.v_ref, s32[1,1024]{1,0:T(1,128)} %bitcast.72), custom_call_target="tpu_custom_call" | custom-call | flops 3221225472 | bytes 7864320 | tf_op jit(solution)/shard_map/attend/pallas_call | solution.py:187
  185.6 36.4 %feed.1 = (bf16[1024,768]{1,0:T(8,128)(2,1)}, bf16[1024,768]{1,0:T(8,128)(2,1)}, bf16[1024,2048]{1,0:T(8,128)(2,1)}, bf16[1024,2048]{1,0:T(8,128)(2,1)}, bf16[10...) custom-call(bf16[1024,768]{1,0:T(8,128)(2,1)} %maximum_select_fusion.refs_0_, ...), custom_call_target="tpu_custom_call" | custom-call | flops 21743271936 | bytes 28311552 | tf_op jit(solution)/shard_map/feed/pallas_call | solution.py:361
  222.0 21.7 %grad_mid.1 = (bf16[8,48,4864]{2,1,0:T(8,128)(2,1)}, bf16[8,48,4864]{2,1,0:T(8,128)(2,1)}) custom-call(bf16[1024,768]{1,0:T(8,128)(2,1)} %get-tuple-element.35.refs_1_.refs_0_, bf16[1024,768]{1,0:T(8,128)(2,1)} %get-tuple-element.44.refs_1_.refs_2_, bf16[1024,768]{1,0:T(8,128)(2,1)} %get-tuple-element.44.refs_1_.refs_2_, ...), custom_call_target="tpu_custom_call" | custom-call | flops 7650410496 | bytes 19005440 | tf_op jit(solution)/shard_map/grad_mid/pallas_call | solution.py:429
  244.1 8.8 %grad_down.1 = (bf16[8,128,768]{2,1,0:T(8,128)(2,1)}, bf16[8,128,768]{2,1,0:T(8,128)(2,1)}) custom-call(bf16[1024,2048]{1,0:T(8,128)(2,1)} %get-tuple-element.50.refs_0_, bf16[1024,768]{1,0:T(8,128)(2,1)} %maximum_select_fusion.1.refs_2_.refs_1_), custom_call_target="tpu_custom_call" | custom-call | flops 3221225472 | bytes 8912896 | tf_op jit(solution)/shard_map/grad_down/pallas_call | solution.py:429
  252.9 28.0 %attend_back.1.refs_2_.refs_1_ = bf16[1024,2304]{1,0:T(8,128)(2,1)} custom-call(s32[8]{0:T(128)} %and_select_fusion.first_ref, bf16[1024,768]{1,0:T(8,128)(2,1)} %get-tuple-element.32.q_ref, bf16[1024,768]{1,0:T(8,128)(2,1)} %get-tuple-element.33.k_ref, bf16[1024,768]{1,0:T(8,128)(2,1)} %get-tuple-element.34.v_ref, ...), custom_call_target="tpu_custom_call" | custom-call | flops 8053063680 | bytes 12582912 | tf_op jit(solution)/shard_map/attend_back/pallas_call | solution.py:274
  280.9 10.8 %grad_in.1 = (bf16[8,48,2304]{2,1,0:T(8,128)(2,1)}, bf16[8,48,2304]{2,1,0:T(8,128)(2,1)}) custom-call(bf16[1024,768]{1,0:T(8,128)(2,1)} %get-tuple-element.41.refs_0_, bf16[1024,2304]{1,0:T(8,128)(2,1)} %attend_back.1.refs_2_.refs_1_), custom_call_target="tpu_custom_call" | custom-call | flops 3623878656 | bytes 9830400 | tf_op jit(solution)/shard_map/grad_in/pallas_call | solution.py:429
  292.3 11.0 %input_grad.1 = f32[1024,768]{1,0:T(8,128)} custom-call(bf16[1024,768]{1,0:T(8,128)(2,1)} %maximum_select_fusion.refs_0_, f32[1024,768]{1,0:T(8,128)} %get-tuple-element.38.refs_1_, bf16[1024,2304]{1,0:T(8,128)(2,1)} %attend_back.1.refs_2_.refs_1_, f32[8,768]{1,0:T(8,128)} %get-tuple-element.36.refs_3_, bf16[48,2432]{1,0:T(8,128)(2,1)} %copy-done.6, ...), custom_call_target="tpu_custom_call" | custom-call | flops 3623878656 | bytes 16121856 | tf_op jit(solution)/shard_map/input_grad/pallas_call | solution.py:469
  309.1 17.4 %collective-permute-done.49 = bf16[512,768]{1,0:T(8,128)(2,1)} collective-permute-done((bf16[512,768]{1,0:T(8,128)(2,1)}, bf16[512,768]{1,0:T(8,128)(2,1)}, u32[]{:S(2)}, u32[]{:S(2)}) %collective-permute-start.49) | collective-permute-done | bytes 786464 | tf_op jit(solution)/shard_map/ppermute | solution.py:491
  336.7 5.6 %collective-permute-done.48 = bf16[512,768]{1,0:T(8,128)(2,1)S(1)} collective-permute-done((bf16[512,768]{1,0:T(8,128)(2,1)S(1)}, bf16[512,768]{1,0:T(8,128)(2,1)S(1)}, u32[]{:S(2)}, u32[]{:S(2)}) %collective-permute-start.48) | collective-permute-done | bytes 786464 | tf_op jit(solution)/shard_map/ppermute | solution.py:491
  342.7 7.4 %collective-permute-done.63 = bf16[4,128,768]{2,1,0:T(8,128)(2,1)S(1)} collective-permute-done((bf16[4,128,768]{2,1,0:T(8,128)(2,1)S(1)}, bf16[4,128,768]{2,1,0:T(8,128)(2,1)S(1)}, u32[]{:S(2)}, u32[]{:S(2)}) %collective-permute-start.63) | collective-permute-done | bytes 786464 | tf_op jit(solution)/shard_map/ppermute | solution.py:487
  358.3 3.2 collective-permute-done.66
  361.6 6.6 %collective-permute-done.65 = bf16[128,768]{1,0:T(8,128)(2,1)S(1)} collective-permute-done((bf16[128,768]{1,0:T(8,128)(2,1)S(1)}, bf16[128,768]{1,0:T(8,128)(2,1)S(1)}, u32[]{:S(2)}, u32[]{:S(2)}) %collective-permute-start.65) | collective-permute-done | bytes 196640 | tf_op jit(solution)/shard_map/ppermute | solution.py:487
  375.8 30.5 %collective-permute-done.57 = bf16[4,48,4864]{2,1,0:T(8,128)(2,1)S(1)} collective-permute-done((bf16[4,48,4864]{2,1,0:T(8,128)(2,1)S(1)}, bf16[4,48,4864]{2,1,0:T(8,128)(2,1)S(1)}, u32[]{:S(2)}, u32[]{:S(2)}) %collective-permute-start.57) | collective-permute-done | bytes 1867808 | tf_op jit(solution)/shard_map/ppermute | solution.py:487
  408.5 2.9 collective-permute-start.60
  414.3 5.3 %collective-permute-done.58 = bf16[48,4864]{1,0:T(8,128)(2,1)S(1)} collective-permute-done((bf16[48,4864]{1,0:T(8,128)(2,1)S(1)}, bf16[48,4864]{1,0:T(8,128)(2,1)S(1)}, u32[]{:S(2)}, u32[]{:S(2)}) %collective-permute-start.58) | collective-permute-done | bytes 466976 | tf_op jit(solution)/shard_map/ppermute | solution.py:487
  419.6 13.4 %collective-permute-done.60 = bf16[48,4864]{1,0:T(8,128)(2,1)S(1)} collective-permute-done((bf16[48,4864]{1,0:T(8,128)(2,1)S(1)}, bf16[48,4864]{1,0:T(8,128)(2,1)S(1)}, u32[]{:S(2)}, u32[]{:S(2)}) %collective-permute-start.60) | collective-permute-done | bytes 466976 | tf_op jit(solution)/shard_map/ppermute | solution.py:487
  433.0 17.9 %collective-permute-done.59 = bf16[48,4864]{1,0:T(8,128)(2,1)S(1)} collective-permute-done((bf16[48,4864]{1,0:T(8,128)(2,1)S(1)}, bf16[48,4864]{1,0:T(8,128)(2,1)S(1)}, u32[]{:S(2)}, u32[]{:S(2)}) %collective-permute-start.59) | collective-permute-done | bytes 466976 | tf_op jit(solution)/shard_map/ppermute | solution.py:487
  454.0 8.5 %collective-permute-done.61 = bf16[48,4864]{1,0:T(8,128)(2,1)S(1)} collective-permute-done((bf16[48,4864]{1,0:T(8,128)(2,1)S(1)}, bf16[48,4864]{1,0:T(8,128)(2,1)S(1)}, u32[]{:S(2)}, u32[]{:S(2)}) %collective-permute-start.61) | collective-permute-done | bytes 466976 | tf_op jit(solution)/shard_map/ppermute | solution.py:491
  (255 shorter events, 96.2 us)
Async XLA Ops:
  18.4 24.9 %collective-permute-start.9 = (bf16[48,2432]{1,0:T(8,128)(2,1)S(1)}, bf16[48,2432]{1,0:T(8,128)(2,1)S(1)}, u32[]{:S(2)}, u32[]{:S(2)}) collective-permute-start(bf16[48,2432]{1,0:T(8,128)(2,1)S(1)} %fusion.16.refs_3_.refs_4_), channel_id=1, source_target_pairs={{0,8},{1,9},{2,10},{3,11},{4,12},{5,13},{6,14},{7,15},{8,0},{9,1},... | collective-permute-start | bytes 700424 | tf_op jit(solution)/shard_map/ppermute | solution.py:487
  18.4 24.9 %collective-permute-start.5 = (bf16[48,2432]{1,0:T(8,128)(2,1)S(1)}, bf16[48,2432]{1,0:T(8,128)(2,1)S(1)}, u32[]{:S(2)}, u32[]{:S(2)}) collective-permute-start(bf16[48,2432]{1,0:T(8,128)(2,1)S(1)} %fusion.16.refs_3_.refs_4_), channel_id=1, source_target_pairs={{0,4},{1,5},{2,6},{3,7},{4,0},{5,1},{6,2},{7,3},{8,12},{9,13},{10,... | collective-permute-start | bytes 700424 | tf_op jit(solution)/shard_map/ppermute | solution.py:487
  19.0 25.2 %collective-permute-start.3 = (bf16[48,2432]{1,0:T(8,128)(2,1)S(1)}, bf16[48,2432]{1,0:T(8,128)(2,1)S(1)}, u32[]{:S(2)}, u32[]{:S(2)}) collective-permute-start(bf16[48,2432]{1,0:T(8,128)(2,1)S(1)} %fusion.16.refs_3_.refs_4_), channel_id=1, source_target_pairs={{0,2},{1,3},{2,0},{3,1},{4,6},{5,7},{6,4},{7,5},{8,10},{9,11},{10,... | collective-permute-start | bytes 700424 | tf_op jit(solution)/shard_map/ppermute | solution.py:487
  22.1 22.3 %collective-permute-start.2 = (bf16[48,2432]{1,0:T(8,128)(2,1)S(1)}, bf16[48,2432]{1,0:T(8,128)(2,1)S(1)}, u32[]{:S(2)}, u32[]{:S(2)}) collective-permute-start(bf16[48,2432]{1,0:T(8,128)(2,1)S(1)} %fusion.16.refs_3_.refs_4_), channel_id=1, source_target_pairs={{0,1},{1,0},{2,3},{3,2},{4,5},{5,4},{6,7},{7,6},{8,9},{9,8},{10,11... | collective-permute-start | bytes 700424 | tf_op jit(solution)/shard_map/ppermute | solution.py:487
  68.2 38.6 %collective-permute-start.25 = (bf16[48,4864]{1,0:T(8,128)(2,1)}, bf16[48,4864]{1,0:T(8,128)(2,1)}, u32[]{:S(2)}, u32[]{:S(2)}) collective-permute-start(bf16[48,4864]{1,0:T(8,128)(2,1)} %constant_dynamic-update-slice_fusion.refs_4_), channel_id=1, source_target_pairs={{0,8},{1,9},{2,10},{3,11},{4,12},{5,13},{6,14},{7,15},{8,0},{9,1},... | collective-permute-start | bytes 1400840 | tf_op jit(solution)/shard_map/ppermute | solution.py:487
  69.8 38.4 %collective-permute-start.21 = (bf16[48,4864]{1,0:T(8,128)(2,1)}, bf16[48,4864]{1,0:T(8,128)(2,1)}, u32[]{:S(2)}, u32[]{:S(2)}) collective-permute-start(bf16[48,4864]{1,0:T(8,128)(2,1)} %constant_dynamic-update-slice_fusion.refs_4_), channel_id=1, source_target_pairs={{0,4},{1,5},{2,6},{3,7},{4,0},{5,1},{6,2},{7,3},{8,12},{9,13},{10,... | collective-permute-start | bytes 1400840 | tf_op jit(solution)/shard_map/ppermute | solution.py:487
  69.8 38.5 %collective-permute-start.19 = (bf16[48,4864]{1,0:T(8,128)(2,1)}, bf16[48,4864]{1,0:T(8,128)(2,1)}, u32[]{:S(2)}, u32[]{:S(2)}) collective-permute-start(bf16[48,4864]{1,0:T(8,128)(2,1)} %constant_dynamic-update-slice_fusion.refs_4_), channel_id=1, source_target_pairs={{0,2},{1,3},{2,0},{3,1},{4,6},{5,7},{6,4},{7,5},{8,10},{9,11},{10,... | collective-permute-start | bytes 1400840 | tf_op jit(solution)/shard_map/ppermute | solution.py:487
  72.1 36.7 %collective-permute-start.18 = (bf16[48,4864]{1,0:T(8,128)(2,1)}, bf16[48,4864]{1,0:T(8,128)(2,1)}, u32[]{:S(2)}, u32[]{:S(2)}) collective-permute-start(bf16[48,4864]{1,0:T(8,128)(2,1)} %constant_dynamic-update-slice_fusion.refs_4_), channel_id=1, source_target_pairs={{0,1},{1,0},{2,3},{3,2},{4,5},{5,4},{6,7},{7,6},{8,9},{9,8},{10,11... | collective-permute-start | bytes 1400840 | tf_op jit(solution)/shard_map/ppermute | solution.py:487
  81.1 35.7 %collective-permute-start = (bf16[512,768]{1,0:T(8,128)(2,1)S(1)}, bf16[512,768]{1,0:T(8,128)(2,1)}, u32[]{:S(2)}, u32[]{:S(2)}) collective-permute-start(bf16[512,768]{1,0:T(8,128)(2,1)S(1)} %get-tuple-element.113), channel_id=1, source_target_pairs={{0,16},{16,0},{1,17},{17,1},{2,18},{18,2},{3,19},{19,3},{4,20},{20... | collective-permute-start | bytes 2359304 | tf_op jit(solution)/shard_map/ppermute | solution.py:491
  106.8 17.8 %collective-permute-start.17 = (bf16[512,768]{1,0:T(8,128)(2,1)S(1)}, bf16[512,768]{1,0:T(8,128)(2,1)}, u32[]{:S(2)}, u32[]{:S(2)}) collective-permute-start(bf16[512,768]{1,0:T(8,128)(2,1)S(1)} %get-tuple-element.111), channel_id=1, source_target_pairs={{0,16},{16,0},{1,17},{17,1},{2,18},{18,2},{3,19},{19,3},{4,20},{20... | collective-permute-start | bytes 2359304 | tf_op jit(solution)/shard_map/ppermute | solution.py:491
  116.3 22.3 %collective-permute-start.27 = (bf16[48,4864]{1,0:T(8,128)(2,1)}, bf16[48,4864]{1,0:T(8,128)(2,1)}, u32[]{:S(2)}, u32[]{:S(2)}) collective-permute-start(bf16[48,4864]{1,0:T(8,128)(2,1)} %collective-permute-done.25.refs_12_), channel_id=1, source_target_pairs={{0,2},{1,3},{2,0},{3,1},{4,6},{5,7},{6,4},{7,5},{8,10},{9,11},{10,... | collective-permute-start | bytes 1400840 | tf_op jit(solution)/shard_map/ppermute | solution.py:487
  116.9 21.8 %collective-permute-start.26 = (bf16[48,4864]{1,0:T(8,128)(2,1)}, bf16[48,4864]{1,0:T(8,128)(2,1)S(1)}, u32[]{:S(2)}, u32[]{:S(2)}) collective-permute-start(bf16[48,4864]{1,0:T(8,128)(2,1)} %collective-permute-done.25.refs_12_), channel_id=1, source_target_pairs={{0,1},{1,0},{2,3},{3,2},{4,5},{5,4},{6,7},{7,6},{8,9},{9,8},{10,11... | collective-permute-start | bytes 1400840 | tf_op jit(solution)/shard_map/ppermute | solution.py:487
  124.5 23.1 %collective-permute-start.23 = (bf16[48,4864]{1,0:T(8,128)(2,1)}, bf16[48,4864]{1,0:T(8,128)(2,1)S(1)}, u32[]{:S(2)}, u32[]{:S(2)}) collective-permute-start(bf16[48,4864]{1,0:T(8,128)(2,1)} %collective-permute-done.21.refs_8_), channel_id=1, source_target_pairs={{0,2},{1,3},{2,0},{3,1},{4,6},{5,7},{6,4},{7,5},{8,10},{9,11},{10,... | collective-permute-start | bytes 1400840 | tf_op jit(solution)/shard_map/ppermute | solution.py:487
  130.5 54.0 %collective-permute-start.22 = (bf16[48,4864]{1,0:T(8,128)(2,1)}, bf16[48,4864]{1,0:T(8,128)(2,1)S(1)}, u32[]{:S(2)}, u32[]{:S(2)}) collective-permute-start(bf16[48,4864]{1,0:T(8,128)(2,1)} %collective-permute-done.21.refs_8_), channel_id=1, source_target_pairs={{0,1},{1,0},{2,3},{3,2},{4,5},{5,4},{6,7},{7,6},{8,9},{9,8},{10,11... | collective-permute-start | bytes 1400840 | tf_op jit(solution)/shard_map/ppermute | solution.py:487
  130.5 54.0 %collective-permute-start.20 = (bf16[48,4864]{1,0:T(8,128)(2,1)}, bf16[48,4864]{1,0:T(8,128)(2,1)S(1)}, u32[]{:S(2)}, u32[]{:S(2)}) collective-permute-start(bf16[48,4864]{1,0:T(8,128)(2,1)} %collective-permute-done.19.refs_6_), channel_id=1, source_target_pairs={{0,1},{1,0},{2,3},{3,2},{4,5},{5,4},{6,7},{7,6},{8,9},{9,8},{10,11... | collective-permute-start | bytes 1400840 | tf_op jit(solution)/shard_map/ppermute | solution.py:487
  138.6 45.9 %collective-permute-start.32 = (bf16[48,4864]{1,0:T(8,128)(2,1)}, bf16[48,4864]{1,0:T(8,128)(2,1)S(1)}, u32[]{:S(2)}, u32[]{:S(2)}) collective-permute-start(bf16[48,4864]{1,0:T(8,128)(2,1)} %collective-permute-done.31.refs_18_), channel_id=1, source_target_pairs={{0,1},{1,0},{2,3},{3,2},{4,5},{5,4},{6,7},{7,6},{8,9},{9,8},{10,11... | collective-permute-start | bytes 1400840 | tf_op jit(solution)/shard_map/ppermute | solution.py:487
  138.6 45.9 %collective-permute-start.28 = (bf16[48,4864]{1,0:T(8,128)(2,1)}, bf16[48,4864]{1,0:T(8,128)(2,1)}, u32[]{:S(2)}, u32[]{:S(2)}) collective-permute-start(bf16[48,4864]{1,0:T(8,128)(2,1)} %collective-permute-done.27.refs_14_), channel_id=1, source_target_pairs={{0,1},{1,0},{2,3},{3,2},{4,5},{5,4},{6,7},{7,6},{8,9},{9,8},{10,11... | collective-permute-start | bytes 1400840 | tf_op jit(solution)/shard_map/ppermute | solution.py:487
  147.6 36.9 %collective-permute-start.24 = (bf16[48,4864]{1,0:T(8,128)(2,1)S(1)}, bf16[48,4864]{1,0:T(8,128)(2,1)}, u32[]{:S(2)}, u32[]{:S(2)}) collective-permute-start(bf16[48,4864]{1,0:T(8,128)(2,1)S(1)} %collective-permute-done.23.refs_10_), channel_id=1, source_target_pairs={{0,1},{1,0},{2,3},{3,2},{4,5},{5,4},{6,7},{7,6},{8,9},{9,8},{10,11... | collective-permute-start | bytes 1400840 | tf_op jit(solution)/shard_map/ppermute | solution.py:487
  243.6 89.5 %collective-permute-start.56 = (bf16[8,48,4864]{2,1,0:T(8,128)(2,1)}, bf16[8,48,4864]{2,1,0:T(8,128)(2,1)}, u32[]{:S(2)}, u32[]{:S(2)}) collective-permute-start(bf16[8,48,4864]{2,1,0:T(8,128)(2,1)} %get-tuple-element.49), channel_id=1, source_target_pairs={{0,1},{1,0},{2,3},{3,2},{4,5},{5,4},{6,7},{7,6},{8,9},{9,8},{10,11... | collective-permute-start | bytes 11206664 | tf_op jit(solution)/shard_map/ppermute | solution.py:487
  252.9 75.2 %collective-permute-start.62 = (bf16[8,128,768]{2,1,0:T(8,128)(2,1)}, bf16[8,128,768]{2,1,0:T(8,128)(2,1)}, u32[]{:S(2)}, u32[]{:S(2)}) collective-permute-start(bf16[8,128,768]{2,1,0:T(8,128)(2,1)} %get-tuple-element.52), channel_id=1, source_target_pairs={{0,1},{1,0},{2,3},{3,2},{4,5},{5,4},{6,7},{7,6},{8,9},{9,8},{10,11... | collective-permute-start | bytes 4718600 | tf_op jit(solution)/shard_map/ppermute | solution.py:487
  291.8 39.3 %collective-permute-start.50 = (bf16[8,48,2304]{2,1,0:T(8,128)(2,1)}, bf16[8,48,2304]{2,1,0:T(8,128)(2,1)}, u32[]{:S(2)}, u32[]{:S(2)}) collective-permute-start(bf16[8,48,2304]{2,1,0:T(8,128)(2,1)} %get-tuple-element.43), channel_id=1, source_target_pairs={{0,1},{1,0},{2,3},{3,2},{4,5},{5,4},{6,7},{7,6},{8,9},{9,8},{10,11... | collective-permute-start | bytes 5308424 | tf_op jit(solution)/shard_map/ppermute | solution.py:487
  305.9 20.7 %collective-permute-start.49 = (bf16[512,768]{1,0:T(8,128)(2,1)}, bf16[512,768]{1,0:T(8,128)(2,1)}, u32[]{:S(2)}, u32[]{:S(2)}) collective-permute-start(bf16[512,768]{1,0:T(8,128)(2,1)} %dynamic-slice_convert_fusion), channel_id=1, source_target_pairs={{0,16},{16,0},{1,17},{17,1},{2,18},{18,2},{3,19},{19,3},{4,20},{20... | collective-permute-start | bytes 2359304 | tf_op jit(solution)/shard_map/ppermute | solution.py:491
  307.1 35.3 %collective-permute-start.48 = (bf16[512,768]{1,0:T(8,128)(2,1)S(1)}, bf16[512,768]{1,0:T(8,128)(2,1)S(1)}, u32[]{:S(2)}, u32[]{:S(2)}) collective-permute-start(bf16[512,768]{1,0:T(8,128)(2,1)S(1)} %constant_dynamic-slice_fusion), channel_id=1, source_target_pairs={{0,16},{16,0},{1,17},{17,1},{2,18},{18,2},{3,19},{19,3},{4,20},{20... | collective-permute-start | bytes 2359304 | tf_op jit(solution)/shard_map/ppermute | solution.py:491
  329.6 20.5 %collective-permute-start.63 = (bf16[4,128,768]{2,1,0:T(8,128)(2,1)S(1)}, bf16[4,128,768]{2,1,0:T(8,128)(2,1)S(1)}, u32[]{:S(2)}, u32[]{:S(2)}) collective-permute-start(bf16[4,128,768]{2,1,0:T(8,128)(2,1)S(1)} %add_convert_fusion.2), channel_id=1, source_target_pairs={{0,2},{1,3},{2,0},{3,1},{4,6},{5,7},{6,4},{7,5},{8,10},{9,11},{10,... | collective-permute-start | bytes 2359304 | tf_op jit(solution)/shard_map/ppermute | solution.py:487
  332.5 36.9 %collective-permute-start.51 = (bf16[4,48,2304]{2,1,0:T(8,128)(2,1)S(1)}, bf16[4,48,2304]{2,1,0:T(8,128)(2,1)S(1)}, u32[]{:S(2)}, u32[]{:S(2)}) collective-permute-start(bf16[4,48,2304]{2,1,0:T(8,128)(2,1)S(1)} %add_convert_fusion.1), channel_id=1, source_target_pairs={{0,2},{1,3},{2,0},{3,1},{4,6},{5,7},{6,4},{7,5},{8,10},{9,11},{10,... | collective-permute-start | bytes 2654216 | tf_op jit(solution)/shard_map/ppermute | solution.py:487
  335.3 71.0 %collective-permute-start.57 = (bf16[4,48,4864]{2,1,0:T(8,128)(2,1)S(1)}, bf16[4,48,4864]{2,1,0:T(8,128)(2,1)S(1)}, u32[]{:S(2)}, u32[]{:S(2)}) collective-permute-start(bf16[4,48,4864]{2,1,0:T(8,128)(2,1)S(1)} %add_convert_fusion), channel_id=1, source_target_pairs={{0,2},{1,3},{2,0},{3,1},{4,6},{5,7},{6,4},{7,5},{8,10},{9,11},{10,... | collective-permute-start | bytes 5603336 | tf_op jit(solution)/shard_map/ppermute | solution.py:487
  370.8 40.6 %collective-permute-start.52 = (bf16[48,2304]{1,0:T(8,128)(2,1)S(1)}, bf16[48,2304]{1,0:T(8,128)(2,1)S(1)}, u32[]{:S(2)}, u32[]{:S(2)}) collective-permute-start(bf16[48,2304]{1,0:T(8,128)(2,1)S(1)} %get-tuple-element.100), channel_id=1, source_target_pairs={{0,4},{1,5},{2,6},{3,7},{4,0},{5,1},{6,2},{7,3},{8,12},{9,13},{10,... | collective-permute-start | bytes 663560 | tf_op jit(solution)/shard_map/ppermute | solution.py:487
  370.9 41.0 %collective-permute-start.54 = (bf16[48,2304]{1,0:T(8,128)(2,1)S(1)}, bf16[48,2304]{1,0:T(8,128)(2,1)S(1)}, u32[]{:S(2)}, u32[]{:S(2)}) collective-permute-start(bf16[48,2304]{1,0:T(8,128)(2,1)S(1)} %get-tuple-element.101), channel_id=1, source_target_pairs={{0,12},{1,13},{2,14},{3,15},{4,8},{5,9},{6,10},{7,11},{8,4},{9,5},... | collective-permute-start | bytes 663560 | tf_op jit(solution)/shard_map/ppermute | solution.py:487
  373.5 38.4 %collective-permute-start.53 = (bf16[48,2304]{1,0:T(8,128)(2,1)S(1)}, bf16[48,2304]{1,0:T(8,128)(2,1)S(1)}, u32[]{:S(2)}, u32[]{:S(2)}) collective-permute-start(bf16[48,2304]{1,0:T(8,128)(2,1)S(1)} %get-tuple-element.102), channel_id=1, source_target_pairs={{0,8},{1,9},{2,10},{3,11},{4,12},{5,13},{6,14},{7,15},{8,0},{9,1},... | collective-permute-start | bytes 663560 | tf_op jit(solution)/shard_map/ppermute | solution.py:487
  408.5 24.5 %collective-permute-start.60 = (bf16[48,4864]{1,0:T(8,128)(2,1)S(1)}, bf16[48,4864]{1,0:T(8,128)(2,1)S(1)}, u32[]{:S(2)}, u32[]{:S(2)}) collective-permute-start(bf16[48,4864]{1,0:T(8,128)(2,1)S(1)} %get-tuple-element.98), channel_id=1, source_target_pairs={{0,12},{1,13},{2,14},{3,15},{4,8},{5,9},{6,10},{7,11},{8,4},{9,5},... | collective-permute-start | bytes 1400840 | tf_op jit(solution)/shard_map/ppermute | solution.py:487
  411.4 39.4 %collective-permute-start.59 = (bf16[48,4864]{1,0:T(8,128)(2,1)S(1)}, bf16[48,4864]{1,0:T(8,128)(2,1)S(1)}, u32[]{:S(2)}, u32[]{:S(2)}) collective-permute-start(bf16[48,4864]{1,0:T(8,128)(2,1)S(1)} %get-tuple-element.99), channel_id=1, source_target_pairs={{0,8},{1,9},{2,10},{3,11},{4,12},{5,13},{6,14},{7,15},{8,0},{9,1},... | collective-permute-start | bytes 1400840 | tf_op jit(solution)/shard_map/ppermute | solution.py:487
  413.1 39.4 %collective-permute-start.55 = (bf16[48,2304]{1,0:T(8,128)(2,1)S(1)}, bf16[48,2304]{1,0:T(8,128)(2,1)S(1)}, u32[]{:S(2)}, u32[]{:S(2)}) collective-permute-start(bf16[48,2304]{1,0:T(8,128)(2,1)S(1)} %fusion.12), channel_id=1, source_target_pairs={{0,16},{16,0},{1,17},{17,1},{2,18},{18,2},{3,19},{19,3},{4,20},{20... | collective-permute-start | bytes 663560 | tf_op jit(solution)/shard_map/ppermute | solution.py:491
  (86 other events, 1327.3 us)

commit v2 on v1

v2 whole, which is shorter than its diff:
```python
import functools
import math

import jax
import jax.numpy as jnp
from jax import lax
from jax.experimental import pallas as pl
from jax.experimental.pallas import tpu as pltpu
from jax.sharding import PartitionSpec as P

HEAD_DIM = 64
EPSILON = 1e-05
MASK_FILL = -1e30
LONGEST = 512
PAIR = 2 * HEAD_DIM
QBLOCK = 128
TBLOCK = 512
FBLOCK = 512
FSTEP = 512
TILE = 1024
BF = jnp.bfloat16
F32 = jnp.float32
ANY = pl.BlockSpec(memory_space=pl.ANY)


def cost(flops, nbytes, trans=0):
    return pl.CostEstimate(flops=int(flops), bytes_accessed=int(nbytes), transcendentals=int(trans))


def whole(shape):
    zeros = (0,) * len(shape)
    return pl.BlockSpec(shape, lambda *_: zeros)


def dot_nt(left, right):
    return lax.dot_general(left, right, (((1,), (1,)), ((), ())), preferred_element_type=F32)


def dot_nn(left, right):
    return lax.dot_general(left, right, (((1,), (0,)), ((), ())), preferred_element_type=F32)


def swap_halves(values):
    lane = lax.broadcasted_iota(jnp.int32, values.shape, 1)
    width = values.shape[1]
    half = HEAD_DIM // 2
    ahead = pltpu.roll(values, width - half, 1)
    behind = pltpu.roll(values, half, 1)
    return jnp.where((lane & (HEAD_DIM - 1)) < half, ahead, behind)


def wide(table, width):
    return jnp.concatenate([table] * (width // table.shape[1]), axis=1)


def load_copies(groups, scratch, sem):
    if len(groups) == 1:
        return [pltpu.make_async_copy(groups[0][0], scratch, sem)]
    rows = scratch.shape[0] // sum(len(places) for _, places in groups)
    me = lax.axis_index("fsdp")
    copies = []
    for piece, places in groups:
        for at, place in enumerate(places):
            target = pl.ds(pl.multiple_of(lax.bitwise_xor(me, place) * rows, 16), rows)
            copies.append(pltpu.make_async_copy(piece.at[pl.ds(at * rows, rows), :], scratch.at[target, :], sem))
    return copies


def start_all(copies):
    for copy in copies:
        copy.start()


def wait_all(copies):
    for copy in copies:
        copy.wait()


def rows_of(block):
    return jnp.transpose(block.astype(F32))[0:8, :]


def project_kernel(places, width, *refs):
    x_ref, cos_ref, sin_ref = refs[:3]
    count = len(places)
    groups = list(zip(refs[3 : 3 + count], places))
    n_ref, q_ref, k_ref, v_ref, gains_ref = refs[3 + count : 8 + count]
    weights, gain, sem = refs[8 + count :]

    @pl.when(pl.program_id(0) == 0)
    def _():
        copies = load_copies(groups, weights, sem)
        start_all(copies)
        wait_all(copies)
        gain[...] = rows_of(weights[:, 3 * width : 3 * width + 128])
        gains_ref[...] = gain[...]

    x = x_ref[...].astype(F32)
    inverse = lax.rsqrt(jnp.mean(x * x, axis=1, keepdims=True) + EPSILON)
    normed = (x * inverse * gain[0:1, :]).astype(BF)
    n_ref[...] = normed
    cosine, sine = wide(cos_ref[...], width // 2), wide(sin_ref[...], width // 2)
    for part, out in enumerate((q_ref, k_ref)):
        for at in range(0, width, width // 2):
            linear = dot_nn(normed, weights[:, part * width + at : part * width + at + width // 2])
            turned = (linear * cosine + swap_halves(linear) * sine).astype(BF)
            if part == 0:
                turned = turned * jnp.asarray(HEAD_DIM**-0.5, BF)
            out[:, at : at + width // 2] = turned
    v_ref[...] = dot_nn(normed, weights[:, 2 * width : 3 * width]).astype(BF)


def project(x, cosine, sine, groups):
    tokens, width = x.shape
    total = groups[0][0].shape[1]
    shape = jax.ShapeDtypeStruct((tokens, width), BF)
    block = pl.BlockSpec((TBLOCK, width), lambda i: (i, 0))
    table = pl.BlockSpec((TBLOCK, PAIR), lambda i: (i, 0))
    return pl.pallas_call(
        functools.partial(project_kernel, [places for _, places in groups], width),
        name="project",
        out_shape=[shape] * 4 + [jax.ShapeDtypeStruct((8, width), F32)],
        grid=(tokens // TBLOCK,),
        in_specs=[block, table, table] + [ANY] * len(groups),
        out_specs=[block] * 4 + [whole((8, width))],
        scratch_shapes=[
            pltpu.VMEM((width, total), BF),
            pltpu.VMEM((8, width), F32),
            pltpu.SemaphoreType.DMA,
        ],
        cost_estimate=cost(6 * tokens * width * width, 6 * width * width + 10 * tokens * width),
    )(x, cosine, sine, *[piece for piece, _ in groups])


def split_heads(values):
    lane = lax.broadcasted_iota(jnp.int32, values.shape, 1)
    zero = jnp.zeros_like(values)
    return jnp.concatenate(
        [jnp.where(lane < HEAD_DIM, values, zero), jnp.where(lane < HEAD_DIM, zero, values)], axis=0
    )


def join_heads(both):
    rows = both.shape[1] // 2
    own = jnp.concatenate([both[:HEAD_DIM, :rows], both[HEAD_DIM:, rows:]], axis=0)
    return jnp.transpose(own)


def masked_bias(starts_row, first_key, span, first_row):
    key = first_key + lax.broadcasted_iota(jnp.int32, (span, QBLOCK), 0)
    query = first_row + lax.broadcasted_iota(jnp.int32, (span, QBLOCK), 1)
    allowed = (key >= starts_row) & (key <= query)
    return jnp.where(allowed, 0.0, MASK_FILL)


def per_span(first_ref, length, body):
    block = pl.program_id(0)
    seen = block - first_ref[block] + 1
    most = min(length, LONGEST + QBLOCK) // QBLOCK
    for blocks in range(1, most + 1):

        @pl.when(seen == blocks)
        def _(blocks=blocks):
            first_key = pl.multiple_of((block - blocks + 1) * QBLOCK, QBLOCK)
            body(blocks * QBLOCK, first_key, block * QBLOCK)


def attend_kernel(pairs, first_ref, q_ref, k_ref, v_ref, starts_ref, out_ref, lse_ref, v_turned, bias):
    @pl.when(pl.program_id(0) == 0)
    def _():
        v_turned[...] = jnp.transpose(v_ref[...])

    def body(span, first_key, first_row):
        bias[:span, :] = masked_bias(starts_ref[...], first_key, span, first_row)
        keys_at = pl.ds(first_key, span)
        lanes = [slice(pair * PAIR, (pair + 1) * PAIR) for pair in range(pairs)]
        scored, weighed = {}, {}
        for step in range(pairs + 2):
            if step < pairs:
                scored[step] = dot_nt(k_ref[keys_at, lanes[step]], split_heads(q_ref[:, lanes[step]])).astype(BF)
            pair = step - 2
            if pair >= 0:
                weights, total = weighed.pop(pair)
                both = dot_nn(v_turned[lanes[pair], keys_at], weights) * (1.0 / total)
                out_ref[:, lanes[pair]] = join_heads(both).astype(BF)
            pair = step - 1
            if 0 <= pair < pairs:
                fill = bias[:span, :]
                scores = scored.pop(pair).astype(F32) + jnp.concatenate([fill, fill], axis=1)
                top = jnp.max(scores, axis=0, keepdims=True)
                weights = jnp.exp(scores - top)
                total = jnp.sum(weights, axis=0, keepdims=True)
                lse_ref[0, pair : pair + 1, :] = top + jnp.log(total)
                weighed[pair] = (weights.astype(BF), total)

    per_span(first_ref, k_ref.shape[0], body)


def attend(queries, keys, values, starts, first):
    length, width = queries.shape
    pairs = width // PAIR
    blocks = length // QBLOCK
    block = pl.BlockSpec((QBLOCK, width), lambda i, f: (i, 0))
    return pl.pallas_call(
        functools.partial(attend_kernel, pairs),
        name="attend",
        out_shape=[
            jax.ShapeDtypeStruct((length, width), BF),
            jax.ShapeDtypeStruct((blocks, pairs, 2 * QBLOCK), F32),
        ],
        grid_spec=pltpu.PrefetchScalarGridSpec(
            num_scalar_prefetch=1,
            grid=(blocks,),
            in_specs=[
                block,
                whole((length, width)),
                whole((length, width)),
                pl.BlockSpec((1, QBLOCK), lambda i, f: (0, i)),
            ],
            out_specs=[block, pl.BlockSpec((1, pairs, 2 * QBLOCK), lambda i, f: (i, 0, 0))],
            scratch_shapes=[
                pltpu.VMEM((width, length), BF),
                pltpu.VMEM((min(length, LONGEST + QBLOCK), QBLOCK), F32),
            ],
        ),
        cost_estimate=cost(4 * length * length * width, 10 * length * width),
    )(first, queries, keys, values, starts)


def attend_back_kernel(
    pairs, first_ref, q_ref, k_ref, v_ref, g_ref, lse_ref, starts_ref, cos_ref, sin_ref, out_ref, k_turned, bias, dk, dv
):
    width = pairs * PAIR
    block = pl.program_id(0)

    @pl.when(block == 0)
    def _():
        k_turned[...] = jnp.transpose(k_ref[...])
        dk[...] = jnp.zeros_like(dk)
        dv[...] = jnp.zeros_like(dv)

    rows = pl.ds(pl.multiple_of(block * QBLOCK, QBLOCK), QBLOCK)
    cosine, sine = cos_ref[rows, :], sin_ref[rows, :]

    def body(span, first_key, first_row):
        bias[:span, :] = masked_bias(starts_ref[...], first_key, span, first_row)
        keys_at = pl.ds(first_key, span)
        lanes = [slice(pair * PAIR, (pair + 1) * PAIR) for pair in range(pairs)]
        scored, ready = {}, {}
        for step in range(pairs + 2):
            if step < pairs:
                at = lanes[step]
                queries, grads = split_heads(q_ref[:, at]), split_heads(g_ref[:, at])
                scores = dot_nt(k_ref[keys_at, at], queries).astype(BF)
                scored[step] = (scores, dot_nt(v_ref[keys_at, at], grads), queries, grads)
            pair = step - 2
            if pair >= 0:
                at = lanes[pair]
                probs, grad_scores, queries, grads = ready.pop(pair)
                dv[keys_at, at] += dot_nn(probs, grads)
                dk[keys_at, at] += dot_nn(grad_scores, queries)
                both = dot_nn(k_turned[at, keys_at], grad_scores)
                dq = (join_heads(both) * HEAD_DIM**-0.5).astype(BF).astype(F32)
                out_ref[rows, at] = (dq * cosine - swap_halves(dq) * sine).astype(BF)
            pair = step - 1
            if 0 <= pair < pairs:
                scores, grad_probs, queries, grads = scored.pop(pair)
                fill = bias[:span, :]
                scores = scores.astype(F32) + jnp.concatenate([fill, fill], axis=1)
                probs = jnp.exp(scores - lse_ref[0, pair : pair + 1, :])
                delta = jnp.sum(probs * grad_probs, axis=0, keepdims=True)
                ready[pair] = (probs.astype(BF), (probs * (grad_probs - delta)).astype(BF), queries, grads)

    per_span(first_ref, k_ref.shape[0], body)

    @pl.when(block == pl.num_programs(0) - 1)
    def _():
        def finish(step, carry):
            at = pl.ds(pl.multiple_of(step * QBLOCK, QBLOCK), QBLOCK)
            turn, slant = cos_ref[at, :], sin_ref[at, :]
            for pair in range(pairs):
                lanes = slice(pair * PAIR, (pair + 1) * PAIR)
                grad = dk[at, lanes].astype(BF).astype(F32)
                out_ref[at, width + pair * PAIR : width + (pair + 1) * PAIR] = (
                    grad * turn - swap_halves(grad) * slant
                ).astype(BF)
            out_ref[at, 2 * width : 3 * width] = dv[at, :].astype(BF)
            return carry

        lax.fori_loop(0, k_ref.shape[0] // QBLOCK, finish, 0)


def attend_back(queries, keys, values, grads, lse, starts, first, cosine, sine):
    length, width = queries.shape
    pairs = width // PAIR
    blocks = length // QBLOCK
    block = pl.BlockSpec((QBLOCK, width), lambda i, f: (i, 0))
    full = whole((length, width))
    table = whole((length, PAIR))
    return pl.pallas_call(
        functools.partial(attend_back_kernel, pairs),
        name="attend_back",
        out_shape=jax.ShapeDtypeStruct((length, 3 * width), BF),
        grid_spec=pltpu.PrefetchScalarGridSpec(
            num_scalar_prefetch=1,
            grid=(blocks,),
            in_specs=[
                block,
                full,
                full,
                block,
                pl.BlockSpec((1, pairs, 2 * QBLOCK), lambda i, f: (i, 0, 0)),
                pl.BlockSpec((1, QBLOCK), lambda i, f: (0, i)),
                table,
                table,
            ],
            out_specs=whole((length, 3 * width)),
            scratch_shapes=[
                pltpu.VMEM((width, length), BF),
                pltpu.VMEM((min(length, LONGEST + QBLOCK), QBLOCK), F32),
                pltpu.VMEM((length, width), F32),
                pltpu.VMEM((length, width), F32),
            ],
        ),
        cost_estimate=cost(10 * length * length * width, 16 * length * width),
    )(first, queries, keys, values, grads, lse, starts, cosine, sine)


def packed_slices(rows, down_rows, width, hidden_width):
    slices = [("down", (0, down_rows), (0, width), 0, 0), ("out", (0, rows), (0, width), down_rows, 0)]
    top = down_rows + rows
    both = 2 * hidden_width
    for at in range(0, both - width + 1, width):
        slices.append(("both", (0, rows), (at, at + width), top, 0))
        top += rows
    rest = both % width
    if rest:
        few = rows * rest // width
        for place in range(width // rest):
            slices.append(("both", (place * few, (place + 1) * few), (both - rest, both), top, place * rest))
        top += few
    return slices, top


def feed_copies(packed, targets, owner, sems):
    w_out, w_both, w_down = targets
    parts = w_out.shape[0] // packed[0]
    rows, down_rows = packed[0], w_down.shape[0] // parts
    slices, height = packed_slices(rows, down_rows, w_out.shape[1], w_down.shape[0])
    kinds = {"out": (w_out, rows, 0), "both": (w_both, rows, 1), "down": (w_down, down_rows, 2)}
    copies = {"out": [], "both": [], "down": []}
    for name, (low, high), (left, right), top, column in slices:
        target, each, number = kinds[name]
        source = packed[1].at[
            pl.ds(pl.multiple_of(owner * height + top, 16), high - low), column : column + right - left
        ]
        goal = target.at[pl.ds(pl.multiple_of(owner * each + low, 16), high - low), left:right]
        copies[name].append(pltpu.make_async_copy(source, goal, sems.at[number]))
    return copies


def feed_kernel(rows, count, width, hidden_width, *refs):
    x_ref, att_ref, dy_ref, gain_ref = refs[:4]
    given, refs = refs[4 : 4 + count], refs[4 + count :]
    y_ref, n_ref, hid_ref, dgate_ref, dup_ref, dm_ref, dmr_ref, datt_ref = refs[:8]
    w_out, w_both, w_down, sems = refs[8:]
    targets = (w_out, w_both, w_down)
    parts = width // rows

    def whole_copies():
        views = (w_out, w_both.at[:, :hidden_width], w_both.at[:, hidden_width:], w_down)
        return [pltpu.make_async_copy(piece, view, sems.at[0]) for piece, view in zip(given, views)]

    def per_owner(act):
        def step(owner, carry):
            act(feed_copies((rows, given[0]), targets, owner, sems))
            return carry

        lax.fori_loop(0, parts, step, 0)

    @pl.when(pl.program_id(0) == 0)
    def _():
        if count > 1:
            copies = whole_copies()
            start_all(copies)
            wait_all(copies)
        else:
            per_owner(lambda copies: start_all(copies["out"] + copies["both"] + copies["down"]))
            per_owner(lambda copies: wait_all(copies["out"] + copies["both"] + copies["down"]))

    gain = gain_ref[1:2, :]
    dy = dy_ref[...]
    middle = x_ref[...].astype(F32) + dot_nn(att_ref[...], w_out[...])
    inverse = lax.rsqrt(jnp.mean(middle * middle, axis=1, keepdims=True) + EPSILON)
    normed = (middle * inverse * gain).astype(BF)
    n_ref[...] = normed
    result = middle
    back = jnp.zeros_like(middle)
    step = min(FSTEP, hidden_width)
    for at in range(0, hidden_width, step):
        part = slice(at, at + step)
        w_gate = w_both[:, at : at + step]
        w_up = w_both[:, hidden_width + at : hidden_width + at + step]
        gate = dot_nn(normed, w_gate)
        up = dot_nn(normed, w_up)
        dh = dot_nt(dy, w_down[part, :])
        sigma = 1.0 / (1.0 + jnp.exp(-gate))
        silu = gate * sigma
        hidden = (silu * up).astype(BF)
        hid_ref[:, part] = hidden
        dgate = (dh * up * (sigma * (1.0 + gate * (1.0 - sigma)))).astype(BF)
        dup = (dh * silu).astype(BF)
        dgate_ref[:, part] = dgate
        dup_ref[:, part] = dup
        result = result + dot_nn(hidden, w_down[part, :])
        back = back + dot_nt(dgate, w_gate) + dot_nt(dup, w_up)
    y_ref[...] = result.astype(BF)
    scaled = back * gain
    dm = dy.astype(F32) + inverse * scaled - middle * (inverse * inverse * inverse) * jnp.mean(
        scaled * middle, axis=1, keepdims=True
    )
    dm_ref[...] = dm
    dmr = dm.astype(BF)
    dmr_ref[...] = dmr
    datt_ref[...] = dot_nt(dmr, w_out[...]).astype(BF)


def feed(x, attended, dy, gain, given, rows, hidden_width):
    tokens, width = x.shape
    block = pl.BlockSpec((FBLOCK, width), lambda i: (i, 0))
    broad = pl.BlockSpec((FBLOCK, hidden_width), lambda i: (i, 0))
    narrow, large = jax.ShapeDtypeStruct((tokens, width), BF), jax.ShapeDtypeStruct((tokens, hidden_width), BF)
    return pl.pallas_call(
        functools.partial(feed_kernel, rows, len(given), width, hidden_width),
        name="feed",
        out_shape=[narrow, narrow, large, large, large, jax.ShapeDtypeStruct((tokens, width), F32), narrow, narrow],
        grid=(tokens // FBLOCK,),
        in_specs=[block, block, block, whole((8, width))] + [ANY] * len(given),
        out_specs=[block, block, broad, broad, broad, block, block, block],
        scratch_shapes=[
            pltpu.VMEM((width, width), BF),
            pltpu.VMEM((width, 2 * hidden_width), BF),
            pltpu.VMEM((hidden_width, width), BF),
            pltpu.SemaphoreType.DMA((3,)),
        ],
        cost_estimate=cost(4 * tokens * width * (width + 3 * hidden_width), 20 * tokens * width + 6 * tokens * hidden_width),
    )(x, attended, dy, gain, *given)


def dot_tn(left, right):
    return lax.dot_general(left, right, (((0,), (0,)), ((), ())), preferred_element_type=F32)


def write_pieces(parts, total, keep, send):
    if parts == 1:
        keep[...] = total[...].astype(BF)
        return
    rows = total.shape[0] // parts
    me = lax.axis_index("fsdp")
    for place in range(parts // 2):
        upper, y_bit = place % (parts // 4), place // (parts // 4)
        for core, out in enumerate((keep, send)):
            owner = lax.bitwise_xor(me, upper * 4 + y_bit * 2 + core)
            out[place] = total[pl.ds(pl.multiple_of(owner * rows, 16), rows), :].astype(BF)


def outer_kernel(parts, counts, edges, *refs):
    lefts = []
    for count in counts:
        lefts.append(refs[:count])
        refs = refs[count:]
    rights, outs, total = refs[: len(counts)], refs[len(counts) : -1], refs[-1]
    step = pl.program_id(0)
    low = 0
    for group, right, high in zip(lefts, rights, edges):

        @pl.when((step >= low) & (step < high))
        def _(group=group, right=right):
            row = 0
            for left in group:
                total[row : row + left.shape[1], :] = dot_tn(left[...], right[...])
                row += left.shape[1]

        low = high
    write_pieces(parts, total, *((outs + (None,))[:2]))


def outer_sums(parts, pairs, tile, name):
    edges, specs, low = [], [], 0
    for lefts, right in pairs:
        steps = right.shape[1] // tile
        specs.append(
            pl.BlockSpec(
                (right.shape[0], tile), lambda j, low=low, steps=steps: (0, jnp.clip(j - low, 0, steps - 1))
            )
        )
        low += steps
        edges.append(low)
    width = low * tile
    tokens = pairs[0][1].shape[0]
    rows = sum(left.shape[1] for left in pairs[0][0])
    every_left = [left for lefts, _ in pairs for left in lefts]
    shape = (rows, width) if parts == 1 else (parts // 2, rows // parts, width)
    out_block = (rows, tile) if parts == 1 else (parts // 2, rows // parts, tile)
    index = (lambda j: (0, j)) if parts == 1 else (lambda j: (0, 0, j))
    n_out = 1 if parts == 1 else 2
    return pl.pallas_call(
        functools.partial(outer_kernel, parts, tuple(len(lefts) for lefts, _ in pairs), tuple(edges)),
        name=name,
        out_shape=[jax.ShapeDtypeStruct(shape, BF)] * n_out,
        grid=(low,),
        in_specs=[whole(left.shape) for left in every_left] + specs,
        out_specs=[pl.BlockSpec(out_block, index)] * n_out,
        scratch_shapes=[pltpu.VMEM((rows, tile), F32)],
        cost_estimate=cost(2 * tokens * rows * width, 2 * tokens * (rows + width) + 2 * rows * width),
    )(*every_left, *[right for _, right in pairs])


def feed_grads_kernel(parts, steps, n_ref, dgate_ref, dup_ref, hid_any, dy_any, out_ref, hidden, dy, total, sems):
    step = pl.program_id(0)
    tile = out_ref.shape[2]
    width = n_ref.shape[1]
    copies = [pltpu.make_async_copy(hid_any, hidden, sems.at[0]), pltpu.make_async_copy(dy_any, dy, sems.at[1])]

    @pl.when(step == 0)
    def _():
        start_all(copies)

    for low, right in ((0, dgate_ref), (steps, dup_ref)):

        @pl.when((step >= low) & (step < low + steps))
        def _(right=right):
            out_ref[...] = dot_tn(n_ref[...], right[...]).astype(BF).reshape(out_ref.shape)

    @pl.when(step == 2 * steps)
    def _():
        wait_all(copies)
        each = hidden.shape[1] // 2
        for at in (0, each):
            grad = dot_tn(hidden[:, at : at + each], dy[...]).astype(BF)
            total[at * parts // hidden.shape[1] : (at + each) * parts // hidden.shape[1]] = grad.reshape(
                parts // 2, hidden.shape[1] // parts, width
            )

    for place in range(steps):

        @pl.when(step == 2 * steps + place)
        def _(place=place):
            unit = 16 * parts
            for group in range(tile // unit):
                rows = slice((place * tile // unit + group) * 16, (place * tile // unit + group + 1) * 16)
                for column in range(width // unit):
                    out_ref[:, column * 16 : (column + 1) * 16, group * unit : (group + 1) * unit] = total[
                        :, rows, column * unit : (column + 1) * unit
                    ]


def feed_grads(parts, normed, dgate, dup, hidden, dy):
    tokens, width = normed.shape
    hidden_width = hidden.shape[1]
    tile = min(TILE, hidden_width)
    steps = hidden_width // tile
    rows = width // parts
    return pl.pallas_call(
        functools.partial(feed_grads_kernel, parts, steps),
        name="feed_grads",
        out_shape=jax.ShapeDtypeStruct((parts, 3 * rows, hidden_width), BF),
        grid=(3 * steps,),
        in_specs=[
            whole((tokens, width)),
            pl.BlockSpec((tokens, tile), lambda j: (0, jnp.minimum(j, steps - 1))),
            pl.BlockSpec((tokens, tile), lambda j: (0, jnp.clip(j - steps, 0, steps - 1))),
            ANY,
            ANY,
        ],
        out_specs=pl.BlockSpec((parts, rows, tile), lambda j: (0, j // steps, j % steps)),
        scratch_shapes=[
            pltpu.VMEM((tokens, hidden_width), BF),
            pltpu.VMEM((tokens, width), BF),
            pltpu.VMEM((parts, hidden_width // parts, width), BF),
            pltpu.SemaphoreType.DMA((2,)),
        ],
        cost_estimate=cost(6 * tokens * width * hidden_width, 6 * tokens * (hidden_width + width)),
    )(normed, dgate, dup, hidden, dy)


def input_grad_kernel(places, width, *refs):
    count = len(places)
    x_ref, dm_ref, grads_ref, gains_ref = refs[:4]
    groups = list(zip(refs[4 : 4 + count], places))
    out_ref, weights, sem = refs[4 + count :]

    @pl.when(pl.program_id(0) == 0)
    def _():
        copies = load_copies(groups, weights, sem)
        start_all(copies)
        wait_all(copies)

    x = x_ref[...].astype(F32)
    inverse = lax.rsqrt(jnp.mean(x * x, axis=1, keepdims=True) + EPSILON)
    scaled = dot_nt(grads_ref[...], weights[:, : 3 * width]) * gains_ref[0:1, :]
    out_ref[...] = (
        dm_ref[...]
        + inverse * scaled
        - x * (inverse * inverse * inverse) * jnp.mean(scaled * x, axis=1, keepdims=True)
    )


def input_grad(x, dm, grads, gains, groups):
    tokens, width = x.shape
    block = pl.BlockSpec((TBLOCK, width), lambda i: (i, 0))
    return pl.pallas_call(
        functools.partial(input_grad_kernel, [places for _, places in groups], width),
        name="input_grad",
        out_shape=jax.ShapeDtypeStruct((tokens, width), F32),
        grid=(tokens // TBLOCK,),
        in_specs=[block, block, pl.BlockSpec((TBLOCK, 3 * width), lambda i: (i, 0)), whole((8, width))]
        + [ANY] * len(groups),
        out_specs=block,
        scratch_shapes=[
            pltpu.VMEM((width, groups[0][0].shape[1]), BF),
            pltpu.SemaphoreType.DMA,
        ],
        cost_estimate=cost(6 * tokens * width * width, 6 * width * width + 16 * tokens * width),
    )(x, dm, grads, gains, *[piece for piece, _ in groups])


def flip(values, bits):
    count = lax.axis_size("fsdp")
    return lax.ppermute(values, "fsdp", [(i, i ^ bits) for i in range(count)])


def across(values):
    return lax.ppermute(values, "seq", [(0, 1), (1, 0)])


def aligned(rows, down_rows, width, hidden_width, count):
    rest = 2 * hidden_width % width
    return (
        count == 16
        and rows % 16 == 0
        and down_rows % 16 == 0
        and (rest == 0 or (width % rest == 0 and rows * rest % (16 * width) == 0))
    )


def gate(values, *others):
    return lax.optimization_barrier((values,) + others)[0]


def gather_rows(shard, parts):
    if parts == 1:
        return [(lax.all_gather(shard, "fsdp", axis=0, tiled=True), (0,))]
    uppers = tuple(range(0, parts, 4))
    mine = jnp.concatenate([shard] + [flip(shard, upper) for upper in uppers[1:]])
    beside = flip(mine, 2)
    groups = [(mine, 0), (beside, 2), (flip(mine, 1), 1), (flip(beside, 1), 3)]
    return [(piece, tuple(upper + low for upper in uppers)) for piece, low in groups]


def pack(w_out, w_gate, w_up, w_down):
    rows, width = w_out.shape
    sources = {"down": w_down, "out": w_out, "both": jnp.concatenate([w_gate, w_up], axis=1)}
    slices, _ = packed_slices(rows, w_down.shape[0], width, w_gate.shape[1])
    strips, line, filled = [], [], 0
    for name, (low, high), (left, right), _, _ in slices:
        line.append(sources[name][low:high, left:right])
        filled += right - left
        if filled == width:
            strips.append(line[0] if len(line) == 1 else jnp.concatenate(line, axis=1))
            line, filled = [], 0
    return jnp.concatenate(strips)


class Scatter:
    def __init__(self, outs, parts):
        self.parts = parts
        if parts == 1:
            self.total = lax.psum_scatter(outs[0], "fsdp", scatter_dimension=0, tiled=True)
            return
        self.keep, send = outs
        self.got = flip(send, 1)

    def y_hop(self):
        if self.parts == 1:
            return []
        upper = self.parts // 4
        ahead = (self.keep[upper:].astype(F32) + self.got[upper:].astype(F32)).astype(BF)
        self.ahead = flip(ahead, 2)
        return [ahead]

    def z_hop(self):
        if self.parts == 1:
            return []
        sums = [
            self.keep[j].astype(F32) + self.got[j].astype(F32) + self.ahead[j].astype(F32)
            for j in range(self.parts // 4)
        ]
        self.own, sends = sums[0], [total.astype(BF) for total in sums[1:]]
        self.others = [flip(send, 4 * (j + 1)) for j, send in enumerate(sends)]
        return sends

    def x_hop(self):
        if self.parts > 1:
            total = self.own
            for piece in self.others:
                total = total + piece.astype(F32)
            self.total = total.astype(BF)
        self.partner = across(self.total)
        return [self.total]

    def result(self):
        return self.total.astype(F32) + self.partner.astype(F32)


def rope_tables(length):
    half = HEAD_DIM // 2
    inverse = jnp.exp(jnp.arange(half, dtype=F32) * (-2.0 * math.log(10000.0) / HEAD_DIM))
    angles = jnp.arange(length, dtype=jnp.int32).astype(F32)[:, None] * inverse[None, :]
    cosine, sine = jnp.cos(angles), jnp.sin(angles)
    return (
        jnp.concatenate([cosine] * 4, axis=1),
        jnp.concatenate([-sine, sine, -sine, sine], axis=1),
    )


def per_device(
    tokens, doc_ids, cotangent, w_query, w_key, w_value, w_out, w_gate, w_up, w_down, gain_attn, gain_ffn
):
    seq_rank = lax.axis_index("seq")
    count = lax.axis_size("fsdp")
    micro, _, span, width = tokens.shape
    hidden_width = w_gate.shape[1]
    rows = w_query.shape[0]
    parts = count if aligned(rows, w_down.shape[0], width, hidden_width, count) else 1

    if parts == 1:
        given = [lax.all_gather(weight, "fsdp", axis=0, tiled=True) for weight in (w_out, w_gate, w_up, w_down)]
    else:
        given = [lax.all_gather(pack(w_out, w_gate, w_up, w_down), "fsdp", axis=0, tiled=True)]

    def exchanged(array):
        own = lax.dynamic_index_in_dim(array, seq_rank, 0, keepdims=False)[0]
        return own, lax.dynamic_index_in_dim(array, 1 - seq_rank, 0, keepdims=False)[0]

    def ordered(own, other):
        return jnp.where(seq_rank == 0, jnp.concatenate([own, other]), jnp.concatenate([other, own]))

    def halves(array):
        own = lax.dynamic_slice_in_dim(array, seq_rank * span, span, 0)
        other = lax.dynamic_slice_in_dim(array, (1 - seq_rank) * span, span, 0)
        return own, other

    def give_back(own, other):
        first, second = jnp.where(seq_rank == 0, own, other), jnp.where(seq_rank == 0, other, own)
        return jnp.stack([first, second])[:, None]

    column = jnp.pad(jnp.stack([gain_attn, gain_ffn], axis=1), ((0, 0), (0, 126)))
    w_in = jnp.concatenate([w_query, w_key, w_value, column], axis=1)
    groups_in = gather_rows(w_in, parts)
    own_x, other_x = exchanged(tokens)
    x = ordered(own_x, across(other_x))
    own_docs, other_docs = exchanged(doc_ids)
    docs = ordered(own_docs, across(other_docs))
    own_dy, other_dy = exchanged(gate(cotangent, x))
    dy = ordered(own_dy, across(other_dy))

    length = x.shape[0]
    cosine, sine = rope_tables(length)
    starts = jnp.sum((docs[None, :] < docs[:, None]).astype(jnp.int32), axis=1)
    first = starts[::QBLOCK] // QBLOCK
    starts = starts[None, :]

    normed, queries, keys, values, gains = project(x, cosine, sine, groups_in)
    attended, lse = attend(queries, keys, values, starts, first)
    y, normed_two, hidden, dgate, dup, dm, dmr, datt = feed(
        x, attended, dy, gains, given, rows if parts > 1 else width, hidden_width
    )
    own_y, other_y = halves(y)
    output = give_back(own_y, across(other_y))

    if parts == 1:
        sum_gate, sum_up, sum_down = [
            lax.psum_scatter(outer_sums(1, [(lefts, right)], tile, name)[0], "fsdp", scatter_dimension=0, tiled=True)
            for lefts, right, tile, name in (
                ([normed_two], dgate, 512, "grad_gate"),
                ([normed_two], dup, 512, "grad_up"),
                ([hidden], dy, width // 2, "grad_down"),
            )
        ]
        sums = (sum_gate, sum_up, sum_down)
    else:
        ff = feed_grads(parts, normed_two, dgate, dup, hidden, dy)
        datt = gate(datt, ff)
        ff = lax.psum_scatter(ff.reshape(-1, hidden_width), "fsdp", scatter_dimension=0, tiled=True)
        sums = (ff,)
    grads = attend_back(queries, keys, values, datt, lse, starts, first, cosine, sine)
    scatter = Scatter(outer_sums(parts, [([normed], grads), ([attended], dmr)], width, "grad_in"), parts)
    grad_x = input_grad(x, dm, grads, gains, groups_in)
    own_g, other_g = halves(grad_x)
    scatter.y_hop()
    grad_tokens = give_back(own_g, across(other_g.astype(BF)).astype(F32))
    scatter.z_hop()
    scatter.x_hop()
    sum_in = scatter.result()
    sums = [part.astype(F32) + across(part).astype(F32) for part in sums]
    if parts == 1:
        sum_gate, sum_up, sum_down = sums
    else:
        sum_gate, sum_up, rest = sums[0][:rows], sums[0][rows : 2 * rows], sums[0][2 * rows :]
        unit = 16 * parts
        rest = rest.reshape(rows // 16, 16, hidden_width // unit, unit)
        sum_down = rest.transpose(2, 1, 0, 3).reshape(w_down.shape)

    sum_in, sum_out = sum_in[:, : 3 * width], sum_in[:, 3 * width :]
    grad_gain_attn = jnp.sum(w_in[:, : 3 * width].astype(F32) * sum_in, axis=1) / gain_attn.astype(F32)
    grad_gain_ffn = (
        jnp.sum(w_gate.astype(F32) * sum_gate, axis=1) + jnp.sum(w_up.astype(F32) * sum_up, axis=1)
    ) / gain_ffn.astype(F32)
    by_part = [sum_in[:, at * width : (at + 1) * width] for at in range(3)]
    return (output, grad_tokens, *by_part, sum_out, sum_gate, sum_up, sum_down, grad_gain_attn, grad_gain_ffn)


def solution(mesh):
    rows = P("fsdp", None)
    acts = P(None, "fsdp", "seq", None)
    return jax.shard_map(
        per_device,
        mesh=mesh,
        in_specs=(acts, P(None, "fsdp", "seq"), acts) + (rows,) * 7 + (P("fsdp"),) * 2,
        out_specs=(acts, acts) + (rows,) * 7 + (P("fsdp"),) * 2,
        check_vma=False,
    )
```

time: 473 us -> 343 us (0.73)
  waiting for transfers between devices: 209 us -> 143 us
  starting transfers between devices: 54.3 us -> 22.8 us
  Pallas kernels: 150 us -> 120 us
  between operations: 1.81 us -> 14.6 us
  other arithmetic: 33.3 us -> 22.3 us
    ppermute x60 -> x11, waiting for transfers between devices: 169 us -> 120 us  [flip(): return lax.ppermute(values, 'fsdp', [(i, i ^ bits) for i in range(count)])]
    ppermute x60 -> x11, starting transfers between devices: 46.6 us -> 13.8 us  [flip(): return lax.ppermute(values, 'fsdp', [(i, i ^ bits) for i in range(count)])]
    ppermute x8 -> x7, waiting for transfers between devices: 40 us -> 22.8 us  [across(): return lax.ppermute(values, 'seq', [(0, 1), (1, 0)])]
    pallas_call x6 -> x5, Pallas kernels: 98.6 us -> 82.7 us  [the longest x1 34.6 us: feed(): pl.pallas_call(functools.partial(feed_kernel, rows, len(given), width, hi...]
    convert_element_type x9 -> x3, other arithmetic: 13.2 us -> 3.37 us  [the longest x1 2.72 us: y_hop(): (self.keep[upper:].astype(F32) + self.got[upper:].astype(F32)).astype(BF)]
    pallas_call x1, Pallas kernels: 23.8 us -> 14.2 us  [attend(): pl.pallas_call(functools.partial(attend_kernel, pairs), name='attend', ou...]
    pallas_call x1, Pallas kernels: 28 us -> 23.2 us  [attend_back(): pl.pallas_call(functools.partial(attend_back_kernel, pairs), name='attend...]
  transfers between devices with their start and end apart: 68 -> 20, of which waited for: 27 -> 10; matrix products, arithmetic and copies ran while one was open for 10% -> 7% of each run, Pallas kernels for 20% -> 21%
where the time goes in v2:
time: 343 us; the launch traced here: 337 us
  waiting for transfers between devices  143 us (42%)
  Pallas kernels  120 us (35%)
  starting transfers between devices  22.8 us (7%)
  other arithmetic  22.3 us (7%)
  between operations  14.6 us (4%)
  local copies, waits for them, and re-layouts  13.4 us (4%)
    ppermute x11, waiting for transfers between devices, flip(): return lax.ppermute(values, 'fsdp', [(i, i ^ bits) for i in range(count)])  120 us
    pallas_call x1, Pallas kernels, feed(): pl.pallas_call(functools.partial(feed_kernel, rows, len(given), width, hi...  34.6 us
    pallas_call x1, Pallas kernels, attend_back(): pl.pallas_call(functools.partial(attend_back_kernel, pairs), name='attend...  23.2 us
    ppermute x7, waiting for transfers between devices, across(): return lax.ppermute(values, 'seq', [(0, 1), (1, 0)])  22.8 us
    pallas_call x1, Pallas kernels, feed_grads(): pl.pallas_call(functools.partial(feed_grads_kernel, parts, steps), name='...  15.9 us
    pallas_call x1, Pallas kernels, attend(): pl.pallas_call(functools.partial(attend_kernel, pairs), name='attend', ou...  14.2 us
    ppermute x11, starting transfers between devices, flip(): return lax.ppermute(values, 'fsdp', [(i, i ^ bits) for i in range(count)])  13.8 us
    pallas_call x1, Pallas kernels, input_grad(): pl.pallas_call(functools.partial(input_grad_kernel, [places for _, places...  10.9 us
  transfers between devices with their start and end apart: 20, of which 10 were waited for; matrix products, arithmetic and copies ran while one was open for 7% of the time, Pallas kernels for 21%

profile of v2, /device:TPU:0, one launch (start us, length us, event | category | flops | bytes accessed | tf_op | source)
XLA Modules:
  0.0 336.6 jit_solution(9967248367174150496)
XLA Ops:
  16.2 5.1 %collective-permute-start.4 = (bf16[48,2432]{1,0:T(8,128)(2,1)}, bf16[48,2432]{1,0:T(8,128)(2,1)}, u32[]{:S(2)}, u32[]{:S(2)}) collective-permute-start(bf16[48,2432]{1,0:T(8,128)(2,1)} %pad_maximum_fusion.3), channel_id=1, source_target_pairs={{0,12},{1,13},{2,14},{3,15},{4,8},{5,9},{6,10},{7,11},{8,4},{9,5},... | collective-permute-start | bytes 700424 | tf_op jit(solution)/shard_map/ppermute | solution.py:630
  22.8 1.7 collective-permute-start
  24.5 3.7 %collective-permute-done.4 = bf16[48,2432]{1,0:T(8,128)(2,1)} collective-permute-done((bf16[48,2432]{1,0:T(8,128)(2,1)}, bf16[48,2432]{1,0:T(8,128)(2,1)}, u32[]{:S(2)}, u32[]{:S(2)}) %collective-permute-start.4) | collective-permute-done | bytes 233504 | tf_op jit(solution)/shard_map/ppermute | solution.py:630
  28.2 33.8 %collective-permute-done.3 = bf16[48,2432]{1,0:T(8,128)(2,1)} collective-permute-done((bf16[48,2432]{1,0:T(8,128)(2,1)}, bf16[48,2432]{1,0:T(8,128)(2,1)}, u32[]{:S(2)}, u32[]{:S(2)}) %collective-permute-start.3) | collective-permute-done | bytes 233504 | tf_op jit(solution)/shard_map/ppermute | solution.py:630
  63.3 1.6 collective-permute-start.5
  64.9 1.5 collective-permute-start.1
  66.5 1.8 maximum_select_fusion.refs_0_
  69.0 30.4 %collective-permute-done.5.refs_4_.refs_5_ = bf16[192,2432]{1,0:T(8,128)(2,1)S(1)} collective-permute-done((bf16[192,2432]{1,0:T(8,128)(2,1)S(1)}, bf16[192,2432]{1,0:T(8,128)(2,1)S(1)}, u32[]{:S(2)}, u32[]{:S(2)}) %collective-permute-start.5) | collective-permute-done | bytes 933920 | tf_op jit(solution)/shard_map/ppermute | solution.py:630
  99.4 1.9 fusion.9
  101.3 1.9 pad_maximum_fusion.1
  104.4 3.2 maximum_select_fusion.1.refs_2_.dy_any
  107.6 10.5 %project.1 = (bf16[1024,768]{1,0:T(8,128)(2,1)}, bf16[1024,768]{1,0:T(8,128)(2,1)}, bf16[1024,768]{1,0:T(8,128)(2,1)}, bf16[1024,768]{1,0:T(8,128)(2,1)}, f32[8,768]{1,0:T(8,128)}) custom-call(bf16[1024,768]{1,0:T(8,128)(2,1)} %maximum_select_fusion.refs_0_, f32[1024,128]{1,0:T(8,128)} %get-tuple-element.134.refs_1_.cos_ref, ...), custom_call_target="tpu_custom_call" | custom-call | flops 3623878656 | bytes 11403264 | tf_op jit(solution)/shard_map/project/pallas_call | solution.py:119
  118.1 14.2 %attend.1 = (bf16[1024,768]{1,0:T(8,128)(2,1)}, f32[8,6,256]{2,1,0:T(8,128)}) custom-call(s32[8]{0:T(128)} %and_select_fusion.first_ref, bf16[1024,768]{1,0:T(8,128)(2,1)} %get-tuple-element.30.q_ref, bf16[1024,768]{1,0:T(8,128)(2,1)} %get-tuple-element.31.k_ref, bf16[1024,768]{1,0:T(8,128)(2,1)} %get-tuple-element.32.v_ref, s32[1,1024]{1,0:T(1,128)} %bitcast.57), custom_call_target="tpu_custom_call" | custom-call | flops 3221225472 | bytes 7864320 | tf_op jit(solution)/shard_map/attend/pallas_call | solution.py:204
  132.3 34.6 %feed.1 = (bf16[1024,768]{1,0:T(8,128)(2,1)}, bf16[1024,768]{1,0:T(8,128)(2,1)}, bf16[1024,2048]{1,0:T(8,128)(2,1)}, bf16[1024,2048]{1,0:T(8,128)(2,1)}, bf16[10...) custom-call(bf16[1024,768]{1,0:T(8,128)(2,1)} %maximum_select_fusion.refs_0_, ...), custom_call_target="tpu_custom_call" | custom-call | flops 21743271936 | bytes 28311552 | tf_op jit(solution)/shard_map/feed/pallas_call | solution.py:433
  166.9 15.9 %feed_grads.1 = bf16[16,144,2048]{2,1,0:T(8,128)(2,1)} custom-call(bf16[1024,768]{1,0:T(8,128)(2,1)} %get-tuple-element.39.n_ref, bf16[1024,2048]{1,0:T(8,128)(2,1)} %get-tuple-element.40.dgate_ref, bf16[1024,2048]{1,0:T(8,128)(2,1)} %get-tuple-element.41.dup_ref, bf16[1024,2048]{1,0:T(8,128)(2,1)} %get-tuple-element.42.hid_any, ...), custom_call_target="tpu_custom_call" | custom-call | flops 9663676416 | bytes 17301504 | tf_op jit(solution)/shard_map/feed_grads/pallas_call | solution.py:564
  182.9 23.2 %attend_back.1.refs_2_ = bf16[1024,2304]{1,0:T(8,128)(2,1)} custom-call(s32[8]{0:T(128)} %and_select_fusion.first_ref, bf16[1024,768]{1,0:T(8,128)(2,1)} %get-tuple-element.30.q_ref, bf16[1024,768]{1,0:T(8,128)(2,1)} %get-tuple-element.31.k_ref, bf16[1024,768]{1,0:T(8,128)(2,1)} %get-tuple-element.32.v_ref, bf16[1024,768]{1,0:T(8,128)(2,1)} %get-tuple-element.43.g_ref, ...), custom_call_target="tpu_custom_call" | custom-call | flops 8053063680 | bytes 12582912 | tf_op jit(solution)/shard_map/attend_back/pallas_call | solution.py:300
  206.1 10.7 %grad_in.1 = (bf16[8,48,3072]{2,1,0:T(8,128)(2,1)}, bf16[8,48,3072]{2,1,0:T(8,128)(2,1)}) custom-call(bf16[1024,768]{1,0:T(8,128)(2,1)} %get-tuple-element.45.refs_0_, bf16[1024,768]{1,0:T(8,128)(2,1)} %get-tuple-element.33.refs_1_, bf16[1024,2304]{1,0:T(8,128)(2,1)} %attend_back.1.refs_2_, bf16[1024,768]{1,0:T(8,128)(2,1)} %get-tuple-element.46.refs_3_), custom_call_target="tpu_custom_call" | custom-call | flops 4831838208 | bytes 12582912 | tf_op jit(solution)/shard_map/grad_in/pallas_call | solution.py:507
  216.8 4.7 %collective-permute-done.11 = bf16[8,48,3072]{2,1,0:T(8,128)(2,1)S(1)} collective-permute-done((bf16[8,48,3072]{2,1,0:T(8,128)(2,1)}, bf16[8,48,3072]{2,1,0:T(8,128)(2,1)S(1)}, u32[]{:S(2)}, u32[]{:S(2)}) %collective-permute-start.11) | collective-permute-done | bytes 2359328 | tf_op jit(solution)/shard_map/ppermute | solution.py:630
  221.6 2.7 add_convert_fusion
  224.3 3.0 collective-permute-start.12
  227.3 10.9 %input_grad.1 = f32[1024,768]{1,0:T(8,128)} custom-call(bf16[1024,768]{1,0:T(8,128)(2,1)} %maximum_select_fusion.refs_0_, f32[1024,768]{1,0:T(8,128)} %get-tuple-element.37.refs_1_, bf16[1024,2304]{1,0:T(8,128)(2,1)} %attend_back.1.refs_2_, f32[8,768]{1,0:T(8,128)} %get-tuple-element.35.refs_3_, bf16[192,2432]{1,0:T(8,128)(2,1)} %copy-done.1, ...), custom_call_target="tpu_custom_call" | custom-call | flops 3623878656 | bytes 16121856 | tf_op jit(solution)/shard_map/input_grad/pallas_call | solution.py:612
  238.2 1.6 dynamic-slice_convert_fusion
  241.2 2.0 collective-permute-start.9
  243.2 17.6 %collective-permute-done.12 = bf16[4,48,3072]{2,1,0:T(8,128)(2,1)S(1)} collective-permute-done((bf16[4,48,3072]{2,1,0:T(8,128)(2,1)}, bf16[4,48,3072]{2,1,0:T(8,128)(2,1)S(1)}, u32[]{:S(2)}, u32[]{:S(2)}) %collective-permute-start.12) | collective-permute-done | bytes 1179680 | tf_op jit(solution)/shard_map/ppermute | solution.py:630
  262.2 2.0 collective-permute-start.15
  265.1 11.2 %collective-permute-done.9 = bf16[512,768]{1,0:T(8,128)(2,1)S(1)} collective-permute-done((bf16[512,768]{1,0:T(8,128)(2,1)S(1)}, bf16[512,768]{1,0:T(8,128)(2,1)S(1)}, u32[]{:S(2)}, u32[]{:S(2)}) %collective-permute-start.9) | collective-permute-done | bytes 786464 | tf_op jit(solution)/shard_map/ppermute | solution.py:634
  276.6 1.8 collective-permute-done.15
  278.4 28.4 %collective-permute-done.14 = bf16[48,3072]{1,0:T(8,128)(2,1)S(1)} collective-permute-done((bf16[48,3072]{1,0:T(8,128)(2,1)S(1)}, bf16[48,3072]{1,0:T(8,128)(2,1)S(1)}, u32[]{:S(2)}, u32[]{:S(2)}) %collective-permute-start.14) | collective-permute-done | bytes 294944 | tf_op jit(solution)/shard_map/ppermute | solution.py:630
  309.8 1.9 maximum_bitcast_fusion
  311.7 2.4 collective-permute-done.16
  314.2 1.5 collective-permute-start.17
  317.3 9.2 %collective-permute-done.17 = bf16[144,2048]{1,0:T(8,128)(2,1)S(1)} collective-permute-done((bf16[144,2048]{1,0:T(8,128)(2,1)}, bf16[144,2048]{1,0:T(8,128)(2,1)S(1)}, u32[]{:S(2)}, u32[]{:S(2)}) %collective-permute-start.17) | collective-permute-done | bytes 589856 | tf_op jit(solution)/shard_map/ppermute | solution.py:634
  (109 shorter events, 25.1 us)
Async XLA Ops:
  7.2 8.2 %copy-start.10 = (bf16[48,768]{1,0:T(8,128)(2,1)S(1)}, bf16[48,768]{1,0:T(8,128)(2,1)}, u32[]{:S(2)}) copy-start(bf16[48,768]{1,0:T(8,128)(2,1)} %param.17) | copy-start | bytes 221188
  7.2 8.2 %copy-start.12 = (bf16[48,768]{1,0:T(8,128)(2,1)S(1)}, bf16[48,768]{1,0:T(8,128)(2,1)}, u32[]{:S(2)}) copy-start(bf16[48,768]{1,0:T(8,128)(2,1)} %param.16) | copy-start | bytes 221188
  7.2 14.6 %copy-start.4 = (bf16[2,1,512,768]{3,2,1,0:T(8,128)(2,1)S(1)}, bf16[2,1,512,768]{3,2,1,0:T(8,128)(2,1)}, u32[]{:S(2)}) copy-start(bf16[2,1,512,768]{3,2,1,0:T(8,128)(2,1)} %param.12) | copy-start | bytes 4718596
  7.2 125.0 %all-gather.2.cloned.1.call-start = ((), (), s32[]{:S(2)}) async-start(), calls=%async_computation.1 | async-start | bytes 11280384 | tf_op jit(solution)/shard_map/all_gather | solution.py:740
  15.2 298.9 %reduce-scatter.2.cloned.1.call-start = ((), (), s32[]{:S(2)}) async-start(), calls=%async_computation.2 | async-start | bytes 10027008 | tf_op jit(solution)/shard_map/reduce_scatter | solution.py:795
  16.2 12.1 %collective-permute-start.4 = (bf16[48,2432]{1,0:T(8,128)(2,1)}, bf16[48,2432]{1,0:T(8,128)(2,1)}, u32[]{:S(2)}, u32[]{:S(2)}) collective-permute-start(bf16[48,2432]{1,0:T(8,128)(2,1)} %pad_maximum_fusion.3), channel_id=1, source_target_pairs={{0,12},{1,13},{2,14},{3,15},{4,8},{5,9},{6,10},{7,11},{8,4},{9,5},... | collective-permute-start | bytes 700424 | tf_op jit(solution)/shard_map/ppermute | solution.py:630
  21.2 40.8 %collective-permute-start.3 = (bf16[48,2432]{1,0:T(8,128)(2,1)}, bf16[48,2432]{1,0:T(8,128)(2,1)}, u32[]{:S(2)}, u32[]{:S(2)}) collective-permute-start(bf16[48,2432]{1,0:T(8,128)(2,1)} %pad_maximum_fusion.3), channel_id=1, source_target_pairs={{0,8},{1,9},{2,10},{3,11},{4,12},{5,13},{6,14},{7,15},{8,0},{9,1},... | collective-permute-start | bytes 700424 | tf_op jit(solution)/shard_map/ppermute | solution.py:630
  21.3 40.8 %collective-permute-start.2 = (bf16[48,2432]{1,0:T(8,128)(2,1)}, bf16[48,2432]{1,0:T(8,128)(2,1)}, u32[]{:S(2)}, u32[]{:S(2)}) collective-permute-start(bf16[48,2432]{1,0:T(8,128)(2,1)} %pad_maximum_fusion.3), channel_id=1, source_target_pairs={{0,4},{1,5},{2,6},{3,7},{4,0},{5,1},{6,2},{7,3},{8,12},{9,13},{10,... | collective-permute-start | bytes 700424 | tf_op jit(solution)/shard_map/ppermute | solution.py:630
  21.8 40.2 %copy-start.13 = (bf16[48,768]{1,0:T(8,128)(2,1)S(1)}, bf16[48,768]{1,0:T(8,128)(2,1)}, u32[]{:S(2)}) copy-start(bf16[48,768]{1,0:T(8,128)(2,1)} %param.16) | copy-start | bytes 221188
  21.8 40.2 %copy-start.16 = (bf16[48,768]{1,0:T(8,128)(2,1)S(1)}, bf16[48,768]{1,0:T(8,128)(2,1)}, u32[]{:S(2)}) copy-start(bf16[48,768]{1,0:T(8,128)(2,1)} %param.15) | copy-start | bytes 221188
  22.8 42.1 %copy-start.20 = (s32[2,1,512]{2,1,0:T(1,128)S(1)}, s32[2,1,512]{2,1,0:T(1,128)}, u32[]{:S(2)}) copy-start(s32[2,1,512]{2,1,0:T(1,128)} %param.13) | copy-start | bytes 12292
  22.8 43.7 %collective-permute-start = (bf16[512,768]{1,0:T(8,128)(2,1)}, bf16[512,768]{1,0:T(8,128)(2,1)S(1)}, u32[]{:S(2)}, u32[]{:S(2)}) collective-permute-start(bf16[512,768]{1,0:T(8,128)(2,1)} %get-tuple-element.118), channel_id=1, source_target_pairs={{0,16},{16,0},{1,17},{17,1},{2,18},{18,2},{3,19},{19,3},{4,20},{20... | collective-permute-start | bytes 2359304 | tf_op jit(solution)/shard_map/ppermute | solution.py:634
  63.3 36.1 %collective-permute-start.5 = (bf16[192,2432]{1,0:T(8,128)(2,1)S(1)}, bf16[192,2432]{1,0:T(8,128)(2,1)S(1)}, u32[]{:S(2)}, u32[]{:S(2)}) collective-permute-start(bf16[192,2432]{1,0:T(8,128)(2,1)S(1)} %pad_maximum_fusion.refs_3_.refs_4_), channel_id=1, source_target_pairs={{0,2},{1,3},{2,0},{3,1},{4,6},{5,7},{6,4},{7,5},{8,10},{9,11},{10,... | collective-permute-start | bytes 2801672 | tf_op jit(solution)/shard_map/ppermute | solution.py:630
  64.9 38.3 %collective-permute-start.1 = (s32[512]{0:T(512)S(1)}, s32[512]{0:T(512)S(1)}, u32[]{:S(2)}, u32[]{:S(2)}) collective-permute-start(s32[512]{0:T(512)S(1)} %bitcast.59), channel_id=1, source_target_pairs={{0,16},{16,0},{1,17},{17,1},{2,18},{18,2},{3,19},{19,3},{4,20},{20... | collective-permute-start | bytes 6152 | tf_op jit(solution)/shard_map/ppermute | solution.py:634
  66.4 41.2 %collective-permute-start.6 = (bf16[192,2432]{1,0:T(8,128)(2,1)S(1)}, bf16[192,2432]{1,0:T(8,128)(2,1)}, u32[]{:S(2)}, u32[]{:S(2)}) collective-permute-start(bf16[192,2432]{1,0:T(8,128)(2,1)S(1)} %pad_maximum_fusion.refs_3_.refs_4_), channel_id=1, source_target_pairs={{0,1},{1,0},{2,3},{3,2},{4,5},{5,4},{6,7},{7,6},{8,9},{9,8},{10,11... | collective-permute-start | bytes 2801672 | tf_op jit(solution)/shard_map/ppermute | solution.py:630
  68.4 36.0 %collective-permute-start.8 = (bf16[512,768]{1,0:T(8,128)(2,1)S(1)}, bf16[512,768]{1,0:T(8,128)(2,1)}, u32[]{:S(2)}, u32[]{:S(2)}) collective-permute-start(bf16[512,768]{1,0:T(8,128)(2,1)S(1)} %get-tuple-element.116), channel_id=1, source_target_pairs={{0,16},{16,0},{1,17},{17,1},{2,18},{18,2},{3,19},{19,3},{4,20},{20... | collective-permute-start | bytes 2359304 | tf_op jit(solution)/shard_map/ppermute | solution.py:634
  99.4 8.2 %collective-permute-start.7 = (bf16[192,2432]{1,0:T(8,128)(2,1)S(1)}, bf16[192,2432]{1,0:T(8,128)(2,1)}, u32[]{:S(2)}, u32[]{:S(2)}) collective-permute-start(bf16[192,2432]{1,0:T(8,128)(2,1)S(1)} %collective-permute-done.5.refs_4_.refs_5_), channel_id=1, source_target_pairs={{0,1},{1,0},{2,3},{3,2},{4,5},{5,4},{6,7},{7,6},{8,9},{9,8},{10,11... | collective-permute-start | bytes 2801672 | tf_op jit(solution)/shard_map/ppermute | solution.py:630
  216.8 4.7 %collective-permute-start.11 = (bf16[8,48,3072]{2,1,0:T(8,128)(2,1)}, bf16[8,48,3072]{2,1,0:T(8,128)(2,1)S(1)}, u32[]{:S(2)}, u32[]{:S(2)}) collective-permute-start(bf16[8,48,3072]{2,1,0:T(8,128)(2,1)} %get-tuple-element.48), channel_id=1, source_target_pairs={{0,1},{1,0},{2,3},{3,2},{4,5},{5,4},{6,7},{7,6},{8,9},{9,8},{10,11... | collective-permute-start | bytes 7077896 | tf_op jit(solution)/shard_map/ppermute | solution.py:630
  224.3 36.5 %collective-permute-start.12 = (bf16[4,48,3072]{2,1,0:T(8,128)(2,1)}, bf16[4,48,3072]{2,1,0:T(8,128)(2,1)S(1)}, u32[]{:S(2)}, u32[]{:S(2)}) collective-permute-start(bf16[4,48,3072]{2,1,0:T(8,128)(2,1)} %add_convert_fusion), channel_id=1, source_target_pairs={{0,2},{1,3},{2,0},{3,1},{4,6},{5,7},{6,4},{7,5},{8,10},{9,11},{10,... | collective-permute-start | bytes 3538952 | tf_op jit(solution)/shard_map/ppermute | solution.py:630
  238.2 22.7 %copy-start.2 = (bf16[8,48,3072]{2,1,0:T(8,128)(2,1)S(1)}, bf16[8,48,3072]{2,1,0:T(8,128)(2,1)}, u32[]{:S(2)}) copy-start(bf16[8,48,3072]{2,1,0:T(8,128)(2,1)} %get-tuple-element.47) | copy-start | bytes 7077892
  239.8 25.0 %collective-permute-start.10 = (bf16[512,768]{1,0:T(8,128)(2,1)S(1)}, bf16[512,768]{1,0:T(8,128)(2,1)S(1)}, u32[]{:S(2)}, u32[]{:S(2)}) collective-permute-start(bf16[512,768]{1,0:T(8,128)(2,1)S(1)} %dynamic-slice_convert_fusion), channel_id=1, source_target_pairs={{0,16},{16,0},{1,17},{17,1},{2,18},{18,2},{3,19},{19,3},{4,20},{20... | collective-permute-start | bytes 2359304 | tf_op jit(solution)/shard_map/ppermute | solution.py:634
  241.1 23.7 %copy-start = (f32[1024,768]{1,0:T(8,128)S(1)}, f32[1024,768]{1,0:T(8,128)}, u32[]{:S(2)}) copy-start(f32[1024,768]{1,0:T(8,128)} %input_grad.1) | copy-start | bytes 9437188
  241.2 35.1 %collective-permute-start.9 = (bf16[512,768]{1,0:T(8,128)(2,1)S(1)}, bf16[512,768]{1,0:T(8,128)(2,1)S(1)}, u32[]{:S(2)}, u32[]{:S(2)}) collective-permute-start(bf16[512,768]{1,0:T(8,128)(2,1)S(1)} %constant_dynamic-slice_fusion), channel_id=1, source_target_pairs={{0,16},{16,0},{1,17},{17,1},{2,18},{18,2},{3,19},{19,3},{4,20},{20... | collective-permute-start | bytes 2359304 | tf_op jit(solution)/shard_map/ppermute | solution.py:634
  261.3 15.3 %collective-permute-start.13 = (bf16[48,3072]{1,0:T(8,128)(2,1)S(1)}, bf16[48,3072]{1,0:T(8,128)(2,1)S(1)}, u32[]{:S(2)}, u32[]{:S(2)}) collective-permute-start(bf16[48,3072]{1,0:T(8,128)(2,1)S(1)} %get-tuple-element.108), channel_id=1, source_target_pairs={{0,4},{1,5},{2,6},{3,7},{4,0},{5,1},{6,2},{7,3},{8,12},{9,13},{10,... | collective-permute-start | bytes 884744 | tf_op jit(solution)/shard_map/ppermute | solution.py:630
  262.2 16.2 %collective-permute-start.15 = (bf16[48,3072]{1,0:T(8,128)(2,1)S(1)}, bf16[48,3072]{1,0:T(8,128)(2,1)S(1)}, u32[]{:S(2)}, u32[]{:S(2)}) collective-permute-start(bf16[48,3072]{1,0:T(8,128)(2,1)S(1)} %get-tuple-element.109), channel_id=1, source_target_pairs={{0,12},{1,13},{2,14},{3,15},{4,8},{5,9},{6,10},{7,11},{8,4},{9,5},... | collective-permute-start | bytes 884744 | tf_op jit(solution)/shard_map/ppermute | solution.py:630
  264.2 12.1 %copy-start.6 = (bf16[1024,768]{1,0:T(8,128)(2,1)S(1)}, bf16[1024,768]{1,0:T(8,128)(2,1)}, u32[]{:S(2)}) copy-start(bf16[1024,768]{1,0:T(8,128)(2,1)} %get-tuple-element.36) | copy-start | bytes 4718596
  264.2 42.6 %collective-permute-start.14 = (bf16[48,3072]{1,0:T(8,128)(2,1)S(1)}, bf16[48,3072]{1,0:T(8,128)(2,1)S(1)}, u32[]{:S(2)}, u32[]{:S(2)}) collective-permute-start(bf16[48,3072]{1,0:T(8,128)(2,1)S(1)} %get-tuple-element.110), channel_id=1, source_target_pairs={{0,8},{1,9},{2,10},{3,11},{4,12},{5,13},{6,14},{7,15},{8,0},{9,1},... | collective-permute-start | bytes 884744 | tf_op jit(solution)/shard_map/ppermute | solution.py:630
  307.1 7.0 %collective-permute-start.16 = (bf16[48,3072]{1,0:T(8,128)(2,1)S(1)}, bf16[48,3072]{1,0:T(8,128)(2,1)S(1)}, u32[]{:S(2)}, u32[]{:S(2)}) collective-permute-start(bf16[48,3072]{1,0:T(8,128)(2,1)S(1)} %fusion.4), channel_id=1, source_target_pairs={{0,16},{16,0},{1,17},{17,1},{2,18},{18,2},{3,19},{19,3},{4,20},{20... | collective-permute-start | bytes 884744 | tf_op jit(solution)/shard_map/ppermute | solution.py:634
  314.2 12.3 %copy-start.18 = (bf16[144,2048]{1,0:T(8,128)(2,1)S(1)}, bf16[144,2048]{1,0:T(8,128)(2,1)}, u32[]{:S(2)}) copy-start(bf16[144,2048]{1,0:T(8,128)(2,1)} %reduce-scatter.2.cloned.1.call-done) | copy-start | bytes 1769476
  314.2 12.3 %collective-permute-start.17 = (bf16[144,2048]{1,0:T(8,128)(2,1)}, bf16[144,2048]{1,0:T(8,128)(2,1)S(1)}, u32[]{:S(2)}, u32[]{:S(2)}) collective-permute-start(bf16[144,2048]{1,0:T(8,128)(2,1)} %reduce-scatter.2.cloned.1.call-done), channel_id=1, source_target_pairs={{0,16},{16,0},{1,17},{17,1},{2,18},{18,2},{3,19},{19,3},{4,20},{20... | collective-permute-start | bytes 1769480 | tf_op jit(solution)/shard_map/ppermute | solution.py:634
  316.4 10.2 %copy-start.3 = (bf16[48,2048]{1,0:T(8,128)(2,1)S(1)}, bf16[48,2048]{1,0:T(8,128)(2,1)}, u32[]{:S(2)}) copy-start(bf16[48,2048]{1,0:T(8,128)(2,1)} %param.20) | copy-start | bytes 589828
  316.4 10.2 %copy-start.7 = (bf16[48,2048]{1,0:T(8,128)(2,1)S(1)}, bf16[48,2048]{1,0:T(8,128)(2,1)}, u32[]{:S(2)}) copy-start(bf16[48,2048]{1,0:T(8,128)(2,1)} %param.19) | copy-start | bytes 589828
  (11 other events, 57.6 us)
Sparse Core Ops, SparseCore 0:
  15.4 112.4 all-gather.1
  183.0 127.6 reduce-scatter.1

commit v3 on v2

--- a/solution.py
+++ b/solution.py
@@ -56,14 +56,22 @@
 def load_copies(groups, scratch, sem):
     if len(groups) == 1:
         return [pltpu.make_async_copy(groups[0][0], scratch, sem)]
-    rows = scratch.shape[0] // sum(len(places) for _, places in groups)
-    me = lax.axis_index("fsdp")
+    me, rank = lax.axis_index("fsdp"), lax.axis_index("seq")
+    rows = 2 * scratch.shape[0] // sum(len(places) for _, places, _ in groups)
+    half = scratch.shape[1] // 2
     copies = []
-    for piece, places in groups:
+    for piece, places, side in groups:
+        columns = pl.ds(pl.multiple_of(lax.bitwise_xor(rank, side) * half, 128), half)
         for at, place in enumerate(places):
             target = pl.ds(pl.multiple_of(lax.bitwise_xor(me, place) * rows, 16), rows)
-            copies.append(pltpu.make_async_copy(piece.at[pl.ds(at * rows, rows), :], scratch.at[target, :], sem))
+            copies.append(
+                pltpu.make_async_copy(piece.at[pl.ds(at * rows, rows), :], scratch.at[target, columns], sem)
+            )
     return copies
+
+
+def columns_of(groups):
+    return groups[0][0].shape[1] * (1 if len(groups) == 1 else 2)
 
 
 def start_all(copies):
@@ -83,7 +91,7 @@
 def project_kernel(places, width, *refs):
     x_ref, cos_ref, sin_ref = refs[:3]
     count = len(places)
-    groups = list(zip(refs[3 : 3 + count], places))
+    groups = [(piece, *place) for piece, place in zip(refs[3 : 3 + count], places)]
     n_ref, q_ref, k_ref, v_ref, gains_ref = refs[3 + count : 8 + count]
     weights, gain, sem = refs[8 + count :]
 
@@ -112,12 +120,12 @@
 
 def project(x, cosine, sine, groups):
     tokens, width = x.shape
-    total = groups[0][0].shape[1]
+    total = columns_of(groups)
     shape = jax.ShapeDtypeStruct((tokens, width), BF)
     block = pl.BlockSpec((TBLOCK, width), lambda i: (i, 0))
     table = pl.BlockSpec((TBLOCK, PAIR), lambda i: (i, 0))
     return pl.pallas_call(
-        functools.partial(project_kernel, [places for _, places in groups], width),
+        functools.partial(project_kernel, [place for _, *place in groups], width),
         name="project",
         out_shape=[shape] * 4 + [jax.ShapeDtypeStruct((8, width), F32)],
         grid=(tokens // TBLOCK,),
@@ -129,7 +137,7 @@
             pltpu.SemaphoreType.DMA,
         ],
         cost_estimate=cost(6 * tokens * width * width, 6 * width * width + 10 * tokens * width),
-    )(x, cosine, sine, *[piece for piece, _ in groups])
+    )(x, cosine, sine, *[piece for piece, *_ in groups])
 
 
 def split_heads(values):
@@ -363,7 +371,7 @@
     x_ref, att_ref, dy_ref, gain_ref = refs[:4]
     given, refs = refs[4 : 4 + count], refs[4 + count :]
     y_ref, n_ref, hid_ref, dgate_ref, dup_ref, dm_ref, dmr_ref, datt_ref = refs[:8]
-    w_out, w_both, w_down, sems = refs[8:]
+    w_out, w_both, w_down, result, back, sems = refs[8:]
     targets = (w_out, w_both, w_down)
     parts = width // rows
 
@@ -378,29 +386,42 @@
 
         lax.fori_loop(0, parts, step, 0)
 
-    @pl.when(pl.program_id(0) == 0)
+    opening = pl.program_id(0) == 0
+
+    @pl.when(opening)
     def _():
         if count > 1:
             copies = whole_copies()
             start_all(copies)
             wait_all(copies)
         else:
-            per_owner(lambda copies: start_all(copies["out"] + copies["both"] + copies["down"]))
-            per_owner(lambda copies: wait_all(copies["out"] + copies["both"] + copies["down"]))
-
+            per_owner(lambda copies: start_all(copies["out"]))
+            per_owner(lambda copies: start_all(copies["both"] + copies["down"]))
+
+    def wait_for(*kinds):
+        if count == 1:
+
+            @pl.when(opening)
+            def _():
+                per_owner(lambda copies: wait_all([copy for kind in kinds for copy in copies[kind]]))
+
+    wait_for("out")
     gain = gain_ref[1:2, :]
     dy = dy_ref[...]
     middle = x_ref[...].astype(F32) + dot_nn(att_ref[...], w_out[...])
     inverse = lax.rsqrt(jnp.mean(middle * middle, axis=1, keepdims=True) + EPSILON)
     normed = (middle * inverse * gain).astype(BF)
     n_ref[...] = normed
-    result = middle
-    back = jnp.zeros_like(middle)
+    wait_for("both", "down")
+    result[...] = middle
+    back[...] = jnp.zeros_like(middle)
     step = min(FSTEP, hidden_width)
-    for at in range(0, hidden_width, step):
-        part = slice(at, at + step)
-        w_gate = w_both[:, at : at + step]
-        w_up = w_both[:, hidden_width + at : hidden_width + at + step]
+
+    def chunk(number, carry):
+        at = pl.multiple_of(number * step, step)
+        part = pl.ds(at, step)
+        w_gate = w_both[:, part]
+        w_up = w_both[:, pl.ds(pl.multiple_of(hidden_width + at, step), step)]
         gate = dot_nn(normed, w_gate)
         up = dot_nn(normed, w_up)
         dh = dot_nt(dy, w_down[part, :])
@@ -412,10 +433,13 @@
         dup = (dh * silu).astype(BF)
         dgate_ref[:, part] = dgate
         dup_ref[:, part] = dup
-        result = result + dot_nn(hidden, w_down[part, :])
-        back = back + dot_nt(dgate, w_gate) + dot_nt(dup, w_up)
-    y_ref[...] = result.astype(BF)
-    scaled = back * gain
+        result[...] += dot_nn(hidden, w_down[part, :])
+        back[...] += dot_nt(dgate, w_gate) + dot_nt(dup, w_up)
+        return carry
+
+    lax.fori_loop(0, hidden_width // step, chunk, 0)
+    y_ref[...] = result[...].astype(BF)
+    scaled = back[...] * gain
     dm = dy.astype(F32) + inverse * scaled - middle * (inverse * inverse * inverse) * jnp.mean(
         scaled * middle, axis=1, keepdims=True
     )
@@ -441,6 +465,8 @@
             pltpu.VMEM((width, width), BF),
             pltpu.VMEM((width, 2 * hidden_width), BF),
             pltpu.VMEM((hidden_width, width), BF),
+            pltpu.VMEM((FBLOCK, width), F32),
+            pltpu.VMEM((FBLOCK, width), F32),
             pltpu.SemaphoreType.DMA((3,)),
         ],
         cost_estimate=cost(4 * tokens * width * (width + 3 * hidden_width), 20 * tokens * width + 6 * tokens * hidden_width),
@@ -587,7 +613,7 @@
 def input_grad_kernel(places, width, *refs):
     count = len(places)
     x_ref, dm_ref, grads_ref, gains_ref = refs[:4]
-    groups = list(zip(refs[4 : 4 + count], places))
+    groups = [(piece, *place) for piece, place in zip(refs[4 : 4 + count], places)]
     out_ref, weights, sem = refs[4 + count :]
 
     @pl.when(pl.program_id(0) == 0)
@@ -610,7 +636,7 @@
     tokens, width = x.shape
     block = pl.BlockSpec((TBLOCK, width), lambda i: (i, 0))
     return pl.pallas_call(
-        functools.partial(input_grad_kernel, [places for _, places in groups], width),
+        functools.partial(input_grad_kernel, [place for _, *place in groups], width),
         name="input_grad",
         out_shape=jax.ShapeDtypeStruct((tokens, width), F32),
         grid=(tokens // TBLOCK,),
@@ -618,11 +644,11 @@
         + [ANY] * len(groups),
         out_specs=block,
         scratch_shapes=[
-            pltpu.VMEM((width, groups[0][0].shape[1]), BF),
+            pltpu.VMEM((width, columns_of(groups)), BF),
             pltpu.SemaphoreType.DMA,
         ],
         cost_estimate=cost(6 * tokens * width * width, 6 * width * width + 16 * tokens * width),
-    )(x, dm, grads, gains, *[piece for piece, _ in groups])
+    )(x, dm, grads, gains, *[piece for piece, *_ in groups])
 
 
 def flip(values, bits):
@@ -650,74 +676,122 @@
 
 def gather_rows(shard, parts):
     if parts == 1:
-        return [(lax.all_gather(shard, "fsdp", axis=0, tiled=True), (0,))]
+        return [(lax.all_gather(shard, "fsdp", axis=0, tiled=True), (0,), 0)]
     uppers = tuple(range(0, parts, 4))
     mine = jnp.concatenate([shard] + [flip(shard, upper) for upper in uppers[1:]])
     beside = flip(mine, 2)
-    groups = [(mine, 0), (beside, 2), (flip(mine, 1), 1), (flip(beside, 1), 3)]
-    return [(piece, tuple(upper + low for upper in uppers)) for piece, low in groups]
-
-
-def pack(w_out, w_gate, w_up, w_down):
+    got = [(mine, 0, 0), (beside, 2, 0), (across(mine), 0, 1), (across(beside), 2, 1)]
+    got += [(flip(piece, 1), low + 1, side) for piece, low, side in got]
+    return [(piece, tuple(upper + low for upper in uppers), side) for piece, low, side in got]
+
+
+def pack_kernel(q_ref, k_ref, v_ref, column_ref, out_ref, gate_ref, up_ref, down_ref, in_ref, packed_ref):
+    rows, width = out_ref.shape
+    hidden_width = gate_ref.shape[1]
+    half = in_ref.shape[1]
+    for rank in range(2):
+
+        @pl.when(lax.axis_index("seq") == rank)
+        def _(rank=rank):
+            left = 0
+            for piece in (q_ref, k_ref, v_ref, column_ref):
+                start, stop = max(left, rank * half), min(left + piece.shape[1], (rank + 1) * half)
+                if start < stop:
+                    in_ref[:, start - rank * half : stop - rank * half] = piece[:, start - left : stop - left]
+                left += piece.shape[1]
+
+    slices, _ = packed_slices(rows, down_ref.shape[0], width, hidden_width)
+    for name, (low, high), (left, right), top, column in slices:
+        spans = {
+            "down": [(down_ref, left, right, 0)],
+            "out": [(out_ref, left, right, 0)],
+            "both": [
+                (gate_ref, left, min(right, hidden_width), 0),
+                (up_ref, max(left, hidden_width), right, hidden_width),
+            ],
+        }[name]
+        for array, start, stop, base in spans:
+            if start < stop:
+                packed_ref[top : top + high - low, column + start - left : column + stop - left] = array[
+                    low:high, start - base : stop - base
+                ]
+
+
+def pack(w_query, w_key, w_value, column, w_out, w_gate, w_up, w_down):
     rows, width = w_out.shape
-    sources = {"down": w_down, "out": w_out, "both": jnp.concatenate([w_gate, w_up], axis=1)}
-    slices, _ = packed_slices(rows, w_down.shape[0], width, w_gate.shape[1])
-    strips, line, filled = [], [], 0
-    for name, (low, high), (left, right), _, _ in slices:
-        line.append(sources[name][low:high, left:right])
-        filled += right - left
-        if filled == width:
-            strips.append(line[0] if len(line) == 1 else jnp.concatenate(line, axis=1))
-            line, filled = [], 0
-    return jnp.concatenate(strips)
+    _, height = packed_slices(rows, w_down.shape[0], width, w_gate.shape[1])
+    given = (w_query, w_key, w_value, column, w_out, w_gate, w_up, w_down)
+    return pl.pallas_call(
+        pack_kernel,
+        name="pack",
+        out_shape=[
+            jax.ShapeDtypeStruct((rows, (3 * width + column.shape[1]) // 2), BF),
+            jax.ShapeDtypeStruct((height, width), BF),
+        ],
+    )(*given)
 
 
 class Scatter:
-    def __init__(self, outs, parts):
-        self.parts = parts
+    def __init__(self, outs, parts, rank):
+        self.parts, self.rank = parts, rank
         if parts == 1:
             self.total = lax.psum_scatter(outs[0], "fsdp", scatter_dimension=0, tiled=True)
             return
         self.keep, send = outs
         self.got = flip(send, 1)
+        self.half = self.keep.shape[2] // 2
+
+    def columns(self, side, rows):
+        at = lax.bitwise_xor(self.rank, side) * self.half
+        kept, got = [lax.dynamic_slice_in_dim(array, at, self.half, 2)[rows] for array in (self.keep, self.got)]
+        return kept.astype(F32) + got.astype(F32)
+
+    def x_hop(self):
+        if self.parts == 1:
+            return []
+        aside = self.columns(1, slice(None)).astype(BF)
+        self.aside = across(aside)
+        return [aside]
 
     def y_hop(self):
         if self.parts == 1:
             return []
-        upper = self.parts // 4
-        ahead = (self.keep[upper:].astype(F32) + self.got[upper:].astype(F32)).astype(BF)
+        upper = slice(self.parts // 4, None)
+        ahead = (self.columns(0, upper) + self.aside[upper].astype(F32)).astype(BF)
         self.ahead = flip(ahead, 2)
         return [ahead]
 
     def z_hop(self):
         if self.parts == 1:
             return []
-        sums = [
-            self.keep[j].astype(F32) + self.got[j].astype(F32) + self.ahead[j].astype(F32)
-            for j in range(self.parts // 4)
-        ]
+        lower = slice(0, self.parts // 4)
+        sums = self.columns(0, lower) + self.aside[lower].astype(F32) + self.ahead.astype(F32)
         self.own, sends = sums[0], [total.astype(BF) for total in sums[1:]]
         self.others = [flip(send, 4 * (j + 1)) for j, send in enumerate(sends)]
         return sends
 
-    def x_hop(self):
-        if self.parts > 1:
-            total = self.own
-            for piece in self.others:
-                total = total + piece.astype(F32)
-            self.total = total.astype(BF)
-        self.partner = across(self.total)
-        return [self.total]
-
     def result(self):
-        return self.total.astype(F32) + self.partner.astype(F32)
+        if self.parts == 1:
+            return self.total.astype(F32) + across(self.total).astype(F32)
+        total = self.own
+        for piece in self.others:
+            total = total + piece.astype(F32)
+        total = total.astype(BF)
+        partner = across(total)
+        first = jnp.where(self.rank == 0, total, partner)
+        second = jnp.where(self.rank == 0, partner, total)
+        return jnp.concatenate([first, second], axis=1).astype(F32)
 
 
 def rope_tables(length):
     half = HEAD_DIM // 2
     inverse = jnp.exp(jnp.arange(half, dtype=F32) * (-2.0 * math.log(10000.0) / HEAD_DIM))
-    angles = jnp.arange(length, dtype=jnp.int32).astype(F32)[:, None] * inverse[None, :]
-    cosine, sine = jnp.cos(angles), jnp.sin(angles)
+    low = jnp.arange(32, dtype=jnp.int32).astype(F32)[:, None] * inverse[None, :]
+    high = (jnp.arange(length // 32, dtype=jnp.int32) * 32).astype(F32)[:, None] * inverse[None, :]
+    cos_low, sin_low = jnp.cos(low)[None], jnp.sin(low)[None]
+    cos_high, sin_high = jnp.cos(high)[:, None], jnp.sin(high)[:, None]
+    cosine = (cos_high * cos_low - sin_high * sin_low).reshape(length, half)
+    sine = (sin_high * cos_low + cos_high * sin_low).reshape(length, half)
     return (
         jnp.concatenate([cosine] * 4, axis=1),
         jnp.concatenate([-sine, sine, -sine, sine], axis=1),
@@ -734,10 +808,13 @@
     rows = w_query.shape[0]
     parts = count if aligned(rows, w_down.shape[0], width, hidden_width, count) else 1
 
+    column = jnp.pad(jnp.stack([gain_attn, gain_ffn], axis=1), ((0, 0), (0, 254)))
     if parts == 1:
+        w_in = jnp.concatenate([w_query, w_key, w_value, column], axis=1)
         given = [lax.all_gather(weight, "fsdp", axis=0, tiled=True) for weight in (w_out, w_gate, w_up, w_down)]
     else:
-        given = [lax.all_gather(pack(w_out, w_gate, w_up, w_down), "fsdp", axis=0, tiled=True)]
+        w_in, packed = pack(w_query, w_key, w_value, column, w_out, w_gate, w_up, w_down)
+        given = [lax.all_gather(packed, "fsdp", axis=0, tiled=True)]
 
     def exchanged(array):
         own = lax.dynamic_index_in_dim(array, seq_rank, 0, keepdims=False)[0]
@@ -755,14 +832,12 @@
         first, second = jnp.where(seq_rank == 0, own, other), jnp.where(seq_rank == 0, other, own)
         return jnp.stack([first, second])[:, None]
 
-    column = jnp.pad(jnp.stack([gain_attn, gain_ffn], axis=1), ((0, 0), (0, 126)))
-    w_in = jnp.concatenate([w_query, w_key, w_value, column], axis=1)
     groups_in = gather_rows(w_in, parts)
     own_x, other_x = exchanged(tokens)
     x = ordered(own_x, across(other_x))
     own_docs, other_docs = exchanged(doc_ids)
     docs = ordered(own_docs, across(other_docs))
-    own_dy, other_dy = exchanged(gate(cotangent, x))
+    own_dy, other_dy = exchanged(gate(cotangent, x, *[piece for piece, *_ in groups_in]))
     dy = ordered(own_dy, across(other_dy))
 
     length = x.shape[0]
@@ -795,13 +870,15 @@
         ff = lax.psum_scatter(ff.reshape(-1, hidden_width), "fsdp", scatter_dimension=0, tiled=True)
         sums = (ff,)
     grads = attend_back(queries, keys, values, datt, lse, starts, first, cosine, sine)
-    scatter = Scatter(outer_sums(parts, [([normed], grads), ([attended], dmr)], width, "grad_in"), parts)
-    grad_x = input_grad(x, dm, grads, gains, groups_in)
+    scatter = Scatter(
+        outer_sums(parts, [([normed], grads), ([attended], dmr)], width, "grad_in"), parts, seq_rank
+    )
+    sent = scatter.x_hop()
+    grad_x = input_grad(gate(x, *sent), dm, grads, gains, groups_in)
     own_g, other_g = halves(grad_x)
-    scatter.y_hop()
-    grad_tokens = give_back(own_g, across(other_g.astype(BF)).astype(F32))
+    sent = scatter.y_hop()
+    grad_tokens = give_back(own_g, across(gate(other_g.astype(BF), *sent)).astype(F32))
     scatter.z_hop()
-    scatter.x_hop()
     sum_in = scatter.result()
     sums = [part.astype(F32) + across(part).astype(F32) for part in sums]
     if parts == 1:
@@ -813,7 +890,10 @@
         sum_down = rest.transpose(2, 1, 0, 3).reshape(w_down.shape)
 
     sum_in, sum_out = sum_in[:, : 3 * width], sum_in[:, 3 * width :]
-    grad_gain_attn = jnp.sum(w_in[:, : 3 * width].astype(F32) * sum_in, axis=1) / gain_attn.astype(F32)
+    grad_gain_attn = sum(
+        jnp.sum(weight.astype(F32) * sum_in[:, at * width : (at + 1) * width], axis=1)
+        for at, weight in enumerate((w_query, w_key, w_value))
+    ) / gain_attn.astype(F32)
     grad_gain_ffn = (
         jnp.sum(w_gate.astype(F32) * sum_gate, axis=1) + jnp.sum(w_up.astype(F32) * sum_up, axis=1)
     ) / gain_ffn.astype(F32)

time: 343 us -> 312 us (0.910)
  waiting for transfers between devices: 143 us -> 113 us
  local copies, waits for them, and re-layouts: 13.4 us -> 6.01 us
  starting transfers between devices: 22.8 us -> 27.4 us
    ppermute x11 -> x13, waiting for transfers between devices: 120 us -> 35.6 us  [flip(): return lax.ppermute(values, 'fsdp', [(i, i ^ bits) for i in range(count)])]
    ppermute x7 -> x10, waiting for transfers between devices: 22.8 us -> 61.5 us  [across(): return lax.ppermute(values, 'seq', [(0, 1), (1, 0)])]
    all_gather x1, waiting for transfers between devices: 0.01 us -> 15.7 us  [per_device(): given = [lax.all_gather(packed, 'fsdp', axis=0, tiled=True)]]
    unnamed x54 -> x39, local copies, waits for them, and re-layouts: 7.27 us -> 1.05 us
    ppermute x7 -> x10, starting transfers between devices: 8.92 us -> 13.5 us  [across(): return lax.ppermute(values, 'seq', [(0, 1), (1, 0)])]
    pallas_call x2 -> x3, Pallas kernels: 21.4 us -> 24.1 us  [the longest x1 11.3 us: input_grad(): pl.pallas_call(functools.partial(input_grad_kernel, [place for _, *place...]
    ppermute x11 -> x13, starting transfers between devices: 13.8 us -> 13.8 us  [flip(): return lax.ppermute(values, 'fsdp', [(i, i ^ bits) for i in range(count)])]
  transfers between devices with their start and end apart: 20 -> 25, of which waited for: 10 -> 13; matrix products, arithmetic and copies ran while one was open for 7% -> 8% of each run, Pallas kernels for 21% -> 23%
where the time goes in v3:
time: 312 us; the launch traced here: 307 us
  Pallas kernels  122 us (39%)
  waiting for transfers between devices  113 us (36%)
  starting transfers between devices  27.4 us (9%)
  other arithmetic  24.1 us (8%)
  between operations  14.7 us (5%)
  local copies, waits for them, and re-layouts  6.01 us (2%)
    ppermute x10, waiting for transfers between devices, across(): return lax.ppermute(values, 'seq', [(0, 1), (1, 0)])  61.5 us
    ppermute x13, waiting for transfers between devices, flip(): return lax.ppermute(values, 'fsdp', [(i, i ^ bits) for i in range(count)])  35.6 us
    pallas_call x1, Pallas kernels, feed(): pl.pallas_call(functools.partial(feed_kernel, rows, len(given), width, hi...  34.7 us
    pallas_call x1, Pallas kernels, attend_back(): pl.pallas_call(functools.partial(attend_back_kernel, pairs), name='attend...  22.8 us
    pallas_call x1, Pallas kernels, feed_grads(): pl.pallas_call(functools.partial(feed_grads_kernel, parts, steps), name='...  15.7 us
    all_gather x1, waiting for transfers between devices, per_device(): given = [lax.all_gather(packed, 'fsdp', axis=0, tiled=True)]  15.7 us
    pallas_call x1, Pallas kernels, attend(): pl.pallas_call(functools.partial(attend_kernel, pairs), name='attend', ou...  14.1 us
    ppermute x13, starting transfers between devices, flip(): return lax.ppermute(values, 'fsdp', [(i, i ^ bits) for i in range(count)])  13.8 us
  transfers between devices with their start and end apart: 25, of which 13 were waited for; matrix products, arithmetic and copies ran while one was open for 8% of the time, Pallas kernels for 23%

profile of v3, /device:TPU:0, one launch (start us, length us, event | category | flops | bytes accessed | tf_op | source)
XLA Modules:
  0.0 307.3 jit_solution(15029908343082994877)
XLA Ops:
  8.8 2.2 pack.1
  11.0 3.1 %collective-permute-start.2 = (bf16[48,1280]{1,0:T(8,128)(2,1)}, bf16[48,1280]{1,0:T(8,128)(2,1)S(1)}, u32[]{:S(2)}, u32[]{:S(2)}) collective-permute-start(bf16[48,1280]{1,0:T(8,128)(2,1)} %get-tuple-element.34), channel_id=1, source_target_pairs={{0,4},{1,5},{2,6},{3,7},{4,0},{5,1},{6,2},{7,3},{8,12},{9,13},{10,... | collective-permute-start | bytes 368648 | tf_op jit(solution)/shard_map/ppermute | solution.py:656
  14.1 2.6 collective-permute-start.3
  16.8 1.8 collective-permute-start
  19.0 8.9 %collective-permute-done.3 = bf16[48,1280]{1,0:T(8,128)(2,1)S(1)} collective-permute-done((bf16[48,1280]{1,0:T(8,128)(2,1)}, bf16[48,1280]{1,0:T(8,128)(2,1)S(1)}, u32[]{:S(2)}, u32[]{:S(2)}) %collective-permute-start.3) | collective-permute-done | bytes 122912 | tf_op jit(solution)/shard_map/ppermute | solution.py:656
  28.0 1.8 collective-permute-start.5
  32.1 10.3 %collective-permute-done.5.refs_4_.refs_5_ = bf16[192,1280]{1,0:T(8,128)(2,1)} collective-permute-done((bf16[192,1280]{1,0:T(8,128)(2,1)S(1)}, bf16[192,1280]{1,0:T(8,128)(2,1)}, u32[]{:S(2)}, u32[]{:S(2)}) %collective-permute-start.5) | collective-permute-done | bytes 491552 | tf_op jit(solution)/shard_map/ppermute | solution.py:656
  45.8 2.2 collective-permute-done.6.refs_5_.refs_6_
  48.0 8.8 %collective-permute-done.7.refs_6_.refs_7_ = bf16[192,1280]{1,0:T(8,128)(2,1)} collective-permute-done((bf16[192,1280]{1,0:T(8,128)(2,1)}, bf16[192,1280]{1,0:T(8,128)(2,1)}, u32[]{:S(2)}, u32[]{:S(2)}) %collective-permute-start.7) | collective-permute-done | bytes 491552 | tf_op jit(solution)/shard_map/ppermute | solution.py:660
  58.8 1.8 maximum_select_fusion.refs_0_
  62.9 10.7 %project.1 = (bf16[1024,768]{1,0:T(8,128)(2,1)}, bf16[1024,768]{1,0:T(8,128)(2,1)}, bf16[1024,768]{1,0:T(8,128)(2,1)}, bf16[1024,768]{1,0:T(8,128)(2,1)}, f32[8,768]{1,0:T(8,128)}) custom-call(bf16[1024,768]{1,0:T(8,128)(2,1)} %maximum_select_fusion.refs_0_, f32[1024,128]{1,0:T(8,128)} %pad_maximum_fusion.refs_1_.cos_ref, ...), custom_call_target="tpu_custom_call" | custom-call | flops 3623878656 | bytes 11403264 | tf_op jit(solution)/shard_map/project/pallas_call | solution.py:127
  73.6 14.1 %attend.1 = (bf16[1024,768]{1,0:T(8,128)(2,1)}, f32[8,6,256]{2,1,0:T(8,128)}) custom-call(s32[8]{0:T(128)} %and_select_fusion.first_ref, bf16[1024,768]{1,0:T(8,128)(2,1)} %get-tuple-element.35.q_ref, bf16[1024,768]{1,0:T(8,128)(2,1)} %get-tuple-element.36.k_ref, bf16[1024,768]{1,0:T(8,128)(2,1)} %get-tuple-element.37.v_ref, s32[1,1024]{1,0:T(1,128)} %bitcast.64), custom_call_target="tpu_custom_call" | custom-call | flops 3221225472 | bytes 7864320 | tf_op jit(solution)/shard_map/attend/pallas_call | solution.py:212
  87.7 1.9 maximum_select_fusion.1.refs_2_.dy_any
  89.5 15.7 %all-gather.2.cloned.1.call-done.refs_4_ = bf16[6912,768]{1,0:T(8,128)(2,1)} async-done(((bf16[432,768]{1,0:T(8,128)(2,1)}), bf16[6912,768]{1,0:T(8,128)(2,1)}) %all-gather.2.cloned.1.call-update) | async-done | bytes 10616848 | tf_op jit(solution)/shard_map/all_gather | solution.py:817
  105.2 34.7 %feed.1 = (bf16[1024,768]{1,0:T(8,128)(2,1)}, bf16[1024,768]{1,0:T(8,128)(2,1)}, bf16[1024,2048]{1,0:T(8,128)(2,1)}, bf16[1024,2048]{1,0:T(8,128)(2,1)}, bf16[10...) custom-call(bf16[1024,768]{1,0:T(8,128)(2,1)} %maximum_select_fusion.refs_0_, ...), custom_call_target="tpu_custom_call" | custom-call | flops 21743271936 | bytes 28311552 | tf_op jit(solution)/shard_map/feed/pallas_call | solution.py:457
  140.0 15.7 %feed_grads.1 = bf16[16,144,2048]{2,1,0:T(8,128)(2,1)} custom-call(bf16[1024,768]{1,0:T(8,128)(2,1)} %get-tuple-element.45.n_ref, bf16[1024,2048]{1,0:T(8,128)(2,1)} %get-tuple-element.46.dgate_ref, bf16[1024,2048]{1,0:T(8,128)(2,1)} %get-tuple-element.47.dup_ref, bf16[1024,2048]{1,0:T(8,128)(2,1)} %get-tuple-element.48.hid_any, ...), custom_call_target="tpu_custom_call" | custom-call | flops 9663676416 | bytes 17301504 | tf_op jit(solution)/shard_map/feed_grads/pallas_call | solution.py:590
  155.7 22.8 %attend_back.1.refs_2_ = bf16[1024,2304]{1,0:T(8,128)(2,1)} custom-call(s32[8]{0:T(128)} %and_select_fusion.first_ref, bf16[1024,768]{1,0:T(8,128)(2,1)} %get-tuple-element.35.q_ref, bf16[1024,768]{1,0:T(8,128)(2,1)} %get-tuple-element.36.k_ref, bf16[1024,768]{1,0:T(8,128)(2,1)} %get-tuple-element.37.v_ref, bf16[1024,768]{1,0:T(8,128)(2,1)} %get-tuple-element.49.g_ref, ...), custom_call_target="tpu_custom_call" | custom-call | flops 8053063680 | bytes 12582912 | tf_op jit(solution)/shard_map/attend_back/pallas_call | solution.py:308
  178.5 10.8 %grad_in.1 = (bf16[8,48,3072]{2,1,0:T(8,128)(2,1)}, bf16[8,48,3072]{2,1,0:T(8,128)(2,1)}) custom-call(bf16[1024,768]{1,0:T(8,128)(2,1)} %get-tuple-element.43.refs_0_, bf16[1024,768]{1,0:T(8,128)(2,1)} %get-tuple-element.38.refs_1_, bf16[1024,2304]{1,0:T(8,128)(2,1)} %attend_back.1.refs_2_, bf16[1024,768]{1,0:T(8,128)(2,1)} %get-tuple-element.51.refs_3_), custom_call_target="tpu_custom_call" | custom-call | flops 4831838208 | bytes 12582912 | tf_op jit(solution)/shard_map/grad_in/pallas_call | solution.py:533
  189.6 4.5 %collective-permute-done.14 = bf16[8,48,3072]{2,1,0:T(8,128)(2,1)S(1)} collective-permute-done((bf16[8,48,3072]{2,1,0:T(8,128)(2,1)}, bf16[8,48,3072]{2,1,0:T(8,128)(2,1)S(1)}, u32[]{:S(2)}, u32[]{:S(2)}) %collective-permute-start.14) | collective-permute-done | bytes 2359328 | tf_op jit(solution)/shard_map/ppermute | solution.py:656
  194.1 3.5 %add_convert_fusion = bf16[8,48,1536]{2,1,0:T(8,128)(2,1)} fusion(bf16[8,48,3072]{2,1,0:T(8,128)(2,1)S(1)} %collective-permute-done.14, s32[]{:T(128)S(6)} %select_n.110, bf16[8,48,3072]{2,1,0:T(8,128)(2,1)} %get-tuple-element.52), kind=kLoop, calls=%fused_computation.2 | loop fusion | flops 2359296 | bytes 3538948 | tf_op jit(solution)/shard_map/convert_element_type | solution.py:752
  198.9 2.1 constant_dynamic-slice_fusion
  201.7 24.9 %collective-permute-done.15 = bf16[8,48,1536]{2,1,0:T(8,128)(2,1)S(1)} collective-permute-done((bf16[8,48,1536]{2,1,0:T(8,128)(2,1)}, bf16[8,48,1536]{2,1,0:T(8,128)(2,1)S(1)}, u32[]{:S(2)}, u32[]{:S(2)}) %collective-permute-start.15) | collective-permute-done | bytes 1179680 | tf_op jit(solution)/shard_map/ppermute | solution.py:660
  226.6 2.1 add_convert_fusion.1
  229.9 13.0 %collective-permute-done.13 = bf16[512,768]{1,0:T(8,128)(2,1)} collective-permute-done((bf16[512,768]{1,0:T(8,128)(2,1)}, bf16[512,768]{1,0:T(8,128)(2,1)}, u32[]{:S(2)}, u32[]{:S(2)}) %collective-permute-start.13) | collective-permute-done | bytes 786464 | tf_op jit(solution)/shard_map/ppermute | solution.py:660
  244.3 11.3 %input_grad.1 = f32[1024,768]{1,0:T(8,128)} custom-call(bf16[1024,768]{1,0:T(8,128)(2,1)} %maximum_select_fusion.refs_0_, f32[1024,768]{1,0:T(8,128)} %get-tuple-element.55.refs_1_, bf16[1024,2304]{1,0:T(8,128)(2,1)} %attend_back.1.refs_2_, f32[8,768]{1,0:T(8,128)} %get-tuple-element.40.refs_3_, bf16[192,1280]{1,0:T(8,128)(2,1)} %copy-done.7, ...), custom_call_target="tpu_custom_call" | custom-call | flops 3623878656 | bytes 16121856 | tf_op jit(solution)/shard_map/input_grad/pallas_call | solution.py:638
  258.6 1.7 fusion.6
  263.2 1.6 collective-permute-start.20
  266.1 6.5 %collective-permute-done.18 = bf16[48,1536]{1,0:T(8,128)(2,1)S(1)} collective-permute-done((bf16[48,1536]{1,0:T(8,128)(2,1)S(1)}, bf16[48,1536]{1,0:T(8,128)(2,1)S(1)}, u32[]{:S(2)}, u32[]{:S(2)}) %collective-permute-start.18) | collective-permute-done | bytes 147488 | tf_op jit(solution)/shard_map/ppermute | solution.py:656
  272.6 5.0 %collective-permute-done.20 = bf16[48,1536]{1,0:T(8,128)(2,1)S(1)} collective-permute-done((bf16[48,1536]{1,0:T(8,128)(2,1)S(1)}, bf16[48,1536]{1,0:T(8,128)(2,1)S(1)}, u32[]{:S(2)}, u32[]{:S(2)}) %collective-permute-start.20) | collective-permute-done | bytes 147488 | tf_op jit(solution)/shard_map/ppermute | solution.py:656
  279.5 1.9 maximum_bitcast_fusion
  283.0 1.6 collective-permute-start.22
  286.2 10.9 %collective-permute-done.22 = bf16[144,2048]{1,0:T(8,128)(2,1)S(1)} collective-permute-done((bf16[144,2048]{1,0:T(8,128)(2,1)}, bf16[144,2048]{1,0:T(8,128)(2,1)S(1)}, u32[]{:S(2)}, u32[]{:S(2)}) %collective-permute-start.22) | collective-permute-done | bytes 589856 | tf_op jit(solution)/shard_map/ppermute | solution.py:660
  (106 shorter events, 32.2 us)
Async XLA Ops:
  7.2 98.1 %all-gather.2.cloned.1.call-start = ((), (), s32[]{:S(2)}) async-start(), calls=%async_computation.1 | async-start | bytes 11280384 | tf_op jit(solution)/shard_map/all_gather | solution.py:817
  11.0 272.1 %reduce-scatter.2.cloned.1.call-start = ((), (), s32[]{:S(2)}) async-start(), calls=%async_computation.2 | async-start | bytes 10027008 | tf_op jit(solution)/shard_map/reduce_scatter | solution.py:870
  11.0 8.0 %collective-permute-start.2 = (bf16[48,1280]{1,0:T(8,128)(2,1)}, bf16[48,1280]{1,0:T(8,128)(2,1)S(1)}, u32[]{:S(2)}, u32[]{:S(2)}) collective-permute-start(bf16[48,1280]{1,0:T(8,128)(2,1)} %get-tuple-element.34), channel_id=1, source_target_pairs={{0,4},{1,5},{2,6},{3,7},{4,0},{5,1},{6,2},{7,3},{8,12},{9,13},{10,... | collective-permute-start | bytes 368648 | tf_op jit(solution)/shard_map/ppermute | solution.py:656
  14.1 13.9 %collective-permute-start.3 = (bf16[48,1280]{1,0:T(8,128)(2,1)}, bf16[48,1280]{1,0:T(8,128)(2,1)S(1)}, u32[]{:S(2)}, u32[]{:S(2)}) collective-permute-start(bf16[48,1280]{1,0:T(8,128)(2,1)} %get-tuple-element.34), channel_id=1, source_target_pairs={{0,8},{1,9},{2,10},{3,11},{4,12},{5,13},{6,14},{7,15},{8,0},{9,1},... | collective-permute-start | bytes 368648 | tf_op jit(solution)/shard_map/ppermute | solution.py:656
  16.7 11.3 %collective-permute-start.4 = (bf16[48,1280]{1,0:T(8,128)(2,1)}, bf16[48,1280]{1,0:T(8,128)(2,1)S(1)}, u32[]{:S(2)}, u32[]{:S(2)}) collective-permute-start(bf16[48,1280]{1,0:T(8,128)(2,1)} %get-tuple-element.34), channel_id=1, source_target_pairs={{0,12},{1,13},{2,14},{3,15},{4,8},{5,9},{6,10},{7,11},{8,4},{9,5},... | collective-permute-start | bytes 368648 | tf_op jit(solution)/shard_map/ppermute | solution.py:656
  16.7 13.1 %copy-start.14 = (s32[2,1,512]{2,1,0:T(1,128)S(1)}, s32[2,1,512]{2,1,0:T(1,128)}, u32[]{:S(2)}) copy-start(s32[2,1,512]{2,1,0:T(1,128)} %param.13) | copy-start | bytes 12292
  16.8 42.0 %collective-permute-start = (bf16[512,768]{1,0:T(8,128)(2,1)S(1)}, bf16[512,768]{1,0:T(8,128)(2,1)S(1)}, u32[]{:S(2)}, u32[]{:S(2)}) collective-permute-start(bf16[512,768]{1,0:T(8,128)(2,1)S(1)} %get-tuple-element.120), channel_id=1, source_target_pairs={{0,16},{16,0},{1,17},{17,1},{2,18},{18,2},{3,19},{19,3},{4,20},{20... | collective-permute-start | bytes 2359304 | tf_op jit(solution)/shard_map/ppermute | solution.py:660
  28.0 17.3 %copy-start.7 = (bf16[192,1280]{1,0:T(8,128)(2,1)}, bf16[192,1280]{1,0:T(8,128)(2,1)S(1)}, u32[]{:S(2)}) copy-start(bf16[192,1280]{1,0:T(8,128)(2,1)S(1)} %constant_dynamic-update-slice_fusion.refs_3_.refs_4_) | copy-start | bytes 1474564
  28.0 14.4 %collective-permute-start.5 = (bf16[192,1280]{1,0:T(8,128)(2,1)S(1)}, bf16[192,1280]{1,0:T(8,128)(2,1)}, u32[]{:S(2)}, u32[]{:S(2)}) collective-permute-start(bf16[192,1280]{1,0:T(8,128)(2,1)S(1)} %constant_dynamic-update-slice_fusion.refs_3_.refs_4_), channel_id=1, source_target_pairs={{0,2},{1,3},{2,0},{3,1},{4,6},{5,7},{6,4},{7,5},{8,10},{9,11},{10,... | collective-permute-start | bytes 1474568 | tf_op jit(solution)/shard_map/ppermute | solution.py:656
  29.8 15.5 %collective-permute-start.1 = (s32[512]{0:T(512)S(1)}, s32[512]{0:T(512)S(1)}, u32[]{:S(2)}, u32[]{:S(2)}) collective-permute-start(s32[512]{0:T(512)S(1)} %bitcast.66), channel_id=1, source_target_pairs={{0,16},{16,0},{1,17},{17,1},{2,18},{18,2},{3,19},{19,3},{4,20},{20... | collective-permute-start | bytes 6152 | tf_op jit(solution)/shard_map/ppermute | solution.py:660
  31.5 16.5 %collective-permute-start.6 = (bf16[192,1280]{1,0:T(8,128)(2,1)S(1)}, bf16[192,1280]{1,0:T(8,128)(2,1)}, u32[]{:S(2)}, u32[]{:S(2)}) collective-permute-start(bf16[192,1280]{1,0:T(8,128)(2,1)S(1)} %constant_dynamic-update-slice_fusion.refs_3_.refs_4_), channel_id=1, source_target_pairs={{0,16},{16,0},{1,17},{17,1},{2,18},{18,2},{3,19},{19,3},{4,20},{20... | collective-permute-start | bytes 1474568 | tf_op jit(solution)/shard_map/ppermute | solution.py:660
  42.4 14.5 %collective-permute-start.7 = (bf16[192,1280]{1,0:T(8,128)(2,1)}, bf16[192,1280]{1,0:T(8,128)(2,1)}, u32[]{:S(2)}, u32[]{:S(2)}) collective-permute-start(bf16[192,1280]{1,0:T(8,128)(2,1)} %collective-permute-done.5.refs_4_.refs_5_), channel_id=1, source_target_pairs={{0,16},{16,0},{1,17},{17,1},{2,18},{18,2},{3,19},{19,3},{4,20},{20... | collective-permute-start | bytes 1474568 | tf_op jit(solution)/shard_map/ppermute | solution.py:660
  45.3 15.3 %collective-permute-start.8 = (bf16[192,1280]{1,0:T(8,128)(2,1)S(1)}, bf16[192,1280]{1,0:T(8,128)(2,1)}, u32[]{:S(2)}, u32[]{:S(2)}) collective-permute-start(bf16[192,1280]{1,0:T(8,128)(2,1)S(1)} %constant_dynamic-update-slice_fusion.refs_3_.refs_4_), channel_id=1, source_target_pairs={{0,1},{1,0},{2,3},{3,2},{4,5},{5,4},{6,7},{7,6},{8,9},{9,8},{10,11... | collective-permute-start | bytes 1474568 | tf_op jit(solution)/shard_map/ppermute | solution.py:656
  45.3 15.3 %collective-permute-start.9 = (bf16[192,1280]{1,0:T(8,128)(2,1)}, bf16[192,1280]{1,0:T(8,128)(2,1)}, u32[]{:S(2)}, u32[]{:S(2)}) collective-permute-start(bf16[192,1280]{1,0:T(8,128)(2,1)} %collective-permute-done.5.refs_4_.refs_5_), channel_id=1, source_target_pairs={{0,1},{1,0},{2,3},{3,2},{4,5},{5,4},{6,7},{7,6},{8,9},{9,8},{10,11... | collective-permute-start | bytes 1474568 | tf_op jit(solution)/shard_map/ppermute | solution.py:656
  48.0 12.7 %collective-permute-start.10 = (bf16[192,1280]{1,0:T(8,128)(2,1)}, bf16[192,1280]{1,0:T(8,128)(2,1)}, u32[]{:S(2)}, u32[]{:S(2)}) collective-permute-start(bf16[192,1280]{1,0:T(8,128)(2,1)} %collective-permute-done.6.refs_5_.refs_6_), channel_id=1, source_target_pairs={{0,1},{1,0},{2,3},{3,2},{4,5},{5,4},{6,7},{7,6},{8,9},{9,8},{10,11... | collective-permute-start | bytes 1474568 | tf_op jit(solution)/shard_map/ppermute | solution.py:656
  56.8 3.8 %collective-permute-start.11 = (bf16[192,1280]{1,0:T(8,128)(2,1)}, bf16[192,1280]{1,0:T(8,128)(2,1)}, u32[]{:S(2)}, u32[]{:S(2)}) collective-permute-start(bf16[192,1280]{1,0:T(8,128)(2,1)} %collective-permute-done.7.refs_6_.refs_7_), channel_id=1, source_target_pairs={{0,1},{1,0},{2,3},{3,2},{4,5},{5,4},{6,7},{7,6},{8,9},{9,8},{10,11... | collective-permute-start | bytes 1474568 | tf_op jit(solution)/shard_map/ppermute | solution.py:656
  60.8 26.8 %collective-permute-start.12 = (bf16[512,768]{1,0:T(8,128)(2,1)S(1)}, bf16[512,768]{1,0:T(8,128)(2,1)S(1)}, u32[]{:S(2)}, u32[]{:S(2)}) collective-permute-start(bf16[512,768]{1,0:T(8,128)(2,1)S(1)} %get-tuple-element.118), channel_id=1, source_target_pairs={{0,16},{16,0},{1,17},{17,1},{2,18},{18,2},{3,19},{19,3},{4,20},{20... | collective-permute-start | bytes 2359304 | tf_op jit(solution)/shard_map/ppermute | solution.py:660
  189.3 4.7 %collective-permute-start.14 = (bf16[8,48,3072]{2,1,0:T(8,128)(2,1)}, bf16[8,48,3072]{2,1,0:T(8,128)(2,1)S(1)}, u32[]{:S(2)}, u32[]{:S(2)}) collective-permute-start(bf16[8,48,3072]{2,1,0:T(8,128)(2,1)} %get-tuple-element.53), channel_id=1, source_target_pairs={{0,1},{1,0},{2,3},{3,2},{4,5},{5,4},{6,7},{7,6},{8,9},{9,8},{10,11... | collective-permute-start | bytes 7077896 | tf_op jit(solution)/shard_map/ppermute | solution.py:656
  194.1 32.6 %copy-start.1 = (bf16[8,48,3072]{2,1,0:T(8,128)(2,1)}, bf16[8,48,3072]{2,1,0:T(8,128)(2,1)S(1)}, u32[]{:S(2)}) copy-start(bf16[8,48,3072]{2,1,0:T(8,128)(2,1)S(1)} %collective-permute-done.14) | copy-start | bytes 7077892
  197.6 29.1 %collective-permute-start.15 = (bf16[8,48,1536]{2,1,0:T(8,128)(2,1)}, bf16[8,48,1536]{2,1,0:T(8,128)(2,1)S(1)}, u32[]{:S(2)}, u32[]{:S(2)}) collective-permute-start(bf16[8,48,1536]{2,1,0:T(8,128)(2,1)} %add_convert_fusion), channel_id=1, source_target_pairs={{0,16},{16,0},{1,17},{17,1},{2,18},{18,2},{3,19},{19,3},{4,20},{20... | collective-permute-start | bytes 3538952 | tf_op jit(solution)/shard_map/ppermute | solution.py:660
  201.0 41.9 %collective-permute-start.13 = (bf16[512,768]{1,0:T(8,128)(2,1)}, bf16[512,768]{1,0:T(8,128)(2,1)}, u32[]{:S(2)}, u32[]{:S(2)}) collective-permute-start(bf16[512,768]{1,0:T(8,128)(2,1)} %constant_dynamic-slice_fusion), channel_id=1, source_target_pairs={{0,16},{16,0},{1,17},{17,1},{2,18},{18,2},{3,19},{19,3},{4,20},{20... | collective-permute-start | bytes 2359304 | tf_op jit(solution)/shard_map/ppermute | solution.py:660
  201.7 41.2 %copy-start.4 = (bf16[1024,768]{1,0:T(8,128)(2,1)S(1)}, bf16[1024,768]{1,0:T(8,128)(2,1)}, u32[]{:S(2)}) copy-start(bf16[1024,768]{1,0:T(8,128)(2,1)} %get-tuple-element.42) | copy-start | bytes 4718596
  228.7 29.9 %collective-permute-start.17 = (bf16[4,48,1536]{2,1,0:T(8,128)(2,1)}, bf16[4,48,1536]{2,1,0:T(8,128)(2,1)}, u32[]{:S(2)}, u32[]{:S(2)}) collective-permute-start(bf16[4,48,1536]{2,1,0:T(8,128)(2,1)} %add_convert_fusion.1), channel_id=1, source_target_pairs={{0,2},{1,3},{2,0},{3,1},{4,6},{5,7},{6,4},{7,5},{8,10},{9,11},{10,... | collective-permute-start | bytes 1769480 | tf_op jit(solution)/shard_map/ppermute | solution.py:656
  257.1 22.1 %collective-permute-start.16 = (bf16[512,768]{1,0:T(8,128)(2,1)S(1)}, bf16[512,768]{1,0:T(8,128)(2,1)S(1)}, u32[]{:S(2)}, u32[]{:S(2)}) collective-permute-start(bf16[512,768]{1,0:T(8,128)(2,1)S(1)} %dynamic-slice_convert_fusion), channel_id=1, source_target_pairs={{0,16},{16,0},{1,17},{17,1},{2,18},{18,2},{3,19},{19,3},{4,20},{20... | collective-permute-start | bytes 2359304 | tf_op jit(solution)/shard_map/ppermute | solution.py:660
  260.4 12.2 %collective-permute-start.18 = (bf16[48,1536]{1,0:T(8,128)(2,1)S(1)}, bf16[48,1536]{1,0:T(8,128)(2,1)S(1)}, u32[]{:S(2)}, u32[]{:S(2)}) collective-permute-start(bf16[48,1536]{1,0:T(8,128)(2,1)S(1)} %get-tuple-element.129), channel_id=1, source_target_pairs={{0,4},{1,5},{2,6},{3,7},{4,0},{5,1},{6,2},{7,3},{8,12},{9,13},{10,... | collective-permute-start | bytes 442376 | tf_op jit(solution)/shard_map/ppermute | solution.py:656
  261.7 10.9 %collective-permute-start.19 = (bf16[48,1536]{1,0:T(8,128)(2,1)S(1)}, bf16[48,1536]{1,0:T(8,128)(2,1)S(1)}, u32[]{:S(2)}, u32[]{:S(2)}) collective-permute-start(bf16[48,1536]{1,0:T(8,128)(2,1)S(1)} %get-tuple-element.131), channel_id=1, source_target_pairs={{0,8},{1,9},{2,10},{3,11},{4,12},{5,13},{6,14},{7,15},{8,0},{9,1},... | collective-permute-start | bytes 442376 | tf_op jit(solution)/shard_map/ppermute | solution.py:656
  263.2 14.4 %collective-permute-start.20 = (bf16[48,1536]{1,0:T(8,128)(2,1)S(1)}, bf16[48,1536]{1,0:T(8,128)(2,1)S(1)}, u32[]{:S(2)}, u32[]{:S(2)}) collective-permute-start(bf16[48,1536]{1,0:T(8,128)(2,1)S(1)} %get-tuple-element.130), channel_id=1, source_target_pairs={{0,12},{1,13},{2,14},{3,15},{4,8},{5,9},{6,10},{7,11},{8,4},{9,5},... | collective-permute-start | bytes 442376 | tf_op jit(solution)/shard_map/ppermute | solution.py:656
  264.8 14.4 %copy-start = (f32[1024,768]{1,0:T(8,128)S(1)}, f32[1024,768]{1,0:T(8,128)}, u32[]{:S(2)}) copy-start(f32[1024,768]{1,0:T(8,128)} %input_grad.1) | copy-start | bytes 9437188
  277.7 5.3 %collective-permute-start.21 = (bf16[48,1536]{1,0:T(8,128)(2,1)S(1)}, bf16[48,1536]{1,0:T(8,128)(2,1)S(1)}, u32[]{:S(2)}, u32[]{:S(2)}) collective-permute-start(bf16[48,1536]{1,0:T(8,128)(2,1)S(1)} %fusion.5), channel_id=1, source_target_pairs={{0,16},{16,0},{1,17},{17,1},{2,18},{18,2},{3,19},{19,3},{4,20},{20... | collective-permute-start | bytes 442376 | tf_op jit(solution)/shard_map/ppermute | solution.py:660
  283.0 14.1 %copy-start.8 = (bf16[144,2048]{1,0:T(8,128)(2,1)S(1)}, bf16[144,2048]{1,0:T(8,128)(2,1)}, u32[]{:S(2)}) copy-start(bf16[144,2048]{1,0:T(8,128)(2,1)} %reduce-scatter.2.cloned.1.call-done) | copy-start | bytes 1769476
  283.0 14.1 %collective-permute-start.22 = (bf16[144,2048]{1,0:T(8,128)(2,1)}, bf16[144,2048]{1,0:T(8,128)(2,1)S(1)}, u32[]{:S(2)}, u32[]{:S(2)}) collective-permute-start(bf16[144,2048]{1,0:T(8,128)(2,1)} %reduce-scatter.2.cloned.1.call-done), channel_id=1, source_target_pairs={{0,16},{16,0},{1,17},{17,1},{2,18},{18,2},{3,19},{19,3},{4,20},{20... | collective-permute-start | bytes 1769480 | tf_op jit(solution)/shard_map/ppermute | solution.py:660
  284.7 12.6 %copy-start.5 = (bf16[48,2048]{1,0:T(8,128)(2,1)S(1)}, bf16[48,2048]{1,0:T(8,128)(2,1)}, u32[]{:S(2)}) copy-start(bf16[48,2048]{1,0:T(8,128)(2,1)} %gate_ref.1) | copy-start | bytes 589828
  (10 other events, 49.1 us)
Sparse Core Ops, SparseCore 0:
  11.1 94.1 all-gather.1
  155.8 116.3 reduce-scatter.1

commit v4 on v3

--- a/solution.py
+++ b/solution.py
@@ -674,13 +674,13 @@
     return lax.optimization_barrier((values,) + others)[0]
 
 
-def gather_rows(shard, parts):
+def gather_rows(shard, parts, before):
     if parts == 1:
         return [(lax.all_gather(shard, "fsdp", axis=0, tiled=True), (0,), 0)]
     uppers = tuple(range(0, parts, 4))
     mine = jnp.concatenate([shard] + [flip(shard, upper) for upper in uppers[1:]])
     beside = flip(mine, 2)
-    got = [(mine, 0, 0), (beside, 2, 0), (across(mine), 0, 1), (across(beside), 2, 1)]
+    got = [(mine, 0, 0), (beside, 2, 0), (across(gate(mine, before)), 0, 1), (across(beside), 2, 1)]
     got += [(flip(piece, 1), low + 1, side) for piece, low, side in got]
     return [(piece, tuple(upper + low for upper in uppers), side) for piece, low, side in got]
 
@@ -832,9 +832,10 @@
         first, second = jnp.where(seq_rank == 0, own, other), jnp.where(seq_rank == 0, other, own)
         return jnp.stack([first, second])[:, None]
 
-    groups_in = gather_rows(w_in, parts)
     own_x, other_x = exchanged(tokens)
-    x = ordered(own_x, across(other_x))
+    other_x = across(other_x)
+    groups_in = gather_rows(w_in, parts, other_x)
+    x = ordered(own_x, other_x)
     own_docs, other_docs = exchanged(doc_ids)
     docs = ordered(own_docs, across(other_docs))
     own_dy, other_dy = exchanged(gate(cotangent, x, *[piece for piece, *_ in groups_in]))
@@ -852,7 +853,8 @@
         x, attended, dy, gains, given, rows if parts > 1 else width, hidden_width
     )
     own_y, other_y = halves(y)
-    output = give_back(own_y, across(other_y))
+    other_y = across(other_y)
+    output = give_back(own_y, other_y)
 
     if parts == 1:
         sum_gate, sum_up, sum_down = [
@@ -871,16 +873,20 @@
         sums = (ff,)
     grads = attend_back(queries, keys, values, datt, lse, starts, first, cosine, sine)
     scatter = Scatter(
-        outer_sums(parts, [([normed], grads), ([attended], dmr)], width, "grad_in"), parts, seq_rank
+        outer_sums(parts, [([gate(normed, grads, other_y)], grads), ([attended], dmr)], width, "grad_in"), parts, seq_rank
     )
     sent = scatter.x_hop()
     grad_x = input_grad(gate(x, *sent), dm, grads, gains, groups_in)
     own_g, other_g = halves(grad_x)
+    other_g = other_g.astype(BF)
+    if parts > 1:
+        scatter.aside = gate(scatter.aside, other_g)
     sent = scatter.y_hop()
-    grad_tokens = give_back(own_g, across(gate(other_g.astype(BF), *sent)).astype(F32))
-    scatter.z_hop()
+    other_g = across(gate(other_g, *sent))
+    sent = scatter.z_hop()
+    sums = [part.astype(F32) + across(gate(part, *sent)).astype(F32) for part in sums]
+    grad_tokens = give_back(own_g, gate(other_g, *sent).astype(F32))
     sum_in = scatter.result()
-    sums = [part.astype(F32) + across(part).astype(F32) for part in sums]
     if parts == 1:
         sum_gate, sum_up, sum_down = sums
     else:

time: 312 us -> 309 us (level)
    ppermute x13, waiting for transfers between devices: 35.6 us -> 55.7 us  [flip(): return lax.ppermute(values, 'fsdp', [(i, i ^ bits) for i in range(count)])]
    ppermute x10, waiting for transfers between devices: 61.5 us -> 47.2 us  [across(): return lax.ppermute(values, 'seq', [(0, 1), (1, 0)])]
    all_gather x1, waiting for transfers between devices: 15.7 us -> 7.64 us  [per_device(): given = [lax.all_gather(packed, 'fsdp', axis=0, tiled=True)]]
where the time goes in v4:
time: 309 us; the launch traced here: 304 us
  Pallas kernels  123 us (40%)
  waiting for transfers between devices  111 us (36%)
  starting transfers between devices  24.5 us (8%)
  other arithmetic  24.2 us (8%)
  between operations  14.8 us (5%)
  local copies, waits for them, and re-layouts  6.24 us (2%)
    ppermute x13, waiting for transfers between devices, flip(): return lax.ppermute(values, 'fsdp', [(i, i ^ bits) for i in range(count)])  55.7 us
    ppermute x10, waiting for transfers between devices, across(): return lax.ppermute(values, 'seq', [(0, 1), (1, 0)])  47.2 us
    pallas_call x1, Pallas kernels, feed(): pl.pallas_call(functools.partial(feed_kernel, rows, len(given), width, hi...  34.7 us
    pallas_call x1, Pallas kernels, attend_back(): pl.pallas_call(functools.partial(attend_back_kernel, pairs), name='attend...  23.7 us
    pallas_call x1, Pallas kernels, feed_grads(): pl.pallas_call(functools.partial(feed_grads_kernel, parts, steps), name='...  15.7 us
    pallas_call x1, Pallas kernels, attend(): pl.pallas_call(functools.partial(attend_kernel, pairs), name='attend', ou...  14.4 us
    ppermute x13, starting transfers between devices, flip(): return lax.ppermute(values, 'fsdp', [(i, i ^ bits) for i in range(count)])  12.5 us
    ppermute x10, starting transfers between devices, across(): return lax.ppermute(values, 'seq', [(0, 1), (1, 0)])  11.9 us
  transfers between devices with their start and end apart: 25, of which 13 were waited for; matrix products, arithmetic and copies ran while one was open for 8% of the time, Pallas kernels for 23%

profile of v4, /device:TPU:0, one launch (start us, length us, event | category | flops | bytes accessed | tf_op | source)
XLA Modules:
  0.0 303.5 jit_solution(15115006545627485175)
XLA Ops:
  8.8 2.2 pack.1
  11.0 3.1 %collective-permute-start.2 = (bf16[48,1280]{1,0:T(8,128)(2,1)}, bf16[48,1280]{1,0:T(8,128)(2,1)S(1)}, u32[]{:S(2)}, u32[]{:S(2)}) collective-permute-start(bf16[48,1280]{1,0:T(8,128)(2,1)} %get-tuple-element.39), channel_id=1, source_target_pairs={{0,4},{1,5},{2,6},{3,7},{4,0},{5,1},{6,2},{7,3},{8,12},{9,13},{10,... | collective-permute-start | bytes 368648 | tf_op jit(solution)/shard_map/ppermute | solution.py:656
  14.1 2.6 collective-permute-start.3
  16.8 1.8 collective-permute-start
  19.0 8.9 %collective-permute-done.3 = bf16[48,1280]{1,0:T(8,128)(2,1)S(1)} collective-permute-done((bf16[48,1280]{1,0:T(8,128)(2,1)}, bf16[48,1280]{1,0:T(8,128)(2,1)S(1)}, u32[]{:S(2)}, u32[]{:S(2)}) %collective-permute-start.3) | collective-permute-done | bytes 122912 | tf_op jit(solution)/shard_map/ppermute | solution.py:656
  28.0 1.8 collective-permute-start.5
  31.5 10.8 %collective-permute-done.5.refs_4_.refs_5_ = bf16[192,1280]{1,0:T(8,128)(2,1)S(1)} collective-permute-done((bf16[192,1280]{1,0:T(8,128)(2,1)S(1)}, bf16[192,1280]{1,0:T(8,128)(2,1)S(1)}, u32[]{:S(2)}, u32[]{:S(2)}) %collective-permute-start.5) | collective-permute-done | bytes 491552 | tf_op jit(solution)/shard_map/ppermute | solution.py:656
  46.4 10.0 %collective-permute-done.7.refs_6_.refs_7_ = bf16[192,1280]{1,0:T(8,128)(2,1)S(1)} collective-permute-done((bf16[192,1280]{1,0:T(8,128)(2,1)S(1)}, bf16[192,1280]{1,0:T(8,128)(2,1)S(1)}, u32[]{:S(2)}, u32[]{:S(2)}) %collective-permute-start.7) | collective-permute-done | bytes 491552 | tf_op jit(solution)/shard_map/ppermute | solution.py:660
  56.4 8.3 %collective-permute-done.6.refs_5_.refs_6_ = bf16[192,1280]{1,0:T(8,128)(2,1)} collective-permute-done((bf16[192,1280]{1,0:T(8,128)(2,1)S(1)}, bf16[192,1280]{1,0:T(8,128)(2,1)}, u32[]{:S(2)}, u32[]{:S(2)}) %collective-permute-start.6) | collective-permute-done | bytes 491552 | tf_op jit(solution)/shard_map/ppermute | solution.py:660
  66.7 1.8 maximum_select_fusion.refs_0_
  70.7 10.7 %project.1 = (bf16[1024,768]{1,0:T(8,128)(2,1)}, bf16[1024,768]{1,0:T(8,128)(2,1)}, bf16[1024,768]{1,0:T(8,128)(2,1)}, bf16[1024,768]{1,0:T(8,128)(2,1)}, f32[8,768]{1,0:T(8,128)}) custom-call(bf16[1024,768]{1,0:T(8,128)(2,1)} %maximum_select_fusion.refs_0_, f32[1024,128]{1,0:T(8,128)} %pad_maximum_fusion.refs_1_.cos_ref, ...), custom_call_target="tpu_custom_call" | custom-call | flops 3623878656 | bytes 11403264 | tf_op jit(solution)/shard_map/project/pallas_call | solution.py:127
  81.4 14.4 %attend.1 = (bf16[1024,768]{1,0:T(8,128)(2,1)}, f32[8,6,256]{2,1,0:T(8,128)}) custom-call(s32[8]{0:T(128)} %and_select_fusion.first_ref, bf16[1024,768]{1,0:T(8,128)(2,1)} %get-tuple-element.41.q_ref, bf16[1024,768]{1,0:T(8,128)(2,1)} %get-tuple-element.42.k_ref, bf16[1024,768]{1,0:T(8,128)(2,1)} %get-tuple-element.43.v_ref, s32[1,1024]{1,0:T(1,128)} %bitcast.64), custom_call_target="tpu_custom_call" | custom-call | flops 3221225472 | bytes 7864320 | tf_op jit(solution)/shard_map/attend/pallas_call | solution.py:212
  95.7 1.9 maximum_select_fusion.1.refs_2_.dy_any
  97.6 7.6 %all-gather.2.cloned.1.call-done.refs_4_ = bf16[6912,768]{1,0:T(8,128)(2,1)} async-done(((bf16[432,768]{1,0:T(8,128)(2,1)}), bf16[6912,768]{1,0:T(8,128)(2,1)}) %all-gather.2.cloned.1.call-update) | async-done | bytes 10616848 | tf_op jit(solution)/shard_map/all_gather | solution.py:817
  105.2 34.7 %feed.1 = (bf16[1024,768]{1,0:T(8,128)(2,1)}, bf16[1024,768]{1,0:T(8,128)(2,1)}, bf16[1024,2048]{1,0:T(8,128)(2,1)}, bf16[1024,2048]{1,0:T(8,128)(2,1)}, bf16[10...) custom-call(bf16[1024,768]{1,0:T(8,128)(2,1)} %maximum_select_fusion.refs_0_, ...), custom_call_target="tpu_custom_call" | custom-call | flops 21743271936 | bytes 28311552 | tf_op jit(solution)/shard_map/feed/pallas_call | solution.py:457
  140.0 15.7 %feed_grads.1 = bf16[16,144,2048]{2,1,0:T(8,128)(2,1)} custom-call(bf16[1024,768]{1,0:T(8,128)(2,1)} %get-tuple-element.51.n_ref, bf16[1024,2048]{1,0:T(8,128)(2,1)} %get-tuple-element.52.dgate_ref, bf16[1024,2048]{1,0:T(8,128)(2,1)} %get-tuple-element.53.dup_ref, bf16[1024,2048]{1,0:T(8,128)(2,1)} %get-tuple-element.54.hid_any, ...), custom_call_target="tpu_custom_call" | custom-call | flops 9663676416 | bytes 17301504 | tf_op jit(solution)/shard_map/feed_grads/pallas_call | solution.py:590
  158.7 23.7 %attend_back.1.refs_2_ = bf16[1024,2304]{1,0:T(8,128)(2,1)} custom-call(s32[8]{0:T(128)} %and_select_fusion.first_ref, bf16[1024,768]{1,0:T(8,128)(2,1)} %get-tuple-element.41.q_ref, bf16[1024,768]{1,0:T(8,128)(2,1)} %get-tuple-element.42.k_ref, bf16[1024,768]{1,0:T(8,128)(2,1)} %get-tuple-element.43.v_ref, bf16[1024,768]{1,0:T(8,128)(2,1)} %get-tuple-element.55.g_ref, ...), custom_call_target="tpu_custom_call" | custom-call | flops 8053063680 | bytes 12582912 | tf_op jit(solution)/shard_map/attend_back/pallas_call | solution.py:308
  182.5 10.8 %grad_in.1 = (bf16[8,48,3072]{2,1,0:T(8,128)(2,1)}, bf16[8,48,3072]{2,1,0:T(8,128)(2,1)}) custom-call(bf16[1024,768]{1,0:T(8,128)(2,1)} %get-tuple-element.57.refs_0_, bf16[1024,768]{1,0:T(8,128)(2,1)} %get-tuple-element.44.refs_1_, bf16[1024,2304]{1,0:T(8,128)(2,1)} %attend_back.1.refs_2_, bf16[1024,768]{1,0:T(8,128)(2,1)} %get-tuple-element.58.refs_3_), custom_call_target="tpu_custom_call" | custom-call | flops 4831838208 | bytes 12582912 | tf_op jit(solution)/shard_map/grad_in/pallas_call | solution.py:533
  193.3 4.7 %collective-permute-done.14 = bf16[8,48,3072]{2,1,0:T(8,128)(2,1)S(1)} collective-permute-done((bf16[8,48,3072]{2,1,0:T(8,128)(2,1)}, bf16[8,48,3072]{2,1,0:T(8,128)(2,1)S(1)}, u32[]{:S(2)}, u32[]{:S(2)}) %collective-permute-start.14) | collective-permute-done | bytes 2359328 | tf_op jit(solution)/shard_map/ppermute | solution.py:656
  198.0 3.5 %add_convert_fusion = bf16[8,48,1536]{2,1,0:T(8,128)(2,1)} fusion(bf16[8,48,3072]{2,1,0:T(8,128)(2,1)S(1)} %collective-permute-done.14, s32[]{:T(128)S(6)} %select_n.110, bf16[8,48,3072]{2,1,0:T(8,128)(2,1)} %get-tuple-element.59), kind=kLoop, calls=%fused_computation.2 | loop fusion | flops 2359296 | bytes 3538948 | tf_op jit(solution)/shard_map/convert_element_type | solution.py:752
  202.0 11.1 %input_grad.1 = f32[1024,768]{1,0:T(8,128)} custom-call(bf16[1024,768]{1,0:T(8,128)(2,1)} %maximum_select_fusion.refs_0_, f32[1024,768]{1,0:T(8,128)} %get-tuple-element.62.refs_1_, bf16[1024,2304]{1,0:T(8,128)(2,1)} %attend_back.1.refs_2_, f32[8,768]{1,0:T(8,128)} %get-tuple-element.46.refs_3_, bf16[192,1280]{1,0:T(8,128)(2,1)} %copy-done.10, ...), custom_call_target="tpu_custom_call" | custom-call | flops 3623878656 | bytes 16121856 | tf_op jit(solution)/shard_map/input_grad/pallas_call | solution.py:638
  213.1 2.4 dynamic-slice_convert_fusion
  215.5 14.3 %collective-permute-done.15 = bf16[8,48,1536]{2,1,0:T(8,128)(2,1)S(1)} collective-permute-done((bf16[8,48,1536]{2,1,0:T(8,128)(2,1)}, bf16[8,48,1536]{2,1,0:T(8,128)(2,1)S(1)}, u32[]{:S(2)}, u32[]{:S(2)}) %collective-permute-start.15) | collective-permute-done | bytes 1179680 | tf_op jit(solution)/shard_map/ppermute | solution.py:660
  229.7 2.1 add_convert_fusion.1
  231.9 1.7 select_bitcast_fusion.1
  235.1 14.3 %collective-permute-done.17 = bf16[4,48,1536]{2,1,0:T(8,128)(2,1)} collective-permute-done((bf16[4,48,1536]{2,1,0:T(8,128)(2,1)}, bf16[4,48,1536]{2,1,0:T(8,128)(2,1)}, u32[]{:S(2)}, u32[]{:S(2)}) %collective-permute-start.17) | collective-permute-done | bytes 589856 | tf_op jit(solution)/shard_map/ppermute | solution.py:656
  251.4 4.0 %collective-permute-start.20 = (bf16[48,1536]{1,0:T(8,128)(2,1)S(1)}, bf16[48,1536]{1,0:T(8,128)(2,1)S(1)}, u32[]{:S(2)}, u32[]{:S(2)}) collective-permute-start(bf16[48,1536]{1,0:T(8,128)(2,1)S(1)} %get-tuple-element.139), channel_id=1, source_target_pairs={{0,12},{1,13},{2,14},{3,15},{4,8},{5,9},{6,10},{7,11},{8,4},{9,5},... | collective-permute-start | bytes 442376 | tf_op jit(solution)/shard_map/ppermute | solution.py:656
  256.8 8.5 %collective-permute-done.18 = bf16[48,1536]{1,0:T(8,128)(2,1)S(1)} collective-permute-done((bf16[48,1536]{1,0:T(8,128)(2,1)S(1)}, bf16[48,1536]{1,0:T(8,128)(2,1)S(1)}, u32[]{:S(2)}, u32[]{:S(2)}) %collective-permute-start.18) | collective-permute-done | bytes 147488 | tf_op jit(solution)/shard_map/ppermute | solution.py:656
  265.3 8.0 %collective-permute-done.19 = bf16[48,1536]{1,0:T(8,128)(2,1)S(1)} collective-permute-done((bf16[48,1536]{1,0:T(8,128)(2,1)S(1)}, bf16[48,1536]{1,0:T(8,128)(2,1)S(1)}, u32[]{:S(2)}, u32[]{:S(2)}) %collective-permute-start.19) | collective-permute-done | bytes 147488 | tf_op jit(solution)/shard_map/ppermute | solution.py:656
  273.8 1.9 maximum_bitcast_fusion
  275.7 3.0 collective-permute-done.21
  281.8 11.6 %collective-permute-done.22 = bf16[144,2048]{1,0:T(8,128)(2,1)S(1)} collective-permute-done((bf16[144,2048]{1,0:T(8,128)(2,1)}, bf16[144,2048]{1,0:T(8,128)(2,1)S(1)}, u32[]{:S(2)}, u32[]{:S(2)}) %collective-permute-start.22) | collective-permute-done | bytes 589856 | tf_op jit(solution)/shard_map/ppermute | solution.py:660
  (116 shorter events, 26.8 us)
Async XLA Ops:
  7.2 98.1 %all-gather.2.cloned.1.call-start = ((), (), s32[]{:S(2)}) async-start(), calls=%async_computation.1 | async-start | bytes 11280384 | tf_op jit(solution)/shard_map/all_gather | solution.py:817
  11.0 267.7 %reduce-scatter.2.cloned.1.call-start = ((), (), s32[]{:S(2)}) async-start(), calls=%async_computation.2 | async-start | bytes 10027008 | tf_op jit(solution)/shard_map/reduce_scatter | solution.py:872
  11.0 8.0 %collective-permute-start.2 = (bf16[48,1280]{1,0:T(8,128)(2,1)}, bf16[48,1280]{1,0:T(8,128)(2,1)S(1)}, u32[]{:S(2)}, u32[]{:S(2)}) collective-permute-start(bf16[48,1280]{1,0:T(8,128)(2,1)} %get-tuple-element.39), channel_id=1, source_target_pairs={{0,4},{1,5},{2,6},{3,7},{4,0},{5,1},{6,2},{7,3},{8,12},{9,13},{10,... | collective-permute-start | bytes 368648 | tf_op jit(solution)/shard_map/ppermute | solution.py:656
  14.1 13.9 %collective-permute-start.3 = (bf16[48,1280]{1,0:T(8,128)(2,1)}, bf16[48,1280]{1,0:T(8,128)(2,1)S(1)}, u32[]{:S(2)}, u32[]{:S(2)}) collective-permute-start(bf16[48,1280]{1,0:T(8,128)(2,1)} %get-tuple-element.39), channel_id=1, source_target_pairs={{0,8},{1,9},{2,10},{3,11},{4,12},{5,13},{6,14},{7,15},{8,0},{9,1},... | collective-permute-start | bytes 368648 | tf_op jit(solution)/shard_map/ppermute | solution.py:656
  16.7 11.3 %collective-permute-start.4 = (bf16[48,1280]{1,0:T(8,128)(2,1)}, bf16[48,1280]{1,0:T(8,128)(2,1)S(1)}, u32[]{:S(2)}, u32[]{:S(2)}) collective-permute-start(bf16[48,1280]{1,0:T(8,128)(2,1)} %get-tuple-element.39), channel_id=1, source_target_pairs={{0,12},{1,13},{2,14},{3,15},{4,8},{5,9},{6,10},{7,11},{8,4},{9,5},... | collective-permute-start | bytes 368648 | tf_op jit(solution)/shard_map/ppermute | solution.py:656
  16.7 13.1 %copy-start.19 = (s32[2,1,512]{2,1,0:T(1,128)S(1)}, s32[2,1,512]{2,1,0:T(1,128)}, u32[]{:S(2)}) copy-start(s32[2,1,512]{2,1,0:T(1,128)} %param.13) | copy-start | bytes 12292
  16.8 26.9 %collective-permute-start = (bf16[512,768]{1,0:T(8,128)(2,1)S(1)}, bf16[512,768]{1,0:T(8,128)(2,1)S(1)}, u32[]{:S(2)}, u32[]{:S(2)}) collective-permute-start(bf16[512,768]{1,0:T(8,128)(2,1)S(1)} %get-tuple-element.130), channel_id=1, source_target_pairs={{0,16},{16,0},{1,17},{17,1},{2,18},{18,2},{3,19},{19,3},{4,20},{20... | collective-permute-start | bytes 2359304 | tf_op jit(solution)/shard_map/ppermute | solution.py:660
  28.0 17.8 %copy-start.10 = (bf16[192,1280]{1,0:T(8,128)(2,1)}, bf16[192,1280]{1,0:T(8,128)(2,1)S(1)}, u32[]{:S(2)}) copy-start(bf16[192,1280]{1,0:T(8,128)(2,1)S(1)} %constant_dynamic-update-slice_fusion.refs_3_.refs_4_) | copy-start | bytes 1474564
  28.0 14.3 %collective-permute-start.5 = (bf16[192,1280]{1,0:T(8,128)(2,1)S(1)}, bf16[192,1280]{1,0:T(8,128)(2,1)S(1)}, u32[]{:S(2)}, u32[]{:S(2)}) collective-permute-start(bf16[192,1280]{1,0:T(8,128)(2,1)S(1)} %constant_dynamic-update-slice_fusion.refs_3_.refs_4_), channel_id=1, source_target_pairs={{0,2},{1,3},{2,0},{3,1},{4,6},{5,7},{6,4},{7,5},{8,10},{9,11},{10,... | collective-permute-start | bytes 1474568 | tf_op jit(solution)/shard_map/ppermute | solution.py:656
  29.8 36.2 %collective-permute-start.1 = (s32[512]{0:T(512)S(1)}, s32[512]{0:T(512)S(1)}, u32[]{:S(2)}, u32[]{:S(2)}) collective-permute-start(s32[512]{0:T(512)S(1)} %bitcast.66), channel_id=1, source_target_pairs={{0,16},{16,0},{1,17},{17,1},{2,18},{18,2},{3,19},{19,3},{4,20},{20... | collective-permute-start | bytes 6152 | tf_op jit(solution)/shard_map/ppermute | solution.py:660
  42.3 14.1 %collective-permute-start.7 = (bf16[192,1280]{1,0:T(8,128)(2,1)S(1)}, bf16[192,1280]{1,0:T(8,128)(2,1)S(1)}, u32[]{:S(2)}, u32[]{:S(2)}) collective-permute-start(bf16[192,1280]{1,0:T(8,128)(2,1)S(1)} %collective-permute-done.5.refs_4_.refs_5_), channel_id=1, source_target_pairs={{0,16},{16,0},{1,17},{17,1},{2,18},{18,2},{3,19},{19,3},{4,20},{20... | collective-permute-start | bytes 1474568 | tf_op jit(solution)/shard_map/ppermute | solution.py:660
  43.8 20.9 %collective-permute-start.6 = (bf16[192,1280]{1,0:T(8,128)(2,1)S(1)}, bf16[192,1280]{1,0:T(8,128)(2,1)}, u32[]{:S(2)}, u32[]{:S(2)}) collective-permute-start(bf16[192,1280]{1,0:T(8,128)(2,1)S(1)} %constant_dynamic-update-slice_fusion.refs_3_.refs_4_), channel_id=1, source_target_pairs={{0,16},{16,0},{1,17},{17,1},{2,18},{18,2},{3,19},{19,3},{4,20},{20... | collective-permute-start | bytes 1474568 | tf_op jit(solution)/shard_map/ppermute | solution.py:660
  45.8 22.7 %collective-permute-start.8 = (bf16[192,1280]{1,0:T(8,128)(2,1)S(1)}, bf16[192,1280]{1,0:T(8,128)(2,1)}, u32[]{:S(2)}, u32[]{:S(2)}) collective-permute-start(bf16[192,1280]{1,0:T(8,128)(2,1)S(1)} %constant_dynamic-update-slice_fusion.refs_3_.refs_4_), channel_id=1, source_target_pairs={{0,1},{1,0},{2,3},{3,2},{4,5},{5,4},{6,7},{7,6},{8,9},{9,8},{10,11... | collective-permute-start | bytes 1474568 | tf_op jit(solution)/shard_map/ppermute | solution.py:656
  45.9 22.6 %collective-permute-start.9 = (bf16[192,1280]{1,0:T(8,128)(2,1)S(1)}, bf16[192,1280]{1,0:T(8,128)(2,1)}, u32[]{:S(2)}, u32[]{:S(2)}) collective-permute-start(bf16[192,1280]{1,0:T(8,128)(2,1)S(1)} %collective-permute-done.5.refs_4_.refs_5_), channel_id=1, source_target_pairs={{0,1},{1,0},{2,3},{3,2},{4,5},{5,4},{6,7},{7,6},{8,9},{9,8},{10,11... | collective-permute-start | bytes 1474568 | tf_op jit(solution)/shard_map/ppermute | solution.py:656
  56.4 12.1 %collective-permute-start.11 = (bf16[192,1280]{1,0:T(8,128)(2,1)S(1)}, bf16[192,1280]{1,0:T(8,128)(2,1)}, u32[]{:S(2)}, u32[]{:S(2)}) collective-permute-start(bf16[192,1280]{1,0:T(8,128)(2,1)S(1)} %collective-permute-done.7.refs_6_.refs_7_), channel_id=1, source_target_pairs={{0,1},{1,0},{2,3},{3,2},{4,5},{5,4},{6,7},{7,6},{8,9},{9,8},{10,11... | collective-permute-start | bytes 1474568 | tf_op jit(solution)/shard_map/ppermute | solution.py:656
  64.7 3.8 %collective-permute-start.10 = (bf16[192,1280]{1,0:T(8,128)(2,1)}, bf16[192,1280]{1,0:T(8,128)(2,1)}, u32[]{:S(2)}, u32[]{:S(2)}) collective-permute-start(bf16[192,1280]{1,0:T(8,128)(2,1)} %collective-permute-done.6.refs_5_.refs_6_), channel_id=1, source_target_pairs={{0,1},{1,0},{2,3},{3,2},{4,5},{5,4},{6,7},{7,6},{8,9},{9,8},{10,11... | collective-permute-start | bytes 1474568 | tf_op jit(solution)/shard_map/ppermute | solution.py:656
  68.7 27.1 %collective-permute-start.12 = (bf16[512,768]{1,0:T(8,128)(2,1)S(1)}, bf16[512,768]{1,0:T(8,128)(2,1)S(1)}, u32[]{:S(2)}, u32[]{:S(2)}) collective-permute-start(bf16[512,768]{1,0:T(8,128)(2,1)S(1)} %get-tuple-element.128), channel_id=1, source_target_pairs={{0,16},{16,0},{1,17},{17,1},{2,18},{18,2},{3,19},{19,3},{4,20},{20... | collective-permute-start | bytes 2359304 | tf_op jit(solution)/shard_map/ppermute | solution.py:660
  157.2 25.3 %collective-permute-start.13 = (bf16[512,768]{1,0:T(8,128)(2,1)S(1)}, bf16[512,768]{1,0:T(8,128)(2,1)S(1)}, u32[]{:S(2)}, u32[]{:S(2)}) collective-permute-start(bf16[512,768]{1,0:T(8,128)(2,1)S(1)} %constant_dynamic-slice_fusion), channel_id=1, source_target_pairs={{0,16},{16,0},{1,17},{17,1},{2,18},{18,2},{3,19},{19,3},{4,20},{20... | collective-permute-start | bytes 2359304 | tf_op jit(solution)/shard_map/ppermute | solution.py:660
  193.2 4.8 %collective-permute-start.14 = (bf16[8,48,3072]{2,1,0:T(8,128)(2,1)}, bf16[8,48,3072]{2,1,0:T(8,128)(2,1)S(1)}, u32[]{:S(2)}, u32[]{:S(2)}) collective-permute-start(bf16[8,48,3072]{2,1,0:T(8,128)(2,1)} %get-tuple-element.60), channel_id=1, source_target_pairs={{0,1},{1,0},{2,3},{3,2},{4,5},{5,4},{6,7},{7,6},{8,9},{9,8},{10,11... | collective-permute-start | bytes 7077896 | tf_op jit(solution)/shard_map/ppermute | solution.py:656
  201.5 28.2 %collective-permute-start.15 = (bf16[8,48,1536]{2,1,0:T(8,128)(2,1)}, bf16[8,48,1536]{2,1,0:T(8,128)(2,1)S(1)}, u32[]{:S(2)}, u32[]{:S(2)}) collective-permute-start(bf16[8,48,1536]{2,1,0:T(8,128)(2,1)} %add_convert_fusion), channel_id=1, source_target_pairs={{0,16},{16,0},{1,17},{17,1},{2,18},{18,2},{3,19},{19,3},{4,20},{20... | collective-permute-start | bytes 3538952 | tf_op jit(solution)/shard_map/ppermute | solution.py:660
  202.0 27.7 %copy-start.1 = (bf16[8,48,3072]{2,1,0:T(8,128)(2,1)S(1)}, bf16[8,48,3072]{2,1,0:T(8,128)(2,1)}, u32[]{:S(2)}) copy-start(bf16[8,48,3072]{2,1,0:T(8,128)(2,1)} %get-tuple-element.59) | copy-start | bytes 7077892
  231.8 17.6 %collective-permute-start.17 = (bf16[4,48,1536]{2,1,0:T(8,128)(2,1)}, bf16[4,48,1536]{2,1,0:T(8,128)(2,1)}, u32[]{:S(2)}, u32[]{:S(2)}) collective-permute-start(bf16[4,48,1536]{2,1,0:T(8,128)(2,1)} %add_convert_fusion.1), channel_id=1, source_target_pairs={{0,2},{1,3},{2,0},{3,1},{4,6},{5,7},{6,4},{7,5},{8,10},{9,11},{10,... | collective-permute-start | bytes 1769480 | tf_op jit(solution)/shard_map/ppermute | solution.py:656
  233.6 39.9 %collective-permute-start.16 = (bf16[512,768]{1,0:T(8,128)(2,1)S(1)}, bf16[512,768]{1,0:T(8,128)(2,1)S(1)}, u32[]{:S(2)}, u32[]{:S(2)}) collective-permute-start(bf16[512,768]{1,0:T(8,128)(2,1)S(1)} %copy-done.8), channel_id=1, source_target_pairs={{0,16},{16,0},{1,17},{17,1},{2,18},{18,2},{3,19},{19,3},{4,20},{20... | collective-permute-start | bytes 2359304 | tf_op jit(solution)/shard_map/ppermute | solution.py:660
  251.0 14.3 %collective-permute-start.18 = (bf16[48,1536]{1,0:T(8,128)(2,1)S(1)}, bf16[48,1536]{1,0:T(8,128)(2,1)S(1)}, u32[]{:S(2)}, u32[]{:S(2)}) collective-permute-start(bf16[48,1536]{1,0:T(8,128)(2,1)S(1)} %get-tuple-element.141), channel_id=1, source_target_pairs={{0,4},{1,5},{2,6},{3,7},{4,0},{5,1},{6,2},{7,3},{8,12},{9,13},{10,... | collective-permute-start | bytes 442376 | tf_op jit(solution)/shard_map/ppermute | solution.py:656
  251.2 22.1 %collective-permute-start.19 = (bf16[48,1536]{1,0:T(8,128)(2,1)S(1)}, bf16[48,1536]{1,0:T(8,128)(2,1)S(1)}, u32[]{:S(2)}, u32[]{:S(2)}) collective-permute-start(bf16[48,1536]{1,0:T(8,128)(2,1)S(1)} %get-tuple-element.140), channel_id=1, source_target_pairs={{0,8},{1,9},{2,10},{3,11},{4,12},{5,13},{6,14},{7,15},{8,0},{9,1},... | collective-permute-start | bytes 442376 | tf_op jit(solution)/shard_map/ppermute | solution.py:656
  251.4 21.9 %collective-permute-start.20 = (bf16[48,1536]{1,0:T(8,128)(2,1)S(1)}, bf16[48,1536]{1,0:T(8,128)(2,1)S(1)}, u32[]{:S(2)}, u32[]{:S(2)}) collective-permute-start(bf16[48,1536]{1,0:T(8,128)(2,1)S(1)} %get-tuple-element.139), channel_id=1, source_target_pairs={{0,12},{1,13},{2,14},{3,15},{4,8},{5,9},{6,10},{7,11},{8,4},{9,5},... | collective-permute-start | bytes 442376 | tf_op jit(solution)/shard_map/ppermute | solution.py:656
  255.5 18.0 %copy-start = (f32[1024,768]{1,0:T(8,128)S(1)}, f32[1024,768]{1,0:T(8,128)}, u32[]{:S(2)}) copy-start(f32[1024,768]{1,0:T(8,128)} %input_grad.1) | copy-start | bytes 9437188
  273.4 5.2 %collective-permute-start.21 = (bf16[48,1536]{1,0:T(8,128)(2,1)S(1)}, bf16[48,1536]{1,0:T(8,128)(2,1)S(1)}, u32[]{:S(2)}, u32[]{:S(2)}) collective-permute-start(bf16[48,1536]{1,0:T(8,128)(2,1)S(1)} %fusion.5), channel_id=1, source_target_pairs={{0,16},{16,0},{1,17},{17,1},{2,18},{18,2},{3,19},{19,3},{4,20},{20... | collective-permute-start | bytes 442376 | tf_op jit(solution)/shard_map/ppermute | solution.py:660
  278.7 14.7 %copy-start.11 = (bf16[144,2048]{1,0:T(8,128)(2,1)S(1)}, bf16[144,2048]{1,0:T(8,128)(2,1)}, u32[]{:S(2)}) copy-start(bf16[144,2048]{1,0:T(8,128)(2,1)} %reduce-scatter.2.cloned.1.call-done) | copy-start | bytes 1769476
  278.7 14.7 %collective-permute-start.22 = (bf16[144,2048]{1,0:T(8,128)(2,1)}, bf16[144,2048]{1,0:T(8,128)(2,1)S(1)}, u32[]{:S(2)}, u32[]{:S(2)}) collective-permute-start(bf16[144,2048]{1,0:T(8,128)(2,1)} %reduce-scatter.2.cloned.1.call-done), channel_id=1, source_target_pairs={{0,16},{16,0},{1,17},{17,1},{2,18},{18,2},{3,19},{19,3},{4,20},{20... | collective-permute-start | bytes 1769480 | tf_op jit(solution)/shard_map/ppermute | solution.py:660
  280.3 13.3 %copy-start.6 = (bf16[48,2048]{1,0:T(8,128)(2,1)S(1)}, bf16[48,2048]{1,0:T(8,128)(2,1)}, u32[]{:S(2)}) copy-start(bf16[48,2048]{1,0:T(8,128)(2,1)} %gate_ref.1) | copy-start | bytes 589828
  280.3 13.3 %copy-start.7 = (bf16[48,2048]{1,0:T(8,128)(2,1)S(1)}, bf16[48,2048]{1,0:T(8,128)(2,1)}, u32[]{:S(2)}) copy-start(bf16[48,2048]{1,0:T(8,128)(2,1)} %up_ref.1) | copy-start | bytes 589828
  (15 other events, 74.7 us)
Sparse Core Ops, SparseCore 0:
  11.1 94.1 all-gather.1
  155.9 122.3 reduce-scatter.1

commit v5 on v4

--- a/solution.py
+++ b/solution.py
@@ -350,20 +350,29 @@
     return slices, top
 
 
-def feed_copies(packed, targets, owner, sems):
+def feed_copies(packed, targets, owner, sems, wanted):
     w_out, w_both, w_down = targets
     parts = w_out.shape[0] // packed[0]
-    rows, down_rows = packed[0], w_down.shape[0] // parts
-    slices, height = packed_slices(rows, down_rows, w_out.shape[1], w_down.shape[0])
-    kinds = {"out": (w_out, rows, 0), "both": (w_both, rows, 1), "down": (w_down, down_rows, 2)}
-    copies = {"out": [], "both": [], "down": []}
+    hidden_width = w_down.shape[0]
+    step = min(FSTEP, hidden_width)
+    rows, down_rows = packed[0], hidden_width // parts
+    slices, height = packed_slices(rows, down_rows, w_out.shape[1], hidden_width)
+    kinds = {"out": (w_out, rows), "both": (w_both, rows), "down": (w_down, down_rows)}
+    copies = []
     for name, (low, high), (left, right), top, column in slices:
-        target, each, number = kinds[name]
+        due = name
+        if name == "both":
+            crosses = left < hidden_width < right
+            due = 0 if crosses else left % hidden_width // step
+        if due != wanted:
+            continue
+        target, each = kinds[name]
+        number = due + 2 if name == "both" else ("out", "down").index(name)
         source = packed[1].at[
             pl.ds(pl.multiple_of(owner * height + top, 16), high - low), column : column + right - left
         ]
         goal = target.at[pl.ds(pl.multiple_of(owner * each + low, 16), high - low), left:right]
-        copies[name].append(pltpu.make_async_copy(source, goal, sems.at[number]))
+        copies.append(pltpu.make_async_copy(source, goal, sems.at[number]))
     return copies
 
 
@@ -379,9 +388,11 @@
         views = (w_out, w_both.at[:, :hidden_width], w_both.at[:, hidden_width:], w_down)
         return [pltpu.make_async_copy(piece, view, sems.at[0]) for piece, view in zip(given, views)]
 
-    def per_owner(act):
+    chunks = hidden_width // min(FSTEP, hidden_width)
+
+    def per_owner(act, wanted):
         def step(owner, carry):
-            act(feed_copies((rows, given[0]), targets, owner, sems))
+            act(feed_copies((rows, given[0]), targets, owner, sems, wanted))
             return carry
 
         lax.fori_loop(0, parts, step, 0)
@@ -395,15 +406,15 @@
             start_all(copies)
             wait_all(copies)
         else:
-            per_owner(lambda copies: start_all(copies["out"]))
-            per_owner(lambda copies: start_all(copies["both"] + copies["down"]))
-
-    def wait_for(*kinds):
+            for wanted in ("out", 0, "down", *range(1, chunks)):
+                per_owner(start_all, wanted)
+
+    def wait_for(wanted):
         if count == 1:
 
             @pl.when(opening)
             def _():
-                per_owner(lambda copies: wait_all([copy for kind in kinds for copy in copies[kind]]))
+                per_owner(wait_all, wanted)
 
     wait_for("out")
     gain = gain_ref[1:2, :]
@@ -412,7 +423,7 @@
     inverse = lax.rsqrt(jnp.mean(middle * middle, axis=1, keepdims=True) + EPSILON)
     normed = (middle * inverse * gain).astype(BF)
     n_ref[...] = normed
-    wait_for("both", "down")
+    wait_for("down")
     result[...] = middle
     back[...] = jnp.zeros_like(middle)
     step = min(FSTEP, hidden_width)
@@ -420,6 +431,12 @@
     def chunk(number, carry):
         at = pl.multiple_of(number * step, step)
         part = pl.ds(at, step)
+        for wanted in range(chunks):
+
+            @pl.when(number == wanted)
+            def _(wanted=wanted):
+                wait_for(wanted)
+
         w_gate = w_both[:, part]
         w_up = w_both[:, pl.ds(pl.multiple_of(hidden_width + at, step), step)]
         gate = dot_nn(normed, w_gate)
@@ -467,7 +484,7 @@
             pltpu.VMEM((hidden_width, width), BF),
             pltpu.VMEM((FBLOCK, width), F32),
             pltpu.VMEM((FBLOCK, width), F32),
-            pltpu.SemaphoreType.DMA((3,)),
+            pltpu.SemaphoreType.DMA((2 + hidden_width // min(FSTEP, hidden_width),)),
         ],
         cost_estimate=cost(4 * tokens * width * (width + 3 * hidden_width), 20 * tokens * width + 6 * tokens * hidden_width),
     )(x, attended, dy, gain, *given)

time: 309 us -> 308 us (level)
  Pallas kernels: 123 us -> 119 us
  transfers between devices with their start and end apart: 25 -> 25, of which waited for: 13 -> 13; matrix products, arithmetic and copies ran while one was open for 8% -> 8% of each run, Pallas kernels for 23% -> 22%
where the time goes in v5:
time: 308 us; the launch traced here: 303 us
  Pallas kernels  119 us (39%)
  waiting for transfers between devices  112 us (36%)
  starting transfers between devices  27 us (9%)
  other arithmetic  24.2 us (8%)
  between operations  14.8 us (5%)
  local copies, waits for them, and re-layouts  6.24 us (2%)
    ppermute x13, waiting for transfers between devices, flip(): return lax.ppermute(values, 'fsdp', [(i, i ^ bits) for i in range(count)])  55.8 us
    ppermute x10, waiting for transfers between devices, across(): return lax.ppermute(values, 'seq', [(0, 1), (1, 0)])  46.9 us
    pallas_call x1, Pallas kernels, feed(): pl.pallas_call(functools.partial(feed_kernel, rows, len(given), width, hi...  34.5 us
    pallas_call x1, Pallas kernels, attend_back(): pl.pallas_call(functools.partial(attend_back_kernel, pairs), name='attend...  21.1 us
    pallas_call x1, Pallas kernels, feed_grads(): pl.pallas_call(functools.partial(feed_grads_kernel, parts, steps), name='...  15.7 us
    ppermute x13, starting transfers between devices, flip(): return lax.ppermute(values, 'fsdp', [(i, i ^ bits) for i in range(count)])  15.6 us
    pallas_call x1, Pallas kernels, attend(): pl.pallas_call(functools.partial(attend_kernel, pairs), name='attend', ou...  13.1 us
    ppermute x10, starting transfers between devices, across(): return lax.ppermute(values, 'seq', [(0, 1), (1, 0)])  11.3 us
  transfers between devices with their start and end apart: 25, of which 13 were waited for; matrix products, arithmetic and copies ran while one was open for 8% of the time, Pallas kernels for 22%

profile of v5, /device:TPU:0, one launch (start us, length us, event | category | flops | bytes accessed | tf_op | source)
XLA Modules:
  0.0 303.0 jit_solution(14036348231437191267)
XLA Ops:
  8.8 2.2 pack.1
  11.0 3.1 %collective-permute-start.2 = (bf16[48,1280]{1,0:T(8,128)(2,1)}, bf16[48,1280]{1,0:T(8,128)(2,1)S(1)}, u32[]{:S(2)}, u32[]{:S(2)}) collective-permute-start(bf16[48,1280]{1,0:T(8,128)(2,1)} %get-tuple-element.39), channel_id=1, source_target_pairs={{0,4},{1,5},{2,6},{3,7},{4,0},{5,1},{6,2},{7,3},{8,12},{9,13},{10,... | collective-permute-start | bytes 368648 | tf_op jit(solution)/shard_map/ppermute | solution.py:673
  14.1 2.6 collective-permute-start.3
  16.8 1.8 collective-permute-start
  19.0 8.9 %collective-permute-done.3 = bf16[48,1280]{1,0:T(8,128)(2,1)S(1)} collective-permute-done((bf16[48,1280]{1,0:T(8,128)(2,1)}, bf16[48,1280]{1,0:T(8,128)(2,1)S(1)}, u32[]{:S(2)}, u32[]{:S(2)}) %collective-permute-start.3) | collective-permute-done | bytes 122912 | tf_op jit(solution)/shard_map/ppermute | solution.py:673
  28.0 1.8 collective-permute-start.5
  31.5 10.8 %collective-permute-done.5.refs_4_.refs_5_ = bf16[192,1280]{1,0:T(8,128)(2,1)S(1)} collective-permute-done((bf16[192,1280]{1,0:T(8,128)(2,1)S(1)}, bf16[192,1280]{1,0:T(8,128)(2,1)S(1)}, u32[]{:S(2)}, u32[]{:S(2)}) %collective-permute-start.5) | collective-permute-done | bytes 491552 | tf_op jit(solution)/shard_map/ppermute | solution.py:673
  46.4 10.0 %collective-permute-done.7.refs_6_.refs_7_ = bf16[192,1280]{1,0:T(8,128)(2,1)S(1)} collective-permute-done((bf16[192,1280]{1,0:T(8,128)(2,1)S(1)}, bf16[192,1280]{1,0:T(8,128)(2,1)S(1)}, u32[]{:S(2)}, u32[]{:S(2)}) %collective-permute-start.7) | collective-permute-done | bytes 491552 | tf_op jit(solution)/shard_map/ppermute | solution.py:677
  56.4 8.3 %collective-permute-done.6.refs_5_.refs_6_ = bf16[192,1280]{1,0:T(8,128)(2,1)} collective-permute-done((bf16[192,1280]{1,0:T(8,128)(2,1)S(1)}, bf16[192,1280]{1,0:T(8,128)(2,1)}, u32[]{:S(2)}, u32[]{:S(2)}) %collective-permute-start.6) | collective-permute-done | bytes 491552 | tf_op jit(solution)/shard_map/ppermute | solution.py:677
  66.7 1.8 maximum_select_fusion.refs_0_
  70.7 10.7 %project.1 = (bf16[1024,768]{1,0:T(8,128)(2,1)}, bf16[1024,768]{1,0:T(8,128)(2,1)}, bf16[1024,768]{1,0:T(8,128)(2,1)}, bf16[1024,768]{1,0:T(8,128)(2,1)}, f32[8,768]{1,0:T(8,128)}) custom-call(bf16[1024,768]{1,0:T(8,128)(2,1)} %maximum_select_fusion.refs_0_, f32[1024,128]{1,0:T(8,128)} %pad_maximum_fusion.refs_1_.cos_ref, ...), custom_call_target="tpu_custom_call" | custom-call | flops 3623878656 | bytes 11403264 | tf_op jit(solution)/shard_map/project/pallas_call | solution.py:127
  81.4 13.1 %attend.1 = (bf16[1024,768]{1,0:T(8,128)(2,1)}, f32[8,6,256]{2,1,0:T(8,128)}) custom-call(s32[8]{0:T(128)} %and_select_fusion.first_ref, bf16[1024,768]{1,0:T(8,128)(2,1)} %get-tuple-element.41.q_ref, bf16[1024,768]{1,0:T(8,128)(2,1)} %get-tuple-element.42.k_ref, bf16[1024,768]{1,0:T(8,128)(2,1)} %get-tuple-element.43.v_ref, s32[1,1024]{1,0:T(1,128)} %bitcast.64), custom_call_target="tpu_custom_call" | custom-call | flops 3221225472 | bytes 7864320 | tf_op jit(solution)/shard_map/attend/pallas_call | solution.py:212
  94.5 1.9 maximum_select_fusion.1.refs_2_.dy_any
  96.3 8.9 %all-gather.2.cloned.1.call-done.refs_4_ = bf16[6912,768]{1,0:T(8,128)(2,1)} async-done(((bf16[432,768]{1,0:T(8,128)(2,1)}), bf16[6912,768]{1,0:T(8,128)(2,1)}) %all-gather.2.cloned.1.call-update) | async-done | bytes 10616848 | tf_op jit(solution)/shard_map/all_gather | solution.py:834
  105.2 34.5 %feed.1 = (bf16[1024,768]{1,0:T(8,128)(2,1)}, bf16[1024,768]{1,0:T(8,128)(2,1)}, bf16[1024,2048]{1,0:T(8,128)(2,1)}, bf16[1024,2048]{1,0:T(8,128)(2,1)}, bf16[10...) custom-call(bf16[1024,768]{1,0:T(8,128)(2,1)} %maximum_select_fusion.refs_0_, ...), custom_call_target="tpu_custom_call" | custom-call | flops 21743271936 | bytes 28311552 | tf_op jit(solution)/shard_map/feed/pallas_call | solution.py:474
  139.7 15.7 %feed_grads.1 = bf16[16,144,2048]{2,1,0:T(8,128)(2,1)} custom-call(bf16[1024,768]{1,0:T(8,128)(2,1)} %get-tuple-element.51.n_ref, bf16[1024,2048]{1,0:T(8,128)(2,1)} %get-tuple-element.52.dgate_ref, bf16[1024,2048]{1,0:T(8,128)(2,1)} %get-tuple-element.53.dup_ref, bf16[1024,2048]{1,0:T(8,128)(2,1)} %get-tuple-element.54.hid_any, ...), custom_call_target="tpu_custom_call" | custom-call | flops 9663676416 | bytes 17301504 | tf_op jit(solution)/shard_map/feed_grads/pallas_call | solution.py:607
  158.4 21.1 %attend_back.1.refs_2_ = bf16[1024,2304]{1,0:T(8,128)(2,1)} custom-call(s32[8]{0:T(128)} %and_select_fusion.first_ref, bf16[1024,768]{1,0:T(8,128)(2,1)} %get-tuple-element.41.q_ref, bf16[1024,768]{1,0:T(8,128)(2,1)} %get-tuple-element.42.k_ref, bf16[1024,768]{1,0:T(8,128)(2,1)} %get-tuple-element.43.v_ref, bf16[1024,768]{1,0:T(8,128)(2,1)} %get-tuple-element.55.g_ref, ...), custom_call_target="tpu_custom_call" | custom-call | flops 8053063680 | bytes 12582912 | tf_op jit(solution)/shard_map/attend_back/pallas_call | solution.py:308
  179.5 10.8 %grad_in.1 = (bf16[8,48,3072]{2,1,0:T(8,128)(2,1)}, bf16[8,48,3072]{2,1,0:T(8,128)(2,1)}) custom-call(bf16[1024,768]{1,0:T(8,128)(2,1)} %get-tuple-element.57.refs_0_, bf16[1024,768]{1,0:T(8,128)(2,1)} %get-tuple-element.44.refs_1_, bf16[1024,2304]{1,0:T(8,128)(2,1)} %attend_back.1.refs_2_, bf16[1024,768]{1,0:T(8,128)(2,1)} %get-tuple-element.58.refs_3_), custom_call_target="tpu_custom_call" | custom-call | flops 4831838208 | bytes 12582912 | tf_op jit(solution)/shard_map/grad_in/pallas_call | solution.py:550
  190.4 2.4 collective-permute-start.14
  192.8 4.4 %collective-permute-done.14 = bf16[8,48,3072]{2,1,0:T(8,128)(2,1)S(1)} collective-permute-done((bf16[8,48,3072]{2,1,0:T(8,128)(2,1)}, bf16[8,48,3072]{2,1,0:T(8,128)(2,1)S(1)}, u32[]{:S(2)}, u32[]{:S(2)}) %collective-permute-start.14) | collective-permute-done | bytes 2359328 | tf_op jit(solution)/shard_map/ppermute | solution.py:673
  197.2 3.5 %add_convert_fusion = bf16[8,48,1536]{2,1,0:T(8,128)(2,1)} fusion(bf16[8,48,3072]{2,1,0:T(8,128)(2,1)S(1)} %collective-permute-done.14, s32[]{:T(128)S(6)} %select_n.110, bf16[8,48,3072]{2,1,0:T(8,128)(2,1)} %get-tuple-element.59), kind=kLoop, calls=%fused_computation.2 | loop fusion | flops 2359296 | bytes 3538948 | tf_op jit(solution)/shard_map/convert_element_type | solution.py:769
  201.7 11.1 %input_grad.1 = f32[1024,768]{1,0:T(8,128)} custom-call(bf16[1024,768]{1,0:T(8,128)(2,1)} %maximum_select_fusion.refs_0_, f32[1024,768]{1,0:T(8,128)} %get-tuple-element.62.refs_1_, bf16[1024,2304]{1,0:T(8,128)(2,1)} %attend_back.1.refs_2_, f32[8,768]{1,0:T(8,128)} %get-tuple-element.46.refs_3_, bf16[192,1280]{1,0:T(8,128)(2,1)} %copy-done.10, ...), custom_call_target="tpu_custom_call" | custom-call | flops 3623878656 | bytes 16121856 | tf_op jit(solution)/shard_map/input_grad/pallas_call | solution.py:655
  212.8 2.4 dynamic-slice_convert_fusion
  215.2 14.0 %collective-permute-done.15 = bf16[8,48,1536]{2,1,0:T(8,128)(2,1)S(1)} collective-permute-done((bf16[8,48,1536]{2,1,0:T(8,128)(2,1)}, bf16[8,48,1536]{2,1,0:T(8,128)(2,1)S(1)}, u32[]{:S(2)}, u32[]{:S(2)}) %collective-permute-start.15) | collective-permute-done | bytes 1179680 | tf_op jit(solution)/shard_map/ppermute | solution.py:677
  229.2 2.1 add_convert_fusion.1
  234.1 15.1 %collective-permute-done.17 = bf16[4,48,1536]{2,1,0:T(8,128)(2,1)} collective-permute-done((bf16[4,48,1536]{2,1,0:T(8,128)(2,1)}, bf16[4,48,1536]{2,1,0:T(8,128)(2,1)}, u32[]{:S(2)}, u32[]{:S(2)}) %collective-permute-start.17) | collective-permute-done | bytes 589856 | tf_op jit(solution)/shard_map/ppermute | solution.py:673
  252.1 3.2 %collective-permute-start.20 = (bf16[48,1536]{1,0:T(8,128)(2,1)S(1)}, bf16[48,1536]{1,0:T(8,128)(2,1)S(1)}, u32[]{:S(2)}, u32[]{:S(2)}) collective-permute-start(bf16[48,1536]{1,0:T(8,128)(2,1)S(1)} %get-tuple-element.139), channel_id=1, source_target_pairs={{0,12},{1,13},{2,14},{3,15},{4,8},{5,9},{6,10},{7,11},{8,4},{9,5},... | collective-permute-start | bytes 442376 | tf_op jit(solution)/shard_map/ppermute | solution.py:673
  256.6 8.5 %collective-permute-done.18 = bf16[48,1536]{1,0:T(8,128)(2,1)S(1)} collective-permute-done((bf16[48,1536]{1,0:T(8,128)(2,1)S(1)}, bf16[48,1536]{1,0:T(8,128)(2,1)S(1)}, u32[]{:S(2)}, u32[]{:S(2)}) %collective-permute-start.18) | collective-permute-done | bytes 147488 | tf_op jit(solution)/shard_map/ppermute | solution.py:673
  265.1 7.7 %collective-permute-done.19 = bf16[48,1536]{1,0:T(8,128)(2,1)S(1)} collective-permute-done((bf16[48,1536]{1,0:T(8,128)(2,1)S(1)}, bf16[48,1536]{1,0:T(8,128)(2,1)S(1)}, u32[]{:S(2)}, u32[]{:S(2)}) %collective-permute-start.19) | collective-permute-done | bytes 147488 | tf_op jit(solution)/shard_map/ppermute | solution.py:673
  273.3 1.9 maximum_bitcast_fusion
  275.1 3.0 collective-permute-done.21
  281.2 11.6 %collective-permute-done.22 = bf16[144,2048]{1,0:T(8,128)(2,1)S(1)} collective-permute-done((bf16[144,2048]{1,0:T(8,128)(2,1)}, bf16[144,2048]{1,0:T(8,128)(2,1)S(1)}, u32[]{:S(2)}, u32[]{:S(2)}) %collective-permute-start.22) | collective-permute-done | bytes 589856 | tf_op jit(solution)/shard_map/ppermute | solution.py:677
  (116 shorter events, 29.4 us)
Async XLA Ops:
  7.2 98.1 %all-gather.2.cloned.1.call-start = ((), (), s32[]{:S(2)}) async-start(), calls=%async_computation.1 | async-start | bytes 11280384 | tf_op jit(solution)/shard_map/all_gather | solution.py:834
  11.0 267.2 %reduce-scatter.2.cloned.1.call-start = ((), (), s32[]{:S(2)}) async-start(), calls=%async_computation.2 | async-start | bytes 10027008 | tf_op jit(solution)/shard_map/reduce_scatter | solution.py:889
  11.0 8.0 %collective-permute-start.2 = (bf16[48,1280]{1,0:T(8,128)(2,1)}, bf16[48,1280]{1,0:T(8,128)(2,1)S(1)}, u32[]{:S(2)}, u32[]{:S(2)}) collective-permute-start(bf16[48,1280]{1,0:T(8,128)(2,1)} %get-tuple-element.39), channel_id=1, source_target_pairs={{0,4},{1,5},{2,6},{3,7},{4,0},{5,1},{6,2},{7,3},{8,12},{9,13},{10,... | collective-permute-start | bytes 368648 | tf_op jit(solution)/shard_map/ppermute | solution.py:673
  14.1 13.9 %collective-permute-start.3 = (bf16[48,1280]{1,0:T(8,128)(2,1)}, bf16[48,1280]{1,0:T(8,128)(2,1)S(1)}, u32[]{:S(2)}, u32[]{:S(2)}) collective-permute-start(bf16[48,1280]{1,0:T(8,128)(2,1)} %get-tuple-element.39), channel_id=1, source_target_pairs={{0,8},{1,9},{2,10},{3,11},{4,12},{5,13},{6,14},{7,15},{8,0},{9,1},... | collective-permute-start | bytes 368648 | tf_op jit(solution)/shard_map/ppermute | solution.py:673
  16.7 11.3 %collective-permute-start.4 = (bf16[48,1280]{1,0:T(8,128)(2,1)}, bf16[48,1280]{1,0:T(8,128)(2,1)S(1)}, u32[]{:S(2)}, u32[]{:S(2)}) collective-permute-start(bf16[48,1280]{1,0:T(8,128)(2,1)} %get-tuple-element.39), channel_id=1, source_target_pairs={{0,12},{1,13},{2,14},{3,15},{4,8},{5,9},{6,10},{7,11},{8,4},{9,5},... | collective-permute-start | bytes 368648 | tf_op jit(solution)/shard_map/ppermute | solution.py:673
  16.7 13.1 %copy-start.19 = (s32[2,1,512]{2,1,0:T(1,128)S(1)}, s32[2,1,512]{2,1,0:T(1,128)}, u32[]{:S(2)}) copy-start(s32[2,1,512]{2,1,0:T(1,128)} %param.13) | copy-start | bytes 12292
  16.8 26.9 %collective-permute-start = (bf16[512,768]{1,0:T(8,128)(2,1)S(1)}, bf16[512,768]{1,0:T(8,128)(2,1)S(1)}, u32[]{:S(2)}, u32[]{:S(2)}) collective-permute-start(bf16[512,768]{1,0:T(8,128)(2,1)S(1)} %get-tuple-element.130), channel_id=1, source_target_pairs={{0,16},{16,0},{1,17},{17,1},{2,18},{18,2},{3,19},{19,3},{4,20},{20... | collective-permute-start | bytes 2359304 | tf_op jit(solution)/shard_map/ppermute | solution.py:677
  28.0 17.8 %copy-start.10 = (bf16[192,1280]{1,0:T(8,128)(2,1)}, bf16[192,1280]{1,0:T(8,128)(2,1)S(1)}, u32[]{:S(2)}) copy-start(bf16[192,1280]{1,0:T(8,128)(2,1)S(1)} %constant_dynamic-update-slice_fusion.refs_3_.refs_4_) | copy-start | bytes 1474564
  28.0 14.3 %collective-permute-start.5 = (bf16[192,1280]{1,0:T(8,128)(2,1)S(1)}, bf16[192,1280]{1,0:T(8,128)(2,1)S(1)}, u32[]{:S(2)}, u32[]{:S(2)}) collective-permute-start(bf16[192,1280]{1,0:T(8,128)(2,1)S(1)} %constant_dynamic-update-slice_fusion.refs_3_.refs_4_), channel_id=1, source_target_pairs={{0,2},{1,3},{2,0},{3,1},{4,6},{5,7},{6,4},{7,5},{8,10},{9,11},{10,... | collective-permute-start | bytes 1474568 | tf_op jit(solution)/shard_map/ppermute | solution.py:673
  29.8 36.2 %collective-permute-start.1 = (s32[512]{0:T(512)S(1)}, s32[512]{0:T(512)S(1)}, u32[]{:S(2)}, u32[]{:S(2)}) collective-permute-start(s32[512]{0:T(512)S(1)} %bitcast.66), channel_id=1, source_target_pairs={{0,16},{16,0},{1,17},{17,1},{2,18},{18,2},{3,19},{19,3},{4,20},{20... | collective-permute-start | bytes 6152 | tf_op jit(solution)/shard_map/ppermute | solution.py:677
  42.3 14.1 %collective-permute-start.7 = (bf16[192,1280]{1,0:T(8,128)(2,1)S(1)}, bf16[192,1280]{1,0:T(8,128)(2,1)S(1)}, u32[]{:S(2)}, u32[]{:S(2)}) collective-permute-start(bf16[192,1280]{1,0:T(8,128)(2,1)S(1)} %collective-permute-done.5.refs_4_.refs_5_), channel_id=1, source_target_pairs={{0,16},{16,0},{1,17},{17,1},{2,18},{18,2},{3,19},{19,3},{4,20},{20... | collective-permute-start | bytes 1474568 | tf_op jit(solution)/shard_map/ppermute | solution.py:677
  43.8 20.9 %collective-permute-start.6 = (bf16[192,1280]{1,0:T(8,128)(2,1)S(1)}, bf16[192,1280]{1,0:T(8,128)(2,1)}, u32[]{:S(2)}, u32[]{:S(2)}) collective-permute-start(bf16[192,1280]{1,0:T(8,128)(2,1)S(1)} %constant_dynamic-update-slice_fusion.refs_3_.refs_4_), channel_id=1, source_target_pairs={{0,16},{16,0},{1,17},{17,1},{2,18},{18,2},{3,19},{19,3},{4,20},{20... | collective-permute-start | bytes 1474568 | tf_op jit(solution)/shard_map/ppermute | solution.py:677
  45.8 22.7 %collective-permute-start.8 = (bf16[192,1280]{1,0:T(8,128)(2,1)S(1)}, bf16[192,1280]{1,0:T(8,128)(2,1)}, u32[]{:S(2)}, u32[]{:S(2)}) collective-permute-start(bf16[192,1280]{1,0:T(8,128)(2,1)S(1)} %constant_dynamic-update-slice_fusion.refs_3_.refs_4_), channel_id=1, source_target_pairs={{0,1},{1,0},{2,3},{3,2},{4,5},{5,4},{6,7},{7,6},{8,9},{9,8},{10,11... | collective-permute-start | bytes 1474568 | tf_op jit(solution)/shard_map/ppermute | solution.py:673
  45.9 22.6 %collective-permute-start.9 = (bf16[192,1280]{1,0:T(8,128)(2,1)S(1)}, bf16[192,1280]{1,0:T(8,128)(2,1)}, u32[]{:S(2)}, u32[]{:S(2)}) collective-permute-start(bf16[192,1280]{1,0:T(8,128)(2,1)S(1)} %collective-permute-done.5.refs_4_.refs_5_), channel_id=1, source_target_pairs={{0,1},{1,0},{2,3},{3,2},{4,5},{5,4},{6,7},{7,6},{8,9},{9,8},{10,11... | collective-permute-start | bytes 1474568 | tf_op jit(solution)/shard_map/ppermute | solution.py:673
  56.4 12.1 %collective-permute-start.11 = (bf16[192,1280]{1,0:T(8,128)(2,1)S(1)}, bf16[192,1280]{1,0:T(8,128)(2,1)}, u32[]{:S(2)}, u32[]{:S(2)}) collective-permute-start(bf16[192,1280]{1,0:T(8,128)(2,1)S(1)} %collective-permute-done.7.refs_6_.refs_7_), channel_id=1, source_target_pairs={{0,1},{1,0},{2,3},{3,2},{4,5},{5,4},{6,7},{7,6},{8,9},{9,8},{10,11... | collective-permute-start | bytes 1474568 | tf_op jit(solution)/shard_map/ppermute | solution.py:673
  64.7 3.8 %collective-permute-start.10 = (bf16[192,1280]{1,0:T(8,128)(2,1)}, bf16[192,1280]{1,0:T(8,128)(2,1)}, u32[]{:S(2)}, u32[]{:S(2)}) collective-permute-start(bf16[192,1280]{1,0:T(8,128)(2,1)} %collective-permute-done.6.refs_5_.refs_6_), channel_id=1, source_target_pairs={{0,1},{1,0},{2,3},{3,2},{4,5},{5,4},{6,7},{7,6},{8,9},{9,8},{10,11... | collective-permute-start | bytes 1474568 | tf_op jit(solution)/shard_map/ppermute | solution.py:673
  68.7 25.8 %collective-permute-start.12 = (bf16[512,768]{1,0:T(8,128)(2,1)S(1)}, bf16[512,768]{1,0:T(8,128)(2,1)S(1)}, u32[]{:S(2)}, u32[]{:S(2)}) collective-permute-start(bf16[512,768]{1,0:T(8,128)(2,1)S(1)} %get-tuple-element.128), channel_id=1, source_target_pairs={{0,16},{16,0},{1,17},{17,1},{2,18},{18,2},{3,19},{19,3},{4,20},{20... | collective-permute-start | bytes 2359304 | tf_op jit(solution)/shard_map/ppermute | solution.py:677
  156.9 22.6 %collective-permute-start.13 = (bf16[512,768]{1,0:T(8,128)(2,1)S(1)}, bf16[512,768]{1,0:T(8,128)(2,1)S(1)}, u32[]{:S(2)}, u32[]{:S(2)}) collective-permute-start(bf16[512,768]{1,0:T(8,128)(2,1)S(1)} %constant_dynamic-slice_fusion), channel_id=1, source_target_pairs={{0,16},{16,0},{1,17},{17,1},{2,18},{18,2},{3,19},{19,3},{4,20},{20... | collective-permute-start | bytes 2359304 | tf_op jit(solution)/shard_map/ppermute | solution.py:677
  190.4 6.8 %collective-permute-start.14 = (bf16[8,48,3072]{2,1,0:T(8,128)(2,1)}, bf16[8,48,3072]{2,1,0:T(8,128)(2,1)S(1)}, u32[]{:S(2)}, u32[]{:S(2)}) collective-permute-start(bf16[8,48,3072]{2,1,0:T(8,128)(2,1)} %get-tuple-element.60), channel_id=1, source_target_pairs={{0,1},{1,0},{2,3},{3,2},{4,5},{5,4},{6,7},{7,6},{8,9},{9,8},{10,11... | collective-permute-start | bytes 7077896 | tf_op jit(solution)/shard_map/ppermute | solution.py:673
  200.7 28.5 %collective-permute-start.15 = (bf16[8,48,1536]{2,1,0:T(8,128)(2,1)}, bf16[8,48,1536]{2,1,0:T(8,128)(2,1)S(1)}, u32[]{:S(2)}, u32[]{:S(2)}) collective-permute-start(bf16[8,48,1536]{2,1,0:T(8,128)(2,1)} %add_convert_fusion), channel_id=1, source_target_pairs={{0,16},{16,0},{1,17},{17,1},{2,18},{18,2},{3,19},{19,3},{4,20},{20... | collective-permute-start | bytes 3538952 | tf_op jit(solution)/shard_map/ppermute | solution.py:677
  201.7 27.5 %copy-start.1 = (bf16[8,48,3072]{2,1,0:T(8,128)(2,1)S(1)}, bf16[8,48,3072]{2,1,0:T(8,128)(2,1)}, u32[]{:S(2)}) copy-start(bf16[8,48,3072]{2,1,0:T(8,128)(2,1)} %get-tuple-element.59) | copy-start | bytes 7077892
  231.3 17.9 %collective-permute-start.17 = (bf16[4,48,1536]{2,1,0:T(8,128)(2,1)}, bf16[4,48,1536]{2,1,0:T(8,128)(2,1)}, u32[]{:S(2)}, u32[]{:S(2)}) collective-permute-start(bf16[4,48,1536]{2,1,0:T(8,128)(2,1)} %add_convert_fusion.1), channel_id=1, source_target_pairs={{0,2},{1,3},{2,0},{3,1},{4,6},{5,7},{6,4},{7,5},{8,10},{9,11},{10,... | collective-permute-start | bytes 1769480 | tf_op jit(solution)/shard_map/ppermute | solution.py:673
  233.7 39.3 %collective-permute-start.16 = (bf16[512,768]{1,0:T(8,128)(2,1)S(1)}, bf16[512,768]{1,0:T(8,128)(2,1)S(1)}, u32[]{:S(2)}, u32[]{:S(2)}) collective-permute-start(bf16[512,768]{1,0:T(8,128)(2,1)S(1)} %copy-done.8), channel_id=1, source_target_pairs={{0,16},{16,0},{1,17},{17,1},{2,18},{18,2},{3,19},{19,3},{4,20},{20... | collective-permute-start | bytes 2359304 | tf_op jit(solution)/shard_map/ppermute | solution.py:677
  250.8 14.2 %collective-permute-start.18 = (bf16[48,1536]{1,0:T(8,128)(2,1)S(1)}, bf16[48,1536]{1,0:T(8,128)(2,1)S(1)}, u32[]{:S(2)}, u32[]{:S(2)}) collective-permute-start(bf16[48,1536]{1,0:T(8,128)(2,1)S(1)} %get-tuple-element.141), channel_id=1, source_target_pairs={{0,4},{1,5},{2,6},{3,7},{4,0},{5,1},{6,2},{7,3},{8,12},{9,13},{10,... | collective-permute-start | bytes 442376 | tf_op jit(solution)/shard_map/ppermute | solution.py:673
  250.9 21.9 %collective-permute-start.19 = (bf16[48,1536]{1,0:T(8,128)(2,1)S(1)}, bf16[48,1536]{1,0:T(8,128)(2,1)S(1)}, u32[]{:S(2)}, u32[]{:S(2)}) collective-permute-start(bf16[48,1536]{1,0:T(8,128)(2,1)S(1)} %get-tuple-element.140), channel_id=1, source_target_pairs={{0,8},{1,9},{2,10},{3,11},{4,12},{5,13},{6,14},{7,15},{8,0},{9,1},... | collective-permute-start | bytes 442376 | tf_op jit(solution)/shard_map/ppermute | solution.py:673
  252.1 20.7 %collective-permute-start.20 = (bf16[48,1536]{1,0:T(8,128)(2,1)S(1)}, bf16[48,1536]{1,0:T(8,128)(2,1)S(1)}, u32[]{:S(2)}, u32[]{:S(2)}) collective-permute-start(bf16[48,1536]{1,0:T(8,128)(2,1)S(1)} %get-tuple-element.139), channel_id=1, source_target_pairs={{0,12},{1,13},{2,14},{3,15},{4,8},{5,9},{6,10},{7,11},{8,4},{9,5},... | collective-permute-start | bytes 442376 | tf_op jit(solution)/shard_map/ppermute | solution.py:673
  255.3 17.7 %copy-start = (f32[1024,768]{1,0:T(8,128)S(1)}, f32[1024,768]{1,0:T(8,128)}, u32[]{:S(2)}) copy-start(f32[1024,768]{1,0:T(8,128)} %input_grad.1) | copy-start | bytes 9437188
  272.9 5.2 %collective-permute-start.21 = (bf16[48,1536]{1,0:T(8,128)(2,1)S(1)}, bf16[48,1536]{1,0:T(8,128)(2,1)S(1)}, u32[]{:S(2)}, u32[]{:S(2)}) collective-permute-start(bf16[48,1536]{1,0:T(8,128)(2,1)S(1)} %fusion.5), channel_id=1, source_target_pairs={{0,16},{16,0},{1,17},{17,1},{2,18},{18,2},{3,19},{19,3},{4,20},{20... | collective-permute-start | bytes 442376 | tf_op jit(solution)/shard_map/ppermute | solution.py:677
  278.1 14.7 %copy-start.11 = (bf16[144,2048]{1,0:T(8,128)(2,1)S(1)}, bf16[144,2048]{1,0:T(8,128)(2,1)}, u32[]{:S(2)}) copy-start(bf16[144,2048]{1,0:T(8,128)(2,1)} %reduce-scatter.2.cloned.1.call-done) | copy-start | bytes 1769476
  278.1 14.7 %collective-permute-start.22 = (bf16[144,2048]{1,0:T(8,128)(2,1)}, bf16[144,2048]{1,0:T(8,128)(2,1)S(1)}, u32[]{:S(2)}, u32[]{:S(2)}) collective-permute-start(bf16[144,2048]{1,0:T(8,128)(2,1)} %reduce-scatter.2.cloned.1.call-done), channel_id=1, source_target_pairs={{0,16},{16,0},{1,17},{17,1},{2,18},{18,2},{3,19},{19,3},{4,20},{20... | collective-permute-start | bytes 1769480 | tf_op jit(solution)/shard_map/ppermute | solution.py:677
  279.7 13.3 %copy-start.6 = (bf16[48,2048]{1,0:T(8,128)(2,1)S(1)}, bf16[48,2048]{1,0:T(8,128)(2,1)}, u32[]{:S(2)}) copy-start(bf16[48,2048]{1,0:T(8,128)(2,1)} %gate_ref.1) | copy-start | bytes 589828
  279.7 13.3 %copy-start.7 = (bf16[48,2048]{1,0:T(8,128)(2,1)S(1)}, bf16[48,2048]{1,0:T(8,128)(2,1)}, u32[]{:S(2)}) copy-start(bf16[48,2048]{1,0:T(8,128)(2,1)} %up_ref.1) | copy-start | bytes 589828
  (15 other events, 74.7 us)
Sparse Core Ops, SparseCore 0:
  11.1 94.1 all-gather.1
  155.6 122.1 reduce-scatter.1
